TPU v7x, 32 devices: a whole 2x2x4 slice. The times are simulated.
32 devices in a mesh: head: 4 (over z), frame: 8 (over y, x, core).
Axes of the slice: x: 2, y: 2, z: 4, core: 2. Of those that a mesh axis runs over, the one named last changes fastest.
Arguments:
- queries: bfloat16 [4096, 2048], P(('frame', 'head')), may hold values from -6 to 6
- key_states: bfloat16 [4096, 2048], P(('frame', 'head')), may hold values from -6 to 6
- value_states: bfloat16 [4096, 2048], P(('frame', 'head')), may hold values from -6 to 6
- attn_out: bfloat16 [4096, 2048], P(('frame', 'head')), may hold values from -6 to 6
- grad_out: bfloat16 [4096, 2048], P(('frame', 'head')), may hold values from -192 to 192
- frame_order: int32 [8], replicated, may hold values from 0 to 7, each once
- block_live: int32 [8, 4, 4], replicated, may hold values from 0 to 1, as said below
Outputs:
- grad_queries: bfloat16 [4096, 2048], P('frame', 'head')
- grad_keys: bfloat16 [4096, 2048], P('frame', 'head')
- grad_values: bfloat16 [4096, 2048], P('frame', 'head')
Inputs may be any that keep to these rules, and one draw needn't show every extreme that they name: `block_live`: every entry at distance 0 is 1; every entry at distances of 4 or more is 0.
All inputs are finite; a program needn't handle non-finite values.
Results may differ from a plain program's by a relative error of at most 0.0049.
Values may be sent and summed in bfloat16 or wider, within the bound.
No kernel may reach another device: no remote copies, remote signals or barrier semaphores. Data moves between devices by JAX's collectives and lax.ppermute only.
A program may use at most 128 MiB of HBM per device.

v0:
```python
import functools
import math

import jax
import jax.numpy as jnp
from jax import lax
from jax.experimental import pallas as pl
from jax.experimental.pallas import tpu as pltpu
from jax.sharding import PartitionSpec as P


HEADS = 16
HEAD_DIM = 128
NEG = -1e30
KEY_GROUP = 4
WIDE_GROUP = 6
TOGETHER = 4
REACH = 4
EXTRA = 8


VMEM = pl.BlockSpec(memory_space=pltpu.VMEM)
SMEM = pl.BlockSpec(memory_space=pltpu.SMEM)
HBM = pl.BlockSpec(memory_space=pltpu.HBM)
F32 = jnp.float32
BF16 = jnp.bfloat16
NT = (((1,), (1,)), ((), ()))
TN = (((0,), (0,)), ((), ()))
NN = (((1,), (0,)), ((), ()))


def dot(a, b, dims):
    return lax.dot_general(a, b, dims, preferred_element_type=F32)


def sds(shape, dtype):
    return jax.ShapeDtypeStruct(shape, dtype)


def lasts(microseconds):
    return pl.CostEstimate(flops=0, bytes_accessed=int(microseconds * 3.5e6), transcendentals=0)


def within(*shapes):
    held = sum(math.prod(s.shape) * s.dtype.itemsize for s in shapes)
    return pltpu.CompilerParams(vmem_limit_bytes=int(held * 5 // 4) + (6 << 20))


class Plan:
    def __init__(self, rows):
        self.nz = lax.axis_size("head")
        self.nf = lax.axis_size("frame")
        self.hh = HEADS // self.nz
        self.na = min(self.hh, self.nf)
        self.nb = self.nf // self.na
        self.rows = rows
        self.own = self.na * self.nz
        self.total = self.own * self.nb
        assert self.hh == self.na and rows == HEAD_DIM


def over_head(value, step):
    count = lax.axis_size("head")
    return lax.ppermute(value, "head", [(i, i ^ step) for i in range(count)])


def over_frame(value, step):
    count = lax.axis_size("frame")
    return lax.ppermute(value, "frame", [(i, i ^ step) for i in range(count)])


def bundles(plan, ids, refs, bufs, sems):
    width = plan.hh * HEAD_DIM
    out = []
    for r in range(plan.nz):
        cols = pl.ds(pl.multiple_of((ids[0] ^ r) * width, width), width)
        for w, (ref, buf) in enumerate(zip(refs, bufs)):
            out.append(pltpu.make_async_copy(ref.at[:, cols], buf.at[r], sems.at[w, r]))
    for copy in out:
        copy.start()
    return out


def within_bundle(ids, s):
    return pl.ds(pl.multiple_of((ids[1] ^ s) * HEAD_DIM, HEAD_DIM), HEAD_DIM)


def prep_kernel(plan, q_ref, k_ref, out):
    hd, rows = HEAD_DIM, plan.rows
    for a in range(plan.na):
        for z in range(plan.nz):
            head, place = z * plan.hh + a, a * plan.nz + z
            out[place, :rows] = q_ref[:, head * hd : (head + 1) * hd]
            out[place, rows:] = k_ref[:, head * hd : (head + 1) * hd]


def prep(plan, q, k):
    return pl.pallas_call(
        functools.partial(prep_kernel, plan),
        out_shape=sds((plan.own, 2 * plan.rows, HEAD_DIM), BF16),
        in_specs=[VMEM] * 2,
        out_specs=VMEM,
        cost_estimate=lasts(1.5),
        compiler_params=pltpu.CompilerParams(vmem_limit_bytes=60 << 20),
        name="prep",
    )(q, k)


def part_kernel(plan, ids, x_ref, q_out, k_out):
    rows = plan.rows
    for s in range(plan.na):
        for r in range(plan.nz):
            place = (ids[1] ^ s) * plan.nz + (ids[0] ^ r)
            q_out[s * plan.nz + r] = x_ref[place, :rows]
            k_out[s * plan.nz + r] = x_ref[place, rows:]


def part(plan, ids, x):
    return pl.pallas_call(
        functools.partial(part_kernel, plan),
        out_shape=[sds((plan.own, plan.rows, HEAD_DIM), BF16)] * 2,
        in_specs=[SMEM, VMEM],
        out_specs=[VMEM] * 2,
        cost_estimate=lasts(1),
        compiler_params=within(x, x),
        name="part",
    )(ids, x)


def prep_rest_kernel(plan, ids, g_ref, o_ref, v_ref, *refs):
    na, rows = plan.na, plan.rows
    g_outs, v_outs, bufs, sems = refs[:na], refs[na : 2 * na], refs[2 * na : 2 * na + 3], refs[-1]
    copies = bundles(plan, ids, [g_ref, o_ref, v_ref], bufs, sems)
    ones = jnp.ones((EXTRA, HEAD_DIM), BF16)
    row = lax.broadcasted_iota(jnp.int32, (EXTRA, rows), 0)
    for r in range(plan.nz):
        for copy in copies[3 * r : 3 * r + 3]:
            copy.wait()
        for s in range(na):
            cols = within_bundle(ids, s)
            grad = bufs[0][r, :, cols]
            g_outs[s][r, :rows] = grad
            v_outs[s][r] = bufs[2][r, :, cols]
            product = grad.astype(F32) * bufs[1][r, :, cols].astype(F32)
            high = product.astype(BF16)
            low = (product - high.astype(F32)).astype(BF16)
            delta = dot(ones, high, NT) + dot(ones, low, NT)
            first = delta.astype(BF16).astype(F32)
            rest = delta - first
            second = rest.astype(BF16).astype(F32)
            parts = jnp.where(row == 2, rest - second, 0.0)
            parts = jnp.where(row == 0, first, jnp.where(row == 1, second, parts))
            g_outs[s][r, rows:] = parts.astype(BF16)


def prep_rest(plan, ids, g, o, v):
    na, nz, rows, hd = plan.na, plan.nz, plan.rows, HEAD_DIM
    outs = pl.pallas_call(
        functools.partial(prep_rest_kernel, plan),
        out_shape=[sds((nz, rows + EXTRA, hd), BF16)] * na + [sds((nz, rows, hd), BF16)] * na,
        in_specs=[SMEM] + [HBM] * 3,
        out_specs=[VMEM] * (2 * na),
        scratch_shapes=[pltpu.VMEM((nz, rows, plan.hh * hd), BF16)] * 3
        + [pltpu.SemaphoreType.DMA((3, nz))],
        cost_estimate=lasts(2),
        compiler_params=within(g, o, v, g, v),
        name="prep_rest",
    )(ids, g, o, v)
    return outs[:na], outs[na:]


def turn_kernel(count, *refs):
    pieces, outs = refs[:count], refs[count:]
    joined = len(outs) == 1
    for c in range(pieces[0].shape[0]):
        for p, piece in enumerate(pieces):
            if joined:
                outs[0][c * count + p] = piece[c]
            else:
                outs[c][p] = piece[c]


def turn(pieces, joined=False):
    count, parts, shape = len(pieces), pieces[0].shape[0], pieces[0].shape[1:]
    out = [sds((parts * count, *shape), BF16)] if joined else [sds((count, *shape), BF16)] * parts
    outs = pl.pallas_call(
        functools.partial(turn_kernel, count),
        out_shape=out,
        in_specs=[VMEM] * count,
        out_specs=[VMEM] * len(out),
        cost_estimate=lasts(0.5),
        compiler_params=within(*pieces, *pieces),
    )(*pieces)
    return outs[0] if joined else outs


def lists_kernel(plan, ids, order, live_ref, by_key, n_key, query_of, numbers):
    nz, na, nb = plan.nz, plan.na, plan.nb
    z, a, b = ids[0], ids[1], ids[2]
    true = [z ^ r for r in range(nz)]

    def at_distance(d, carry):
        for rk in range(nz):
            count = jnp.int32(0)
            for r in range(nz):
                query_of[d * nz + rk, count] = jnp.int32(r)
                count = count + (live_ref[true[r], true[rk], d] > 0).astype(jnp.int32)
            numbers[d * nz + rk] = count
        return carry

    lax.fori_loop(1, REACH, at_distance, 0)

    def key_frame(s_key, carry):
        place_key = order[(a ^ s_key) * nb + b]

        def query_frame(ts, counts):
            t = ts // na
            place = order[(a ^ (ts - t * na)) * nb + (b ^ t)]
            d = jnp.abs(place - place_key)

            def found(counts):
                counts = list(counts)
                for rk in range(nz):
                    row = d * nz + rk
                    for u in range(nz):
                        by_key[s_key * nz + rk, counts[rk] + u] = ts * nz + query_of[row, u]
                    counts[rk] = counts[rk] + numbers[row]
                return tuple(counts)

            return lax.cond((d > 0) & (d < REACH), found, lambda counts: counts, counts)

        counts = lax.fori_loop(0, na * nb, query_frame, (jnp.int32(0),) * nz)
        for rk in range(nz):
            n_key[s_key * nz + rk] = counts[rk]
        return carry

    lax.fori_loop(0, na, key_frame, 0)


def lists(plan, ids, order, live):
    own, total, nz = plan.own, plan.total, plan.nz
    return pl.pallas_call(
        functools.partial(lists_kernel, plan),
        out_shape=[sds((own, total + WIDE_GROUP + nz), jnp.int32), sds((own,), jnp.int32)],
        in_specs=[SMEM] * 3,
        out_specs=[SMEM] * 2,
        scratch_shapes=[
            pltpu.SMEM((REACH * nz, nz), jnp.int32),
            pltpu.SMEM((REACH * nz,), jnp.int32),
        ],
        cost_estimate=lasts(3),
        compiler_params=within(),
        name="lists",
    )(ids, order, live)


def picks(table, row, count, first, size):
    out = []
    for u in range(size):
        valid = first + u < count
        out.append((jnp.where(valid, table[row, first + u], 0), valid))
    return out


def steps(count, size):
    return lax.div(count + (size - 1), size)


def totals_kernel(plan, by_key, n_key, k_ref, *refs):
    parts, (out, q_ref, peaks, sums) = refs[: plan.nb], refs[plan.nb :]
    nz, na, own, rows, total = plan.nz, plan.na, plan.own, plan.rows, plan.total
    scale = HEAD_DIM**-0.5
    length = nz * rows
    for t, each in enumerate(parts):
        q_ref[t * own : (t + 1) * own] = each[...]
    peaks[own:, :] = jnp.full((peaks.shape[0] - own, rows), NEG, F32)
    sums[own:, :] = jnp.zeros((peaks.shape[0] - own, rows), F32)

    def near(s, carry):
        span = pl.ds(s * nz, nz)
        keys, q = k_ref[span].reshape(length, HEAD_DIM), q_ref[span].reshape(length, HEAD_DIM)
        scores = scale * dot(keys, q, NT)
        peak = jnp.max(scores, axis=0, keepdims=True)
        mass = jnp.sum(jnp.exp(scores - peak), axis=0, keepdims=True)
        for r in range(nz):
            peaks[pl.ds(s * nz + r, 1), :] = peak[:, r * rows : (r + 1) * rows]
            sums[pl.ds(s * nz + r, 1), :] = mass[:, r * rows : (r + 1) * rows]
        return carry

    lax.fori_loop(0, na, near, 0)

    def local(j, start):
        chosen = picks(by_key, j, n_key[j], start, WIDE_GROUP)
        places = [pl.ds(jnp.where(ok, i, total), 1) for i, ok in chosen]
        q = jnp.concatenate([q_ref[i] for i, _ in chosen], axis=0)
        scores = scale * dot(k_ref[j], q, NT)
        peak = jnp.max(scores, axis=0, keepdims=True)
        mass = jnp.sum(jnp.exp(scores - peak), axis=0, keepdims=True)
        return places, peak, mass

    def merge(places, peak, mass):
        old_peak = jnp.concatenate([peaks[place, :] for place in places], axis=1)
        old_mass = jnp.concatenate([sums[place, :] for place in places], axis=1)
        new_peak = jnp.maximum(old_peak, peak)
        new_mass = old_mass * jnp.exp(old_peak - new_peak) + mass * jnp.exp(peak - new_peak)
        for u, place in enumerate(places):
            peaks[place, :] = new_peak[:, u * rows : (u + 1) * rows]
            sums[place, :] = new_mass[:, u * rows : (u + 1) * rows]

    def away(m, carry):
        for found in [local(m * TOGETHER + u, 0) for u in range(TOGETHER)]:
            merge(*found)
        return carry

    lax.fori_loop(0, own // TOGETHER, away, 0)

    def rest(j, carry):
        def group(step, carry):
            merge(*local(j, step * WIDE_GROUP))
            return carry

        return lax.fori_loop(1, steps(n_key[j], WIDE_GROUP), group, carry)

    lax.fori_loop(0, own, rest, 0)
    peak = peaks[:total, :]
    out[...] = jnp.where(peak > 0.5 * NEG, peak + jnp.log(sums[:total, :]), NEG)


def totals(plan, by_key, n_key, keys, queries):
    return pl.pallas_call(
        functools.partial(totals_kernel, plan),
        out_shape=[
            sds((plan.total, plan.rows), F32),
            sds((plan.total, plan.rows, HEAD_DIM), BF16),
        ],
        in_specs=[SMEM, SMEM, VMEM] + [VMEM] * plan.nb,
        out_specs=[VMEM] * 2,
        scratch_shapes=[pltpu.VMEM((plan.total + 8, plan.rows), F32)] * 2,
        cost_estimate=lasts(6),
        compiler_params=within(keys, *queries, *queries),
        name="totals",
    )(by_key, n_key, keys, *queries)


def rows_kernel(plan, *refs):
    nb, own, rows = plan.nb, plan.own, plan.rows
    g_refs, parts, (lse_all, delta_all, g_all) = refs[:nb], refs[nb : 2 * nb], refs[2 * nb :]
    for t in range(nb):
        rivals = [parts[u][pl.ds((t ^ u) * own, own), :] for u in range(nb)]
        peak = functools.reduce(jnp.maximum, rivals)
        lse_all[pl.ds(t * own, own), :] = peak + jnp.log(sum(jnp.exp(x - peak) for x in rivals))
        for m in range(own):
            extra = g_refs[t][m, rows:].astype(F32)
            delta_all[t * own + m : t * own + m + 1, :] = jnp.sum(extra, axis=0, keepdims=True)
            g_all[t * own + m] = g_refs[t][m, :rows]


def query_rows(plan, out_grads, parts):
    return pl.pallas_call(
        functools.partial(rows_kernel, plan),
        out_shape=[sds((plan.total, plan.rows), F32)] * 2
        + [sds((plan.total, plan.rows, HEAD_DIM), BF16)],
        in_specs=[VMEM] * (2 * plan.nb),
        out_specs=[VMEM] * 3,
        cost_estimate=lasts(1),
        compiler_params=within(*out_grads, *out_grads),
        name="query_rows",
    )(*out_grads, *parts)


def grads_kernel(plan, span, first, last, by_key, n_key, q_ref, g_ref, lse_ref, delta_ref, k_ref, *refs):
    nz, na, nb, own, rows = plan.nz, plan.na, plan.nb, plan.own, plan.rows
    hd = HEAD_DIM
    scale = hd**-0.5
    length = nz * rows
    width = len(span)
    refs = list(refs)
    take = lambda n: [refs.pop(0) for _ in range(n)]
    v_refs = take(width)
    if not first:
        (dq_before,) = take(1)
    kv_outs = take(na)
    dq_outs = take(nb if last else 1)
    dk_all, dv_all = take(2)
    dq_all = refs.pop(0) if last else dq_outs[0]

    def begin(i, carry):
        dq_all[i] = jnp.zeros((rows, hd), F32) if first else dq_before[i]
        return carry

    lax.fori_loop(own if first else 0, plan.total, begin, 0)

    def wide_row(ref, start):
        return jnp.concatenate([ref[pl.ds(start + r, 1), :] for r in range(nz)], axis=1)

    def diagonal(s, carry):
        frame = pl.ds(s * nz, nz)
        k = jnp.concatenate([k_ref[s * nz + r] for r in span], axis=0)
        v = jnp.concatenate([v_ref[s] for v_ref in v_refs], axis=0)
        q, g = q_ref[frame].reshape(length, hd), g_ref[frame].reshape(length, hd)
        lse, delta = wide_row(lse_ref, s * nz), wide_row(delta_ref, s * nz)
        probs = jnp.exp(scale * dot(k, q, NT) - lse)
        dv = dot(probs.astype(BF16), g, NN)
        grad_scores = (probs * (dot(v, g, NT) - delta)).astype(BF16)
        dk = dot(grad_scores, q, NN)
        dq = dot(grad_scores, k, TN).reshape(nz, rows, hd)
        for x in range(width):
            dv_all[s * width + x] = dv[x * rows : (x + 1) * rows]
            dk_all[s * width + x] = dk[x * rows : (x + 1) * rows]
        if first:
            dq_all[frame] = dq
        else:
            dq_all[frame] += dq
        return carry

    lax.fori_loop(0, na, diagonal, 0)

    def terms(s, x, j, start):
        k, v = k_ref[j], v_refs[x][s]
        chosen = picks(by_key, j, n_key[j], start, KEY_GROUP)
        q = jnp.concatenate([q_ref[i] for i, _ in chosen], axis=0)
        g = jnp.concatenate([g_ref[i] for i, _ in chosen], axis=0)
        lse = jnp.concatenate([jnp.where(ok, lse_ref[pl.ds(i, 1), :], -NEG) for i, ok in chosen], axis=1)
        delta = jnp.concatenate([delta_ref[pl.ds(i, 1), :] for i, _ in chosen], axis=1)
        probs = jnp.exp(scale * dot(k, q, NT) - lse)
        dv = dot(probs.astype(BF16), g, NN)
        grad_scores = (probs * (dot(v, g, NT) - delta)).astype(BF16)
        dk = dot(grad_scores, q, NN)
        return chosen, dv, dk, dot(grad_scores, k, TN)

    def add(s, x, found):
        chosen, dv, dk, dq = found
        dv_all[s * width + x] += dv
        dk_all[s * width + x] += dk
        for u, (i, _) in enumerate(chosen):
            dq_all[i] += dq[u * rows : (u + 1) * rows]

    def away(s, carry):
        for x, found in [(x, terms(s, x, s * nz + r, 0)) for x, r in enumerate(span)]:
            add(s, x, found)
        for x, r in enumerate(span):

            def group(step, carry, x=x, r=r):
                add(s, x, terms(s, x, s * nz + r, step * KEY_GROUP))
                return carry

            lax.fori_loop(1, steps(n_key[s * nz + r], KEY_GROUP), group, 0)
        return carry

    lax.fori_loop(0, na, away, 0)

    for s, out in enumerate(kv_outs):
        for x in range(width):
            out[0, x] = (scale * dk_all[s * width + x]).astype(BF16)
            out[1, x] = dv_all[s * width + x].astype(BF16)
    if last:
        for t in range(nb):

            def drain(m, carry, t=t):
                dq_outs[t][m] = scale * dq_all[t * own + m]
                return carry

            lax.fori_loop(0, own, drain, 0)


def grads(plan, span, tables, queries, out_grads, lse, delta, keys, values, dq_before, last):
    nb, na, own, rows, total = plan.nb, plan.na, plan.own, plan.rows, plan.total
    hd, width, first = HEAD_DIM, len(span), dq_before is None
    kv = [sds((2, width, rows, hd), BF16)] * na
    dq = [sds((own, rows, hd), F32)] * nb if last else [sds((total, rows, hd), F32)]
    before = [] if first else [dq_before]
    partial = sds((own, rows, hd), F32)
    outs = pl.pallas_call(
        functools.partial(grads_kernel, plan, span, first, last),
        out_shape=kv + dq,
        in_specs=[SMEM] * 2 + [VMEM] * (5 + width + len(before)),
        out_specs=[VMEM] * (na + len(dq)),
        scratch_shapes=[pltpu.VMEM((na * width, rows, hd), F32)] * 2
        + ([pltpu.VMEM((total, rows, hd), F32)] if last else []),
        cost_estimate=lasts(7),
        compiler_params=within(queries, out_grads, keys, keys, *[partial] * (4 + 3 * nb)),
    )(*tables, queries, out_grads, lse, delta, keys, *values, *before)
    return outs[:na], outs[na:]


def pack_kernel(plan, *refs):
    nb, nz = plan.nb, plan.nz
    for s, out in enumerate(refs[nb:]):
        for r in range(nz):
            out[0, r] = sum(ref[s * nz + r] for ref in refs[:nb]).astype(BF16)


def pack(plan, partials):
    return pl.pallas_call(
        functools.partial(pack_kernel, plan),
        out_shape=[sds((1, plan.nz, plan.rows, HEAD_DIM), BF16)] * plan.na,
        in_specs=[VMEM] * plan.nb,
        out_specs=[VMEM] * plan.na,
        cost_estimate=lasts(1),
        compiler_params=within(*partials, *partials),
        name="pack",
    )(*partials)


def assemble_kernel(plan, spans, n, ids, *refs):
    na, rows, hd = plan.na, plan.rows, HEAD_DIM
    refs = list(refs)
    outs = refs[na * len(spans) :]
    for span in spans:
        for s in range(na):
            piece = refs.pop(0)
            cols = pl.ds(pl.multiple_of((ids[1] ^ s) * hd, hd), hd)
            for w in range(n):
                for x, r in enumerate(span):
                    place = pl.ds(pl.multiple_of((ids[0] ^ r) * rows, rows), rows)
                    outs[w][place, cols] = piece[w, x]


def assemble(plan, ids, spans, groups):
    n = groups[0][0].shape[0]
    pieces = [piece for group in groups for piece in group]
    return pl.pallas_call(
        functools.partial(assemble_kernel, plan, spans, n),
        out_shape=[sds((plan.nz * plan.rows, plan.na * HEAD_DIM), BF16)] * n,
        in_specs=[SMEM] + [VMEM] * len(pieces),
        out_specs=[VMEM] * n,
        cost_estimate=lasts(1.5),
        compiler_params=within(*pieces, *pieces),
    )(ids, *pieces)


def local(queries, key_states, value_states, attn_out, grad_out, frame_order, block_live):
    plan = Plan(queries.shape[0])
    nz, na, nb = plan.nz, plan.na, plan.nb
    slot = lax.axis_index("frame")
    ids = jnp.stack([lax.axis_index("head"), slot // nb, slot % nb]).astype(jnp.int32)

    def staged(order, pieces, send):
        moved = {}
        for step in order:
            moved[step] = send(pieces[step], step)
        return [pieces[0]] + [moved[step] for step in range(1, len(pieces))]

    def head_stage(pieces):
        return staged([*range(2, nz), 1], pieces, over_head)

    def frame_stage(pieces):
        return staged(range(na - 1, 0, -1), pieces, lambda x, s: over_frame(x, s * nb))

    def swapped(parts):
        return staged(range(1, nb), parts, over_frame)

    groups = [
        [(a * nb + b) * nz + z for a in range(na) for z in range(nz)] for b in range(nb)
    ]
    mine = lax.all_to_all(
        prep(plan, queries, key_states), ("frame", "head"), 0, 0,
        tiled=True, axis_index_groups=groups,
    )
    g_near, v_near = prep_rest(plan, ids, grad_out, attn_out, value_states)
    g_near = frame_stage(g_near)
    v_near = frame_stage(v_near)
    by_key, n_key = lists(plan, ids, frame_order, block_live.transpose(1, 2, 0))
    g_own = turn(head_stage(turn(g_near)), joined=True)
    values = head_stage(turn(v_near))
    q_own, keys = part(plan, ids, mine)
    lse_part, q_all = totals(plan, by_key, n_key, keys, swapped([q_own] * nb))
    lse, delta, g_all = query_rows(plan, swapped([g_own] * nb), swapped([lse_part] * nb))
    spans = [range(0, 2), range(2, nz)]
    kv_home, dq = [], None
    for place, span in enumerate(spans):
        last = place == len(spans) - 1
        kv, dq_parts = grads(
            plan, span, (by_key, n_key), q_all, g_all, lse, delta, keys,
            [values[r] for r in span], dq, last,
        )
        dq = dq_parts[0]
        kv_home.append(frame_stage(kv))
    dq_home = frame_stage(pack(plan, swapped(dq_parts)))
    grad_key, grad_value = assemble(plan, ids, spans, kv_home)
    (grad_query,) = assemble(plan, ids, [range(nz)], [dq_home])
    return grad_query, grad_key, grad_value


def solution(mesh):
    rows = P(("frame", "head"), None)
    in_specs = (rows,) * 5 + (P(), P())
    out_specs = (P("frame", "head"),) * 3
    return jax.shard_map(local, mesh=mesh, in_specs=in_specs, out_specs=out_specs, check_vma=False)
```

profile of v0, /device:TPU:0, one launch (start us, length us, event | category | flops | bytes accessed | tf_op | source)
XLA Modules:
  0.0 113.9 jit_solution(3293773377129196251)
XLA Ops:
  0.7 2.5 %prep.1 = bf16[16,256,128]{2,1,0:T(8,128)(2,1)} custom-call(bf16[128,2048]{1,0:T(8,128)(2,1)} %q_ref.1, bf16[128,2048]{1,0:T(8,128)(2,1)} %k_ref.1), custom_call_target="tpu_custom_call" | custom-call | bytes 5250000 | tf_op jit(solution)/shard_map/prep/pallas_call | solution.py:98
  3.2 8.3 %all-to-all-start = ((bf16[16,256,128]{2,1,0:T(8,128)(2,1)}), bf16[16,256,128]{2,1,0:T(8,128)(2,1)S(1)}, u32[]{:S(2)}, u32[]{:S(2)}) async-start(bf16[16,256,128]{2,1,0:T(8,128)(2,1)} %prep.1), calls=%async_computation | async-start | bytes 2097152 | tf_op jit(solution)/shard_map/all_to_all | solution.py:556
  11.5 0.1 pad_add_fusion.ids
  11.6 0.0 copy-start.3
  11.6 0.0 copy-start.4
  11.6 2.1 %prep_rest.1 = (bf16[4,136,128]{2,1,0:T(8,128)(2,1)S(1)}, bf16[4,136,128]{2,1,0:T(8,128)(2,1)S(1)}, bf16[4,136,128]{2,1,0:T(8,128)(2,1)S(1)}, bf16[4,136,128]{2,...) custom-call(s32[3]{0:T(128)S(1)} %pad_add_fusion.ids, ...), custom_call_target="tpu_custom_call" | custom-call | bytes 7000000 | tf_op jit(solution)/shard_map/prep_rest/pallas_call | solution.py:158
  13.7 2.0 %collective-permute-start.1 = (bf16[4,136,128]{2,1,0:T(8,128)(2,1)S(1)}, bf16[4,136,128]{2,1,0:T(8,128)(2,1)S(1)}, u32[]{:S(2)}, u32[]{:S(2)}) collective-permute-start(bf16[4,136,128]{2,1,0:T(8,128)(2,1)S(1)} %get-tuple-element.51), channel_id=1, source_target_pairs={{0,2},{1,3},{2,0},{3,1},{4,6},{5,7},{6,4},{7,5},{8,10},{9,11},{10,... | collective-permute-start | bytes 417800 | tf_op jit(solution)/shard_map/ppermute | solution.py:69
  15.7 1.5 %collective-permute-start.2 = (bf16[4,136,128]{2,1,0:T(8,128)(2,1)S(1)}, bf16[4,136,128]{2,1,0:T(8,128)(2,1)S(1)}, u32[]{:S(2)}, u32[]{:S(2)}) collective-permute-start(bf16[4,136,128]{2,1,0:T(8,128)(2,1)S(1)} %get-tuple-element.52), channel_id=1, source_target_pairs={{0,4},{1,5},{2,6},{3,7},{4,0},{5,1},{6,2},{7,3},{8,12},{9,13},{10,... | collective-permute-start | bytes 417800 | tf_op jit(solution)/shard_map/ppermute | solution.py:69
  17.2 0.1 collective-permute-start.3
  17.3 9.3 %collective-permute-done.1.refs_1_ = bf16[4,136,128]{2,1,0:T(8,128)(2,1)S(1)} collective-permute-done((bf16[4,136,128]{2,1,0:T(8,128)(2,1)S(1)}, bf16[4,136,128]{2,1,0:T(8,128)(2,1)S(1)}, u32[]{:S(2)}, u32[]{:S(2)}) %collective-permute-start.1) | collective-permute-done | bytes 139296 | tf_op jit(solution)/shard_map/ppermute | solution.py:69
  26.5 1.5 %collective-permute-done.2.refs_2_ = bf16[4,136,128]{2,1,0:T(8,128)(2,1)S(1)} collective-permute-done((bf16[4,136,128]{2,1,0:T(8,128)(2,1)S(1)}, bf16[4,136,128]{2,1,0:T(8,128)(2,1)S(1)}, u32[]{:S(2)}, u32[]{:S(2)}) %collective-permute-start.2) | collective-permute-done | bytes 139296 | tf_op jit(solution)/shard_map/ppermute | solution.py:69
  28.0 2.4 %collective-permute-done.3.refs_3_ = bf16[4,136,128]{2,1,0:T(8,128)(2,1)S(1)} collective-permute-done((bf16[4,136,128]{2,1,0:T(8,128)(2,1)S(1)}, bf16[4,136,128]{2,1,0:T(8,128)(2,1)S(1)}, u32[]{:S(2)}, u32[]{:S(2)}) %collective-permute-start.3) | collective-permute-done | bytes 139296 | tf_op jit(solution)/shard_map/ppermute | solution.py:69
  30.5 0.1 collective-permute-start.4
  30.6 5.2 %collective-permute-start.5 = (bf16[4,136,128]{2,1,0:T(8,128)(2,1)S(1)}, bf16[4,136,128]{2,1,0:T(8,128)(2,1)S(1)}, u32[]{:S(2)}, u32[]{:S(2)}) collective-permute-start(bf16[4,136,128]{2,1,0:T(8,128)(2,1)S(1)} %get-tuple-element.56), channel_id=1, source_target_pairs={{0,16},{8,24},{16,0},{24,8},{1,17},{9,25},{17,1},{25,9},{2,18},{10... | collective-permute-start | bytes 417800 | tf_op jit(solution)/shard_map/ppermute | solution.py:64
  35.8 0.0 collective-permute-start.6
  35.8 0.6 collective-permute-done.4.refs_1_
  36.4 10.7 %collective-permute-done.5.refs_2_ = bf16[4,136,128]{2,1,0:T(8,128)(2,1)S(1)} collective-permute-done((bf16[4,136,128]{2,1,0:T(8,128)(2,1)S(1)}, bf16[4,136,128]{2,1,0:T(8,128)(2,1)S(1)}, u32[]{:S(2)}, u32[]{:S(2)}) %collective-permute-start.5) | collective-permute-done | bytes 139296 | tf_op jit(solution)/shard_map/ppermute | solution.py:64
  47.1 0.0 collective-permute-done.6.refs_3_
  47.2 0.1 collective-permute-start.7
  47.2 0.0 all-to-all-done.x_ref
  47.3 0.6 part.1
  47.9 0.6 collective-permute-start
  48.4 1.5 %collective-permute-start.9 = (bf16[4,128,128]{2,1,0:T(8,128)(2,1)S(1)}, bf16[4,128,128]{2,1,0:T(8,128)(2,1)S(1)}, u32[]{:S(2)}, u32[]{:S(2)}) collective-permute-start(bf16[4,128,128]{2,1,0:T(8,128)(2,1)S(1)} %get-tuple-element.63), channel_id=1, source_target_pairs={{0,2},{1,3},{2,0},{3,1},{4,6},{5,7},{6,4},{7,5},{8,10},{9,11},{10,... | collective-permute-start | bytes 393224 | tf_op jit(solution)/shard_map/ppermute | solution.py:69
  49.9 1.5 %collective-permute-start.10 = (bf16[4,128,128]{2,1,0:T(8,128)(2,1)S(1)}, bf16[4,128,128]{2,1,0:T(8,128)(2,1)S(1)}, u32[]{:S(2)}, u32[]{:S(2)}) collective-permute-start(bf16[4,128,128]{2,1,0:T(8,128)(2,1)S(1)} %get-tuple-element.64), channel_id=1, source_target_pairs={{0,4},{1,5},{2,6},{3,7},{4,0},{5,1},{6,2},{7,3},{8,12},{9,13},{10,... | collective-permute-start | bytes 393224 | tf_op jit(solution)/shard_map/ppermute | solution.py:69
  51.4 0.6 collective-permute-start.11
  51.9 2.4 %collective-permute-done.9.refs_1_ = bf16[4,128,128]{2,1,0:T(8,128)(2,1)S(1)} collective-permute-done((bf16[4,128,128]{2,1,0:T(8,128)(2,1)S(1)}, bf16[4,128,128]{2,1,0:T(8,128)(2,1)S(1)}, u32[]{:S(2)}, u32[]{:S(2)}) %collective-permute-start.9) | collective-permute-done | bytes 131104 | tf_op jit(solution)/shard_map/ppermute | solution.py:69
  54.3 3.6 %collective-permute-done.10.refs_2_ = bf16[4,128,128]{2,1,0:T(8,128)(2,1)S(1)} collective-permute-done((bf16[4,128,128]{2,1,0:T(8,128)(2,1)S(1)}, bf16[4,128,128]{2,1,0:T(8,128)(2,1)S(1)}, u32[]{:S(2)}, u32[]{:S(2)}) %collective-permute-start.10) | collective-permute-done | bytes 131104 | tf_op jit(solution)/shard_map/ppermute | solution.py:69
  57.9 0.0 collective-permute-done.11.refs_3_
  57.9 2.6 %collective-permute-start.14 = (bf16[4,128,128]{2,1,0:T(8,128)(2,1)S(1)}, bf16[4,128,128]{2,1,0:T(8,128)(2,1)S(1)}, u32[]{:S(2)}, u32[]{:S(2)}) collective-permute-start(bf16[4,128,128]{2,1,0:T(8,128)(2,1)S(1)} %get-tuple-element.69), channel_id=1, source_target_pairs={{0,8},{8,0},{16,24},{24,16},{1,9},{9,1},{17,25},{25,17},{2,10},{10... | collective-permute-start | bytes 393224 | tf_op jit(solution)/shard_map/ppermute | solution.py:64
  60.6 0.1 collective-permute-start.12
  60.7 2.3 %collective-permute-start.13 = (bf16[4,128,128]{2,1,0:T(8,128)(2,1)S(1)}, bf16[4,128,128]{2,1,0:T(8,128)(2,1)S(1)}, u32[]{:S(2)}, u32[]{:S(2)}) collective-permute-start(bf16[4,128,128]{2,1,0:T(8,128)(2,1)S(1)} %get-tuple-element.67), channel_id=1, source_target_pairs={{0,24},{8,16},{16,8},{24,0},{1,25},{9,17},{17,9},{25,1},{2,26},{10... | collective-permute-start | bytes 393224 | tf_op jit(solution)/shard_map/ppermute | solution.py:64
  63.0 3.5 %lists.1 = (s32[16,42]{1,0:T(8,128)S(1)}, s32[16]{0:T(128)S(1)}) custom-call(s32[3]{0:T(128)S(1)} %pad_add_fusion.ids, s32[8]{0:T(128)S(1)} %copy-done.4, s32[4,4,8]{2,1,0:T(4,128)S(1)} %bitcast.4), custom_call_target="tpu_custom_call" | custom-call | bytes 10500000 | tf_op jit(solution)/shard_map/lists/pallas_call | solution.py:242
  66.5 5.9 %totals.1 = (f32[32,128]{1,0:T(8,128)S(1)}, bf16[32,128,128]{2,1,0:T(8,128)(2,1)S(1)}) custom-call(s32[16,42]{1,0:T(8,128)S(1)} %get-tuple-element.45.by_key, s32[16]{0:T(128)S(1)} %get-tuple-element.46.n_key, bf16[16,128,128]{2,1,0:T(8,128)(2,1)S(1)} %get-tuple-element.47.k_ref, bf16[16,128,128]{2,1,0:T(8,128)(2,1)S(1)} %get-tuple-element.48.refs_0_, ...), custom_call_target="tpu_custom_call" | custom-call | bytes 21000000 | tf_op jit(solution)/shard_map/totals/pallas_call | solution.py:330
  72.4 0.1 collective-permute-start.8
  72.5 0.0 collective-permute-done.7.refs_1_
  72.5 1.2 %collective-permute-done.8.refs_3_ = f32[32,128]{1,0:T(8,128)S(1)} collective-permute-done((f32[32,128]{1,0:T(8,128)S(1)}, f32[32,128]{1,0:T(8,128)S(1)}, u32[]{:S(2)}, u32[]{:S(2)}) %collective-permute-start.8) | collective-permute-done | bytes 16416 | tf_op jit(solution)/shard_map/ppermute | solution.py:69
  73.6 0.1 query_rows.1
  73.7 0.0 collective-permute-done.14.refs_1_
  73.7 8.6 %shard_map.97 = (bf16[2,2,128,128]{3,2,1,0:T(8,128)(2,1)S(1)}, bf16[2,2,128,128]{3,2,1,0:T(8,128)(2,1)S(1)}, bf16[2,2,128,128]{3,2,1,0:T(8,128)(2,1)S(1)}, bf16[...) custom-call(s32[16,42]{1,0:T(8,128)S(1)} %get-tuple-element.45.by_key, s32[16]{0:T(128)S(1)} %get-tuple-element.46.n_key, ...), custom_call_target="tpu_custom_call" | custom-call | bytes 24500000 | tf_op jit(solution)/shard_map/pallas_call | solution.py:473
  82.4 0.0 collective-permute-done.12.refs_0_
  82.4 9.1 %shard_map.98 = (bf16[2,2,128,128]{3,2,1,0:T(8,128)(2,1)S(1)}, bf16[2,2,128,128]{3,2,1,0:T(8,128)(2,1)S(1)}, bf16[2,2,128,128]{3,2,1,0:T(8,128)(2,1)S(1)}, bf16[...) custom-call(s32[16,42]{1,0:T(8,128)S(1)} %get-tuple-element.45.by_key, ...), custom_call_target="tpu_custom_call" | custom-call | bytes 24500000 | tf_op jit(solution)/shard_map/pallas_call | solution.py:473
  91.5 0.2 collective-permute-start.15
  91.7 1.2 %collective-permute-start.22 = (bf16[2,2,128,128]{3,2,1,0:T(8,128)(2,1)S(1)}, bf16[2,2,128,128]{3,2,1,0:T(8,128)(2,1)S(1)}, u32[]{:S(2)}, u32[]{:S(2)}) collective-permute-start(bf16[2,2,128,128]{3,2,1,0:T(8,128)(2,1)S(1)} %get-tuple-element.82), channel_id=1, source_target_pairs={{0,2},{1,3},{2,0},{3,1},{4,6},{5,7},{6,4},{7,5},{8,10},{9,11},{10,... | collective-permute-start | bytes 393224 | tf_op jit(solution)/shard_map/ppermute | solution.py:69
  92.9 0.8 collective-permute-start.23
  93.8 1.5 %collective-permute-start.24 = (bf16[2,2,128,128]{3,2,1,0:T(8,128)(2,1)S(1)}, bf16[2,2,128,128]{3,2,1,0:T(8,128)(2,1)S(1)}, u32[]{:S(2)}, u32[]{:S(2)}) collective-permute-start(bf16[2,2,128,128]{3,2,1,0:T(8,128)(2,1)S(1)} %get-tuple-element.84), channel_id=1, source_target_pairs={{0,6},{1,7},{2,4},{3,5},{4,2},{5,3},{6,0},{7,1},{8,14},{9,15},{10,... | collective-permute-start | bytes 393224 | tf_op jit(solution)/shard_map/ppermute | solution.py:69
  95.2 1.2 %collective-permute-start.19 = (bf16[2,2,128,128]{3,2,1,0:T(8,128)(2,1)S(1)}, bf16[2,2,128,128]{3,2,1,0:T(8,128)(2,1)S(1)}, u32[]{:S(2)}, u32[]{:S(2)}) collective-permute-start(bf16[2,2,128,128]{3,2,1,0:T(8,128)(2,1)S(1)} %get-tuple-element.78), channel_id=1, source_target_pairs={{0,2},{1,3},{2,0},{3,1},{4,6},{5,7},{6,4},{7,5},{8,10},{9,11},{10,... | collective-permute-start | bytes 393224 | tf_op jit(solution)/shard_map/ppermute | solution.py:69
  96.4 0.0 collective-permute-done.15.refs_1_
  96.4 0.8 collective-permute-start.20
  97.3 0.2 pack.1
  97.4 0.7 collective-permute-done.22.refs_5_
  98.1 1.3 %collective-permute-start.21 = (bf16[2,2,128,128]{3,2,1,0:T(8,128)(2,1)S(1)}, bf16[2,2,128,128]{3,2,1,0:T(8,128)(2,1)S(1)}, u32[]{:S(2)}, u32[]{:S(2)}) collective-permute-start(bf16[2,2,128,128]{3,2,1,0:T(8,128)(2,1)S(1)} %get-tuple-element.80), channel_id=1, source_target_pairs={{0,6},{1,7},{2,4},{3,5},{4,2},{5,3},{6,0},{7,1},{8,14},{9,15},{10,... | collective-permute-start | bytes 393224 | tf_op jit(solution)/shard_map/ppermute | solution.py:69
  99.4 1.9 %collective-permute-done.23.refs_6_ = bf16[2,2,128,128]{3,2,1,0:T(8,128)(2,1)S(1)} collective-permute-done((bf16[2,2,128,128]{3,2,1,0:T(8,128)(2,1)S(1)}, bf16[2,2,128,128]{3,2,1,0:T(8,128)(2,1)S(1)}, u32[]{:S(2)}, u32[]{:S(2)}) %collective-permute-start.23) | collective-permute-done | bytes 131104 | tf_op jit(solution)/shard_map/ppermute | solution.py:69
  101.3 1.1 collective-permute-start.16
  102.4 0.0 collective-permute-done.24.refs_7_
  102.4 1.8 %collective-permute-start.17 = (bf16[1,4,128,128]{3,2,1,0:T(8,128)(2,1)S(1)}, bf16[1,4,128,128]{3,2,1,0:T(8,128)(2,1)S(1)}, u32[]{:S(2)}, u32[]{:S(2)}) collective-permute-start(bf16[1,4,128,128]{3,2,1,0:T(8,128)(2,1)S(1)} %get-tuple-element.75), channel_id=1, source_target_pairs={{0,4},{1,5},{2,6},{3,7},{4,0},{5,1},{6,2},{7,3},{8,12},{9,13},{10,... | collective-permute-start | bytes 393224 | tf_op jit(solution)/shard_map/ppermute | solution.py:69
  104.2 0.0 collective-permute-done.19.refs_1_
  104.2 1.2 %collective-permute-start.18 = (bf16[1,4,128,128]{3,2,1,0:T(8,128)(2,1)S(1)}, bf16[1,4,128,128]{3,2,1,0:T(8,128)(2,1)S(1)}, u32[]{:S(2)}, u32[]{:S(2)}) collective-permute-start(bf16[1,4,128,128]{3,2,1,0:T(8,128)(2,1)S(1)} %get-tuple-element.76), channel_id=1, source_target_pairs={{0,6},{1,7},{2,4},{3,5},{4,2},{5,3},{6,0},{7,1},{8,14},{9,15},{10,... | collective-permute-start | bytes 393224 | tf_op jit(solution)/shard_map/ppermute | solution.py:69
  105.3 1.5 %collective-permute-done.20.refs_2_ = bf16[2,2,128,128]{3,2,1,0:T(8,128)(2,1)S(1)} collective-permute-done((bf16[2,2,128,128]{3,2,1,0:T(8,128)(2,1)S(1)}, bf16[2,2,128,128]{3,2,1,0:T(8,128)(2,1)S(1)}, u32[]{:S(2)}, u32[]{:S(2)}) %collective-permute-start.20) | collective-permute-done | bytes 131104 | tf_op jit(solution)/shard_map/ppermute | solution.py:69
  106.9 0.7 collective-permute-done.21.refs_3_
  107.5 1.7 %shard_map.100 = (bf16[512,512]{1,0:T(8,128)(2,1)}, bf16[512,512]{1,0:T(8,128)(2,1)}) custom-call(s32[3]{0:T(128)S(1)} %pad_add_fusion.ids, bf16[2,2,128,128]{3,2,1,0:T(8,128)(2,1)S(1)} %get-tuple-element.77.refs_0_, bf16[2,2,128,128]{3,2,1,0:T(8,128)(2,1)S(1)} %collective-permute-done.19.refs_1_, ...), custom_call_target="tpu_custom_call" | custom-call | bytes 5250000 | tf_op jit(solution)/shard_map/pallas_call | solution.py:522
  109.2 0.2 collective-permute-done.16.refs_1_
  109.4 0.7 collective-permute-done.17.refs_2_
  110.1 2.4 %collective-permute-done.18.refs_3_ = bf16[1,4,128,128]{3,2,1,0:T(8,128)(2,1)S(1)} collective-permute-done((bf16[1,4,128,128]{3,2,1,0:T(8,128)(2,1)S(1)}, bf16[1,4,128,128]{3,2,1,0:T(8,128)(2,1)S(1)}, u32[]{:S(2)}, u32[]{:S(2)}) %collective-permute-start.18) | collective-permute-done | bytes 131104 | tf_op jit(solution)/shard_map/ppermute | solution.py:69
  112.5 1.4 %shard_map.99 = bf16[512,512]{1,0:T(8,128)(2,1)} custom-call(s32[3]{0:T(128)S(1)} %pad_add_fusion.ids, bf16[1,4,128,128]{3,2,1,0:T(8,128)(2,1)S(1)} %get-tuple-element.73.refs_0_, bf16[1,4,128,128]{3,2,1,0:T(8,128)(2,1)S(1)} %collective-permute-done.16.refs_1_, bf16[1,4,128,128]{3,2,1,0:T(8,128)(2,1)S(1)} %collective-permute-done.17.refs_2_, ...), custom_call_target="tpu_custom_call" | custom-call | bytes 5250000 | tf_op jit(solution)/shard_map/pallas_call | solution.py:522
  (13 shorter events, 0.1 us)
Async XLA Ops:
  0.6 11.0 %copy-start = (bf16[128,2048]{1,0:T(8,128)(2,1)S(1)}, bf16[128,2048]{1,0:T(8,128)(2,1)}, u32[]{:S(2)}) copy-start(bf16[128,2048]{1,0:T(8,128)(2,1)} %g_ref.1) | copy-start | bytes 1572868
  0.6 11.0 %copy-start.1 = (bf16[128,2048]{1,0:T(8,128)(2,1)S(1)}, bf16[128,2048]{1,0:T(8,128)(2,1)}, u32[]{:S(2)}) copy-start(bf16[128,2048]{1,0:T(8,128)(2,1)} %o_ref.1) | copy-start | bytes 1572868
  0.7 11.0 %copy-start.2 = (bf16[128,2048]{1,0:T(8,128)(2,1)S(1)}, bf16[128,2048]{1,0:T(8,128)(2,1)}, u32[]{:S(2)}) copy-start(bf16[128,2048]{1,0:T(8,128)(2,1)} %v_ref.1) | copy-start | bytes 1572868
  3.2 44.1 %all-to-all-start = ((bf16[16,256,128]{2,1,0:T(8,128)(2,1)}), bf16[16,256,128]{2,1,0:T(8,128)(2,1)S(1)}, u32[]{:S(2)}, u32[]{:S(2)}) async-start(bf16[16,256,128]{2,1,0:T(8,128)(2,1)} %prep.1), calls=%async_computation | async-start | bytes 2097152 | tf_op jit(solution)/shard_map/all_to_all | solution.py:556
  11.6 51.4 %copy-start.3 = (s32[8,4,4]{0,2,1:T(4,128)S(1)}, s32[8,4,4]{0,2,1:T(4,128)}, u32[]{:S(2)}) copy-start(s32[8,4,4]{0,2,1:T(4,128)} %param.13) | copy-start | bytes 1540
  11.6 51.4 %copy-start.4 = (s32[8]{0:T(128)S(1)}, s32[8]{0:T(128)}, u32[]{:S(2)}) copy-start(s32[8]{0:T(128)} %order.1) | copy-start | bytes 100
  13.7 12.8 %collective-permute-start.1 = (bf16[4,136,128]{2,1,0:T(8,128)(2,1)S(1)}, bf16[4,136,128]{2,1,0:T(8,128)(2,1)S(1)}, u32[]{:S(2)}, u32[]{:S(2)}) collective-permute-start(bf16[4,136,128]{2,1,0:T(8,128)(2,1)S(1)} %get-tuple-element.51), channel_id=1, source_target_pairs={{0,2},{1,3},{2,0},{3,1},{4,6},{5,7},{6,4},{7,5},{8,10},{9,11},{10,... | collective-permute-start | bytes 417800 | tf_op jit(solution)/shard_map/ppermute | solution.py:69
  15.7 12.3 %collective-permute-start.2 = (bf16[4,136,128]{2,1,0:T(8,128)(2,1)S(1)}, bf16[4,136,128]{2,1,0:T(8,128)(2,1)S(1)}, u32[]{:S(2)}, u32[]{:S(2)}) collective-permute-start(bf16[4,136,128]{2,1,0:T(8,128)(2,1)S(1)} %get-tuple-element.52), channel_id=1, source_target_pairs={{0,4},{1,5},{2,6},{3,7},{4,0},{5,1},{6,2},{7,3},{8,12},{9,13},{10,... | collective-permute-start | bytes 417800 | tf_op jit(solution)/shard_map/ppermute | solution.py:69
  17.2 13.3 %collective-permute-start.3 = (bf16[4,136,128]{2,1,0:T(8,128)(2,1)S(1)}, bf16[4,136,128]{2,1,0:T(8,128)(2,1)S(1)}, u32[]{:S(2)}, u32[]{:S(2)}) collective-permute-start(bf16[4,136,128]{2,1,0:T(8,128)(2,1)S(1)} %get-tuple-element.53), channel_id=1, source_target_pairs={{0,6},{1,7},{2,4},{3,5},{4,2},{5,3},{6,0},{7,1},{8,14},{9,15},{10,... | collective-permute-start | bytes 417800 | tf_op jit(solution)/shard_map/ppermute | solution.py:69
  30.5 5.9 %collective-permute-start.4 = (bf16[4,136,128]{2,1,0:T(8,128)(2,1)S(1)}, bf16[4,136,128]{2,1,0:T(8,128)(2,1)S(1)}, u32[]{:S(2)}, u32[]{:S(2)}) collective-permute-start(bf16[4,136,128]{2,1,0:T(8,128)(2,1)S(1)} %get-tuple-element.55), channel_id=1, source_target_pairs={{0,8},{8,0},{16,24},{24,16},{1,9},{9,1},{17,25},{25,17},{2,10},{10... | collective-permute-start | bytes 417800 | tf_op jit(solution)/shard_map/ppermute | solution.py:64
  30.6 16.5 %collective-permute-start.5 = (bf16[4,136,128]{2,1,0:T(8,128)(2,1)S(1)}, bf16[4,136,128]{2,1,0:T(8,128)(2,1)S(1)}, u32[]{:S(2)}, u32[]{:S(2)}) collective-permute-start(bf16[4,136,128]{2,1,0:T(8,128)(2,1)S(1)} %get-tuple-element.56), channel_id=1, source_target_pairs={{0,16},{8,24},{16,0},{24,8},{1,17},{9,25},{17,1},{25,9},{2,18},{10... | collective-permute-start | bytes 417800 | tf_op jit(solution)/shard_map/ppermute | solution.py:64
  35.8 11.3 %collective-permute-start.6 = (bf16[4,136,128]{2,1,0:T(8,128)(2,1)S(1)}, bf16[4,136,128]{2,1,0:T(8,128)(2,1)S(1)}, u32[]{:S(2)}, u32[]{:S(2)}) collective-permute-start(bf16[4,136,128]{2,1,0:T(8,128)(2,1)S(1)} %get-tuple-element.57), channel_id=1, source_target_pairs={{0,24},{8,16},{16,8},{24,0},{1,25},{9,17},{17,9},{25,1},{2,26},{10... | collective-permute-start | bytes 417800 | tf_op jit(solution)/shard_map/ppermute | solution.py:64
  47.2 25.3 %collective-permute-start.7 = (bf16[16,136,128]{2,1,0:T(8,128)(2,1)S(1)}, bf16[16,136,128]{2,1,0:T(8,128)(2,1)S(1)}, u32[]{:S(2)}, u32[]{:S(2)}) collective-permute-start(bf16[16,136,128]{2,1,0:T(8,128)(2,1)S(1)} %shard_map.95.refs_0_), channel_id=1, source_target_pairs={{0,1},{1,0},{2,3},{3,2},{4,5},{5,4},{6,7},{7,6},{8,9},{9,8},{10,11... | collective-permute-start | bytes 1671176 | tf_op jit(solution)/shard_map/ppermute | solution.py:69
  47.9 18.6 %collective-permute-start = (bf16[16,128,128]{2,1,0:T(8,128)(2,1)S(1)}, bf16[16,128,128]{2,1,0:T(8,128)(2,1)S(1)}, u32[]{:S(2)}, u32[]{:S(2)}) collective-permute-start(bf16[16,128,128]{2,1,0:T(8,128)(2,1)S(1)} %get-tuple-element.48.refs_0_), channel_id=1, source_target_pairs={{0,1},{1,0},{2,3},{3,2},{4,5},{5,4},{6,7},{7,6},{8,9},{9,8},{10,11... | collective-permute-start | bytes 1572872 | tf_op jit(solution)/shard_map/ppermute | solution.py:69
  48.4 5.9 %collective-permute-start.9 = (bf16[4,128,128]{2,1,0:T(8,128)(2,1)S(1)}, bf16[4,128,128]{2,1,0:T(8,128)(2,1)S(1)}, u32[]{:S(2)}, u32[]{:S(2)}) collective-permute-start(bf16[4,128,128]{2,1,0:T(8,128)(2,1)S(1)} %get-tuple-element.63), channel_id=1, source_target_pairs={{0,2},{1,3},{2,0},{3,1},{4,6},{5,7},{6,4},{7,5},{8,10},{9,11},{10,... | collective-permute-start | bytes 393224 | tf_op jit(solution)/shard_map/ppermute | solution.py:69
  49.9 8.0 %collective-permute-start.10 = (bf16[4,128,128]{2,1,0:T(8,128)(2,1)S(1)}, bf16[4,128,128]{2,1,0:T(8,128)(2,1)S(1)}, u32[]{:S(2)}, u32[]{:S(2)}) collective-permute-start(bf16[4,128,128]{2,1,0:T(8,128)(2,1)S(1)} %get-tuple-element.64), channel_id=1, source_target_pairs={{0,4},{1,5},{2,6},{3,7},{4,0},{5,1},{6,2},{7,3},{8,12},{9,13},{10,... | collective-permute-start | bytes 393224 | tf_op jit(solution)/shard_map/ppermute | solution.py:69
  51.4 6.5 %collective-permute-start.11 = (bf16[4,128,128]{2,1,0:T(8,128)(2,1)S(1)}, bf16[4,128,128]{2,1,0:T(8,128)(2,1)S(1)}, u32[]{:S(2)}, u32[]{:S(2)}) collective-permute-start(bf16[4,128,128]{2,1,0:T(8,128)(2,1)S(1)} %get-tuple-element.65), channel_id=1, source_target_pairs={{0,6},{1,7},{2,4},{3,5},{4,2},{5,3},{6,0},{7,1},{8,14},{9,15},{10,... | collective-permute-start | bytes 393224 | tf_op jit(solution)/shard_map/ppermute | solution.py:69
  57.9 15.8 %collective-permute-start.14 = (bf16[4,128,128]{2,1,0:T(8,128)(2,1)S(1)}, bf16[4,128,128]{2,1,0:T(8,128)(2,1)S(1)}, u32[]{:S(2)}, u32[]{:S(2)}) collective-permute-start(bf16[4,128,128]{2,1,0:T(8,128)(2,1)S(1)} %get-tuple-element.69), channel_id=1, source_target_pairs={{0,8},{8,0},{16,24},{24,16},{1,9},{9,1},{17,25},{25,17},{2,10},{10... | collective-permute-start | bytes 393224 | tf_op jit(solution)/shard_map/ppermute | solution.py:64
  60.6 21.8 %collective-permute-start.12 = (bf16[4,128,128]{2,1,0:T(8,128)(2,1)S(1)}, bf16[4,128,128]{2,1,0:T(8,128)(2,1)S(1)}, u32[]{:S(2)}, u32[]{:S(2)}) collective-permute-start(bf16[4,128,128]{2,1,0:T(8,128)(2,1)S(1)} %get-tuple-element.66), channel_id=1, source_target_pairs={{0,16},{8,24},{16,0},{24,8},{1,17},{9,25},{17,1},{25,9},{2,18},{10... | collective-permute-start | bytes 393224 | tf_op jit(solution)/shard_map/ppermute | solution.py:64
  60.7 21.7 %collective-permute-start.13 = (bf16[4,128,128]{2,1,0:T(8,128)(2,1)S(1)}, bf16[4,128,128]{2,1,0:T(8,128)(2,1)S(1)}, u32[]{:S(2)}, u32[]{:S(2)}) collective-permute-start(bf16[4,128,128]{2,1,0:T(8,128)(2,1)S(1)} %get-tuple-element.67), channel_id=1, source_target_pairs={{0,24},{8,16},{16,8},{24,0},{1,25},{9,17},{17,9},{25,1},{2,26},{10... | collective-permute-start | bytes 393224 | tf_op jit(solution)/shard_map/ppermute | solution.py:64
  72.4 1.2 %collective-permute-start.8 = (f32[32,128]{1,0:T(8,128)S(1)}, f32[32,128]{1,0:T(8,128)S(1)}, u32[]{:S(2)}, u32[]{:S(2)}) collective-permute-start(f32[32,128]{1,0:T(8,128)S(1)} %get-tuple-element.58.refs_2_), channel_id=1, source_target_pairs={{0,1},{1,0},{2,3},{3,2},{4,5},{5,4},{6,7},{7,6},{8,9},{9,8},{10,11... | collective-permute-start | bytes 49160 | tf_op jit(solution)/shard_map/ppermute | solution.py:69
  91.5 4.9 %collective-permute-start.15 = (f32[16,128,128]{2,1,0:T(8,128)S(1)}, f32[16,128,128]{2,1,0:T(8,128)S(1)}, u32[]{:S(2)}, u32[]{:S(2)}) collective-permute-start(f32[16,128,128]{2,1,0:T(8,128)S(1)} %get-tuple-element.72), channel_id=1, source_target_pairs={{0,1},{1,0},{2,3},{3,2},{4,5},{5,4},{6,7},{7,6},{8,9},{9,8},{10,11... | collective-permute-start | bytes 3145736 | tf_op jit(solution)/shard_map/ppermute | solution.py:69
  91.7 6.4 %collective-permute-start.22 = (bf16[2,2,128,128]{3,2,1,0:T(8,128)(2,1)S(1)}, bf16[2,2,128,128]{3,2,1,0:T(8,128)(2,1)S(1)}, u32[]{:S(2)}, u32[]{:S(2)}) collective-permute-start(bf16[2,2,128,128]{3,2,1,0:T(8,128)(2,1)S(1)} %get-tuple-element.82), channel_id=1, source_target_pairs={{0,2},{1,3},{2,0},{3,1},{4,6},{5,7},{6,4},{7,5},{8,10},{9,11},{10,... | collective-permute-start | bytes 393224 | tf_op jit(solution)/shard_map/ppermute | solution.py:69
  92.9 8.4 %collective-permute-start.23 = (bf16[2,2,128,128]{3,2,1,0:T(8,128)(2,1)S(1)}, bf16[2,2,128,128]{3,2,1,0:T(8,128)(2,1)S(1)}, u32[]{:S(2)}, u32[]{:S(2)}) collective-permute-start(bf16[2,2,128,128]{3,2,1,0:T(8,128)(2,1)S(1)} %get-tuple-element.83), channel_id=1, source_target_pairs={{0,4},{1,5},{2,6},{3,7},{4,0},{5,1},{6,2},{7,3},{8,12},{9,13},{10,... | collective-permute-start | bytes 393224 | tf_op jit(solution)/shard_map/ppermute | solution.py:69
  93.8 8.7 %collective-permute-start.24 = (bf16[2,2,128,128]{3,2,1,0:T(8,128)(2,1)S(1)}, bf16[2,2,128,128]{3,2,1,0:T(8,128)(2,1)S(1)}, u32[]{:S(2)}, u32[]{:S(2)}) collective-permute-start(bf16[2,2,128,128]{3,2,1,0:T(8,128)(2,1)S(1)} %get-tuple-element.84), channel_id=1, source_target_pairs={{0,6},{1,7},{2,4},{3,5},{4,2},{5,3},{6,0},{7,1},{8,14},{9,15},{10,... | collective-permute-start | bytes 393224 | tf_op jit(solution)/shard_map/ppermute | solution.py:69
  95.2 9.0 %collective-permute-start.19 = (bf16[2,2,128,128]{3,2,1,0:T(8,128)(2,1)S(1)}, bf16[2,2,128,128]{3,2,1,0:T(8,128)(2,1)S(1)}, u32[]{:S(2)}, u32[]{:S(2)}) collective-permute-start(bf16[2,2,128,128]{3,2,1,0:T(8,128)(2,1)S(1)} %get-tuple-element.78), channel_id=1, source_target_pairs={{0,2},{1,3},{2,0},{3,1},{4,6},{5,7},{6,4},{7,5},{8,10},{9,11},{10,... | collective-permute-start | bytes 393224 | tf_op jit(solution)/shard_map/ppermute | solution.py:69
  96.4 10.5 %collective-permute-start.20 = (bf16[2,2,128,128]{3,2,1,0:T(8,128)(2,1)S(1)}, bf16[2,2,128,128]{3,2,1,0:T(8,128)(2,1)S(1)}, u32[]{:S(2)}, u32[]{:S(2)}) collective-permute-start(bf16[2,2,128,128]{3,2,1,0:T(8,128)(2,1)S(1)} %get-tuple-element.79), channel_id=1, source_target_pairs={{0,4},{1,5},{2,6},{3,7},{4,0},{5,1},{6,2},{7,3},{8,12},{9,13},{10,... | collective-permute-start | bytes 393224 | tf_op jit(solution)/shard_map/ppermute | solution.py:69
  98.1 9.4 %collective-permute-start.21 = (bf16[2,2,128,128]{3,2,1,0:T(8,128)(2,1)S(1)}, bf16[2,2,128,128]{3,2,1,0:T(8,128)(2,1)S(1)}, u32[]{:S(2)}, u32[]{:S(2)}) collective-permute-start(bf16[2,2,128,128]{3,2,1,0:T(8,128)(2,1)S(1)} %get-tuple-element.80), channel_id=1, source_target_pairs={{0,6},{1,7},{2,4},{3,5},{4,2},{5,3},{6,0},{7,1},{8,14},{9,15},{10,... | collective-permute-start | bytes 393224 | tf_op jit(solution)/shard_map/ppermute | solution.py:69
  101.3 8.1 %collective-permute-start.16 = (bf16[1,4,128,128]{3,2,1,0:T(8,128)(2,1)S(1)}, bf16[1,4,128,128]{3,2,1,0:T(8,128)(2,1)S(1)}, u32[]{:S(2)}, u32[]{:S(2)}) collective-permute-start(bf16[1,4,128,128]{3,2,1,0:T(8,128)(2,1)S(1)} %get-tuple-element.74), channel_id=1, source_target_pairs={{0,2},{1,3},{2,0},{3,1},{4,6},{5,7},{6,4},{7,5},{8,10},{9,11},{10,... | collective-permute-start | bytes 393224 | tf_op jit(solution)/shard_map/ppermute | solution.py:69
  102.4 7.7 %collective-permute-start.17 = (bf16[1,4,128,128]{3,2,1,0:T(8,128)(2,1)S(1)}, bf16[1,4,128,128]{3,2,1,0:T(8,128)(2,1)S(1)}, u32[]{:S(2)}, u32[]{:S(2)}) collective-permute-start(bf16[1,4,128,128]{3,2,1,0:T(8,128)(2,1)S(1)} %get-tuple-element.75), channel_id=1, source_target_pairs={{0,4},{1,5},{2,6},{3,7},{4,0},{5,1},{6,2},{7,3},{8,12},{9,13},{10,... | collective-permute-start | bytes 393224 | tf_op jit(solution)/shard_map/ppermute | solution.py:69
  104.2 8.3 %collective-permute-start.18 = (bf16[1,4,128,128]{3,2,1,0:T(8,128)(2,1)S(1)}, bf16[1,4,128,128]{3,2,1,0:T(8,128)(2,1)S(1)}, u32[]{:S(2)}, u32[]{:S(2)}) collective-permute-start(bf16[1,4,128,128]{3,2,1,0:T(8,128)(2,1)S(1)} %get-tuple-element.76), channel_id=1, source_target_pairs={{0,6},{1,7},{2,4},{3,5},{4,2},{5,3},{6,0},{7,1},{8,14},{9,15},{10,... | collective-permute-start | bytes 393224 | tf_op jit(solution)/shard_map/ppermute | solution.py:69
where the time goes:
time: 114 us
  waiting for transfers between devices  39.7 us (35%)
  starting transfers between devices  37.5 us (33%)
  Pallas kernels  35.8 us (31%)
    ppermute x19, waiting for transfers between devices, over_frame(): return lax.ppermute(value, 'frame', [(i, i ^ step) for i in range(count)])  28.4 us
    ppermute x19, starting transfers between devices, over_frame(): return lax.ppermute(value, 'frame', [(i, i ^ step) for i in range(count)])  18.8 us
    pallas_call x2, Pallas kernels, grads(): pl.pallas_call(functools.partial(grads_kernel, plan, span, first, last),...  17.7 us
    ppermute x6, waiting for transfers between devices, over_head(): return lax.ppermute(value, 'head', [(i, i ^ step) for i in range(count)])  11.3 us
    ppermute x6, starting transfers between devices, over_head(): return lax.ppermute(value, 'head', [(i, i ^ step) for i in range(count)])  10.3 us
    all_to_all x1, starting transfers between devices, local(): lax.all_to_all(prep(plan, queries, key_states), ('frame', 'head'), 0, 0,...  8.34 us
    pallas_call x1, Pallas kernels, totals(): pl.pallas_call(functools.partial(totals_kernel, plan), out_shape=[sds((pl...  5.88 us
    pallas_call x1, Pallas kernels, lists(): pl.pallas_call(functools.partial(lists_kernel, plan), out_shape=[sds((own...  3.47 us
  transfers between devices with their start and end apart: 26, of which 15 were waited for; matrix products, arithmetic and copies ran while one was open for 0% of the time, Pallas kernels for 20%

commit v1 on v0

--- a/solution.py
+++ b/solution.py
@@ -85,45 +85,32 @@
     return pl.ds(pl.multiple_of((ids[1] ^ s) * HEAD_DIM, HEAD_DIM), HEAD_DIM)
 
 
-def prep_kernel(plan, q_ref, k_ref, out):
-    hd, rows = HEAD_DIM, plan.rows
-    for a in range(plan.na):
-        for z in range(plan.nz):
-            head, place = z * plan.hh + a, a * plan.nz + z
-            out[place, :rows] = q_ref[:, head * hd : (head + 1) * hd]
-            out[place, rows:] = k_ref[:, head * hd : (head + 1) * hd]
-
-
-def prep(plan, q, k):
+def prep_kernel(plan, head_first, ids, x_ref, *refs):
+    outs, buf, sems = refs[:-2], refs[-2], refs[-1]
+    copies = bundles(plan, ids, [x_ref], [buf], sems)
+    for r in range(plan.nz):
+        copies[r].wait()
+        for s in range(plan.na):
+            piece = buf[r, :, within_bundle(ids, s)]
+            if head_first:
+                outs[r][s] = piece
+            else:
+                outs[s][r] = piece
+
+
+def prep(plan, ids, x, head_first):
+    pieces, chunk = (plan.nz, plan.na) if head_first else (plan.na, plan.nz)
     return pl.pallas_call(
-        functools.partial(prep_kernel, plan),
-        out_shape=sds((plan.own, 2 * plan.rows, HEAD_DIM), BF16),
-        in_specs=[VMEM] * 2,
-        out_specs=VMEM,
-        cost_estimate=lasts(1.5),
+        functools.partial(prep_kernel, plan, head_first),
+        out_shape=[sds((chunk, plan.rows, HEAD_DIM), BF16)] * pieces,
+        in_specs=[SMEM, HBM],
+        out_specs=[VMEM] * pieces,
+        scratch_shapes=[
+            pltpu.VMEM((plan.nz, plan.rows, plan.hh * HEAD_DIM), BF16),
+            pltpu.SemaphoreType.DMA((1, plan.nz)),
+        ],
+        cost_estimate=lasts(1.2),
         compiler_params=pltpu.CompilerParams(vmem_limit_bytes=60 << 20),
-        name="prep",
-    )(q, k)
-
-
-def part_kernel(plan, ids, x_ref, q_out, k_out):
-    rows = plan.rows
-    for s in range(plan.na):
-        for r in range(plan.nz):
-            place = (ids[1] ^ s) * plan.nz + (ids[0] ^ r)
-            q_out[s * plan.nz + r] = x_ref[place, :rows]
-            k_out[s * plan.nz + r] = x_ref[place, rows:]
-
-
-def part(plan, ids, x):
-    return pl.pallas_call(
-        functools.partial(part_kernel, plan),
-        out_shape=[sds((plan.own, plan.rows, HEAD_DIM), BF16)] * 2,
-        in_specs=[SMEM, VMEM],
-        out_specs=[VMEM] * 2,
-        cost_estimate=lasts(1),
-        compiler_params=within(x, x),
-        name="part",
     )(ids, x)
 
 
@@ -163,28 +150,28 @@
         scratch_shapes=[pltpu.VMEM((nz, rows, plan.hh * hd), BF16)] * 3
         + [pltpu.SemaphoreType.DMA((3, nz))],
         cost_estimate=lasts(2),
-        compiler_params=within(g, o, v, g, v),
+        compiler_params=pltpu.CompilerParams(vmem_limit_bytes=58 << 20),
         name="prep_rest",
     )(ids, g, o, v)
     return outs[:na], outs[na:]
 
 
-def turn_kernel(count, *refs):
+def turn_kernel(count, turned, *refs):
     pieces, outs = refs[:count], refs[count:]
-    joined = len(outs) == 1
-    for c in range(pieces[0].shape[0]):
+    joined, parts = len(outs) == 1, pieces[0].shape[0]
+    for c in range(parts):
         for p, piece in enumerate(pieces):
             if joined:
-                outs[0][c * count + p] = piece[c]
+                outs[0][c * count + p if turned else p * parts + c] = piece[c]
             else:
                 outs[c][p] = piece[c]
 
 
-def turn(pieces, joined=False):
+def turn(pieces, joined=False, turned=True):
     count, parts, shape = len(pieces), pieces[0].shape[0], pieces[0].shape[1:]
     out = [sds((parts * count, *shape), BF16)] if joined else [sds((count, *shape), BF16)] * parts
     outs = pl.pallas_call(
-        functools.partial(turn_kernel, count),
+        functools.partial(turn_kernel, count, turned),
         out_shape=out,
         in_specs=[VMEM] * count,
         out_specs=[VMEM] * len(out),
@@ -550,20 +537,17 @@
     def swapped(parts):
         return staged(range(1, nb), parts, over_frame)
 
-    groups = [
-        [(a * nb + b) * nz + z for a in range(na) for z in range(nz)] for b in range(nb)
-    ]
-    mine = lax.all_to_all(
-        prep(plan, queries, key_states), ("frame", "head"), 0, 0,
-        tiled=True, axis_index_groups=groups,
-    )
+    q_sent = head_stage(prep(plan, ids, queries, True))
+    k_near = frame_stage(prep(plan, ids, key_states, False))
     g_near, v_near = prep_rest(plan, ids, grad_out, attn_out, value_states)
     g_near = frame_stage(g_near)
     v_near = frame_stage(v_near)
     by_key, n_key = lists(plan, ids, frame_order, block_live.transpose(1, 2, 0))
     g_own = turn(head_stage(turn(g_near)), joined=True)
     values = head_stage(turn(v_near))
-    q_own, keys = part(plan, ids, mine)
+    keys = turn(head_stage(turn(k_near)), joined=True)
+    q_near = frame_stage(turn(q_sent))
+    q_own = turn(q_near, joined=True, turned=False)
     lse_part, q_all = totals(plan, by_key, n_key, keys, swapped([q_own] * nb))
     lse, delta, g_all = query_rows(plan, swapped([g_own] * nb), swapped([lse_part] * nb))
     spans = [range(0, 2), range(2, nz)]

time: 114 us -> 135 us (1.18)
  the two profiles are of different devices: /device:TPU:0 before, /device:TPU:4 now
where the time goes in v1:
time: 135 us; the launch traced here: 133 us
  starting transfers between devices  46.5 us (34%)
  waiting for transfers between devices  42.3 us (31%)
  Pallas kernels  39.7 us (29%)
  local copies, waits for them, and re-layouts  2.74 us (2%)
    ppermute x25, starting transfers between devices, over_frame(): return lax.ppermute(value, 'frame', [(i, i ^ step) for i in range(count)])  25.7 us
    ppermute x25, waiting for transfers between devices, over_frame(): return lax.ppermute(value, 'frame', [(i, i ^ step) for i in range(count)])  22.4 us
    ppermute x12, starting transfers between devices, over_head(): return lax.ppermute(value, 'head', [(i, i ^ step) for i in range(count)])  20.8 us
    ppermute x12, waiting for transfers between devices, over_head(): return lax.ppermute(value, 'head', [(i, i ^ step) for i in range(count)])  19.9 us
    pallas_call x2, Pallas kernels, grads(): pl.pallas_call(functools.partial(grads_kernel, plan, span, first, last),...  17.7 us
    pallas_call x1, Pallas kernels, totals(): pl.pallas_call(functools.partial(totals_kernel, plan), out_shape=[sds((pl...  5.87 us
    pallas_call x2, Pallas kernels, prep(): pl.pallas_call(functools.partial(prep_kernel, plan, head_first), out_shap...  5.21 us
    pallas_call x1, Pallas kernels, prep_rest(): pl.pallas_call(functools.partial(prep_rest_kernel, plan), out_shape=[sds(...  3.8 us
  transfers between devices with their start and end apart: 37, of which 16 were waited for; matrix products, arithmetic and copies ran while one was open for 0% of the time, Pallas kernels for 19%

profile of v1, /device:TPU:4, one launch (start us, length us, event | category | flops | bytes accessed | tf_op | source)
XLA Modules:
  0.0 132.8 jit_solution(11207867321151354914)
XLA Ops:
  0.6 0.6 pad_add_fusion.ids
  1.2 3.8 %prep_rest.1 = (bf16[4,136,128]{2,1,0:T(8,128)(2,1)}, bf16[4,136,128]{2,1,0:T(8,128)(2,1)}, bf16[4,136,128]{2,1,0:T(8,128)(2,1)}, bf16[4,136,128]{2,1,0:T(8,128)...) custom-call(s32[3]{0:T(128)} %pad_add_fusion.ids, ...), custom_call_target="tpu_custom_call" | custom-call | bytes 7000000 | tf_op jit(solution)/shard_map/prep_rest/pallas_call | solution.py:145
  5.0 1.6 %collective-permute-start.13 = (bf16[4,136,128]{2,1,0:T(8,128)(2,1)}, bf16[4,136,128]{2,1,0:T(8,128)(2,1)S(1)}, u32[]{:S(2)}, u32[]{:S(2)}) collective-permute-start(bf16[4,136,128]{2,1,0:T(8,128)(2,1)} %get-tuple-element.79), channel_id=1, source_target_pairs={{0,2},{1,3},{2,0},{3,1},{4,6},{5,7},{6,4},{7,5},{8,10},{9,11},{10,... | collective-permute-start | bytes 417800 | tf_op jit(solution)/shard_map/ppermute | solution.py:69
  6.6 0.5 collective-permute-start.14
  7.1 1.5 %collective-permute-start.15 = (bf16[4,136,128]{2,1,0:T(8,128)(2,1)}, bf16[4,136,128]{2,1,0:T(8,128)(2,1)S(1)}, u32[]{:S(2)}, u32[]{:S(2)}) collective-permute-start(bf16[4,136,128]{2,1,0:T(8,128)(2,1)} %get-tuple-element.81), channel_id=1, source_target_pairs={{0,6},{1,7},{2,4},{3,5},{4,2},{5,3},{6,0},{7,1},{8,14},{9,15},{10,... | collective-permute-start | bytes 417800 | tf_op jit(solution)/shard_map/ppermute | solution.py:69
  8.6 2.6 %shard_map.97 = (bf16[4,128,128]{2,1,0:T(8,128)(2,1)}, bf16[4,128,128]{2,1,0:T(8,128)(2,1)}, bf16[4,128,128]{2,1,0:T(8,128)(2,1)}, bf16[4,128,128]{2,1,0:T(8,128)(2,1)}) custom-call(s32[3]{0:T(128)} %pad_add_fusion.ids, bf16[128,2048]{1,0:T(8,128)(2,1)} %x_ref.3), custom_call_target="tpu_custom_call" | custom-call | bytes 4200000 | tf_op jit(solution)/shard_map/pallas_call | solution.py:103
  11.2 1.6 %collective-permute-start.6 = (bf16[4,128,128]{2,1,0:T(8,128)(2,1)}, bf16[4,128,128]{2,1,0:T(8,128)(2,1)S(1)}, u32[]{:S(2)}, u32[]{:S(2)}) collective-permute-start(bf16[4,128,128]{2,1,0:T(8,128)(2,1)} %get-tuple-element.70), channel_id=1, source_target_pairs={{0,8},{8,0},{16,24},{24,16},{1,9},{9,1},{17,25},{25,17},{2,10},{10... | collective-permute-start | bytes 393224 | tf_op jit(solution)/shard_map/ppermute | solution.py:64
  12.9 0.0 collective-permute-done.13.refs_1_
  12.9 2.1 %collective-permute-done.14.refs_2_ = bf16[4,136,128]{2,1,0:T(8,128)(2,1)S(1)} collective-permute-done((bf16[4,136,128]{2,1,0:T(8,128)(2,1)}, bf16[4,136,128]{2,1,0:T(8,128)(2,1)S(1)}, u32[]{:S(2)}, u32[]{:S(2)}) %collective-permute-start.14) | collective-permute-done | bytes 139296 | tf_op jit(solution)/shard_map/ppermute | solution.py:69
  14.9 0.9 copy-done
  15.9 1.6 %collective-permute-start.16 = (bf16[4,136,128]{2,1,0:T(8,128)(2,1)S(1)}, bf16[4,136,128]{2,1,0:T(8,128)(2,1)S(1)}, u32[]{:S(2)}, u32[]{:S(2)}) collective-permute-start(bf16[4,136,128]{2,1,0:T(8,128)(2,1)S(1)} %get-tuple-element.83), channel_id=1, source_target_pairs={{0,8},{8,0},{16,24},{24,16},{1,9},{9,1},{17,25},{25,17},{2,10},{10... | collective-permute-start | bytes 417800 | tf_op jit(solution)/shard_map/ppermute | solution.py:64
  17.5 2.6 %collective-permute-start.7 = (bf16[4,128,128]{2,1,0:T(8,128)(2,1)}, bf16[4,128,128]{2,1,0:T(8,128)(2,1)S(1)}, u32[]{:S(2)}, u32[]{:S(2)}) collective-permute-start(bf16[4,128,128]{2,1,0:T(8,128)(2,1)} %get-tuple-element.71), channel_id=1, source_target_pairs={{0,16},{8,24},{16,0},{24,8},{1,17},{9,25},{17,1},{25,9},{2,18},{10... | collective-permute-start | bytes 393224 | tf_op jit(solution)/shard_map/ppermute | solution.py:64
  20.1 0.2 collective-permute-start.8
  20.3 1.7 %collective-permute-start.17 = (bf16[4,136,128]{2,1,0:T(8,128)(2,1)S(1)}, bf16[4,136,128]{2,1,0:T(8,128)(2,1)S(1)}, u32[]{:S(2)}, u32[]{:S(2)}) collective-permute-start(bf16[4,136,128]{2,1,0:T(8,128)(2,1)S(1)} %get-tuple-element.84), channel_id=1, source_target_pairs={{0,16},{8,24},{16,0},{24,8},{1,17},{9,25},{17,1},{25,9},{2,18},{10... | collective-permute-start | bytes 417800 | tf_op jit(solution)/shard_map/ppermute | solution.py:64
  22.0 1.9 %collective-permute-start.18 = (bf16[4,136,128]{2,1,0:T(8,128)(2,1)S(1)}, bf16[4,136,128]{2,1,0:T(8,128)(2,1)S(1)}, u32[]{:S(2)}, u32[]{:S(2)}) collective-permute-start(bf16[4,136,128]{2,1,0:T(8,128)(2,1)S(1)} %get-tuple-element.85), channel_id=1, source_target_pairs={{0,24},{8,16},{16,8},{24,0},{1,25},{9,17},{17,9},{25,1},{2,26},{10... | collective-permute-start | bytes 417800 | tf_op jit(solution)/shard_map/ppermute | solution.py:64
  23.9 11.1 %collective-permute-done.7.refs_2_ = bf16[4,128,128]{2,1,0:T(8,128)(2,1)S(1)} collective-permute-done((bf16[4,128,128]{2,1,0:T(8,128)(2,1)}, bf16[4,128,128]{2,1,0:T(8,128)(2,1)S(1)}, u32[]{:S(2)}, u32[]{:S(2)}) %collective-permute-start.7) | collective-permute-done | bytes 131104 | tf_op jit(solution)/shard_map/ppermute | solution.py:64
  35.1 0.9 copy-done.2
  36.0 1.2 collective-permute-start.9
  37.2 1.3 collective-permute-start.10
  38.5 1.0 collective-permute-start.11
  39.6 0.9 collective-permute-done.17.refs_2_
  40.5 0.1 collective-permute-start.19
  40.6 0.5 collective-permute-done.9.refs_1_
  41.0 1.1 collective-permute-done.10.refs_2_
  42.2 2.2 %collective-permute-done.11.refs_3_ = bf16[4,128,128]{2,1,0:T(8,128)(2,1)S(1)} collective-permute-done((bf16[4,128,128]{2,1,0:T(8,128)(2,1)S(1)}, bf16[4,128,128]{2,1,0:T(8,128)(2,1)S(1)}, u32[]{:S(2)}, u32[]{:S(2)}) %collective-permute-start.11) | collective-permute-done | bytes 131104 | tf_op jit(solution)/shard_map/ppermute | solution.py:69
  44.4 0.1 collective-permute-start.12
  44.5 2.6 %shard_map.94 = (bf16[4,128,128]{2,1,0:T(8,128)(2,1)}, bf16[4,128,128]{2,1,0:T(8,128)(2,1)}, bf16[4,128,128]{2,1,0:T(8,128)(2,1)}, bf16[4,128,128]{2,1,0:T(8,128)(2,1)}) custom-call(s32[3]{0:T(128)} %pad_add_fusion.ids, bf16[128,2048]{1,0:T(8,128)(2,1)} %x_ref.2), custom_call_target="tpu_custom_call" | custom-call | bytes 4200000 | tf_op jit(solution)/shard_map/pallas_call | solution.py:103
  47.1 0.7 collective-permute-start
  47.8 1.0 collective-permute-start.1
  48.8 1.9 %collective-permute-start.2 = (bf16[4,128,128]{2,1,0:T(8,128)(2,1)}, bf16[4,128,128]{2,1,0:T(8,128)(2,1)S(1)}, u32[]{:S(2)}, u32[]{:S(2)}) collective-permute-start(bf16[4,128,128]{2,1,0:T(8,128)(2,1)} %get-tuple-element.64), channel_id=1, source_target_pairs={{0,6},{1,7},{2,4},{3,5},{4,2},{5,3},{6,0},{7,1},{8,14},{9,15},{10,... | collective-permute-start | bytes 393224 | tf_op jit(solution)/shard_map/ppermute | solution.py:69
  50.7 3.1 %collective-permute-done.refs_1_ = bf16[4,128,128]{2,1,0:T(8,128)(2,1)S(1)} collective-permute-done((bf16[4,128,128]{2,1,0:T(8,128)(2,1)}, bf16[4,128,128]{2,1,0:T(8,128)(2,1)S(1)}, u32[]{:S(2)}, u32[]{:S(2)}) %collective-permute-start) | collective-permute-done | bytes 131104 | tf_op jit(solution)/shard_map/ppermute | solution.py:69
  53.8 0.6 collective-permute-start.21
  54.4 1.9 %collective-permute-done.1.refs_2_ = bf16[4,128,128]{2,1,0:T(8,128)(2,1)S(1)} collective-permute-done((bf16[4,128,128]{2,1,0:T(8,128)(2,1)}, bf16[4,128,128]{2,1,0:T(8,128)(2,1)S(1)}, u32[]{:S(2)}, u32[]{:S(2)}) %collective-permute-start.1) | collective-permute-done | bytes 131104 | tf_op jit(solution)/shard_map/ppermute | solution.py:69
  56.2 0.5 collective-permute-done.2.refs_3_
  56.8 2.9 %collective-permute-start.23 = (bf16[4,128,128]{2,1,0:T(8,128)(2,1)S(1)}, bf16[4,128,128]{2,1,0:T(8,128)(2,1)S(1)}, u32[]{:S(2)}, u32[]{:S(2)}) collective-permute-start(bf16[4,128,128]{2,1,0:T(8,128)(2,1)S(1)} %copy-done.7), channel_id=1, source_target_pairs={{0,6},{1,7},{2,4},{3,5},{4,2},{5,3},{6,0},{7,1},{8,14},{9,15},{10,... | collective-permute-start | bytes 393224 | tf_op jit(solution)/shard_map/ppermute | solution.py:69
  59.6 0.9 copy-done.3
  60.6 3.4 %collective-permute-start.3 = (bf16[4,128,128]{2,1,0:T(8,128)(2,1)S(1)}, bf16[4,128,128]{2,1,0:T(8,128)(2,1)S(1)}, u32[]{:S(2)}, u32[]{:S(2)}) collective-permute-start(bf16[4,128,128]{2,1,0:T(8,128)(2,1)S(1)} %get-tuple-element.66), channel_id=1, source_target_pairs={{0,8},{8,0},{16,24},{24,16},{1,9},{9,1},{17,25},{25,17},{2,10},{10... | collective-permute-start | bytes 393224 | tf_op jit(solution)/shard_map/ppermute | solution.py:64
  64.0 4.2 %collective-permute-start.4 = (bf16[4,128,128]{2,1,0:T(8,128)(2,1)S(1)}, bf16[4,128,128]{2,1,0:T(8,128)(2,1)S(1)}, u32[]{:S(2)}, u32[]{:S(2)}) collective-permute-start(bf16[4,128,128]{2,1,0:T(8,128)(2,1)S(1)} %get-tuple-element.67), channel_id=1, source_target_pairs={{0,16},{8,24},{16,0},{24,8},{1,17},{9,25},{17,1},{25,9},{2,18},{10... | collective-permute-start | bytes 393224 | tf_op jit(solution)/shard_map/ppermute | solution.py:64
  68.2 1.2 collective-permute-start.5
  69.4 1.0 collective-permute-start.26
  70.4 7.9 %collective-permute-done.4.refs_2_ = bf16[4,128,128]{2,1,0:T(8,128)(2,1)S(1)} collective-permute-done((bf16[4,128,128]{2,1,0:T(8,128)(2,1)S(1)}, bf16[4,128,128]{2,1,0:T(8,128)(2,1)S(1)}, u32[]{:S(2)}, u32[]{:S(2)}) %collective-permute-start.4) | collective-permute-done | bytes 131104 | tf_op jit(solution)/shard_map/ppermute | solution.py:64
  78.3 1.4 %collective-permute-start.25 = (bf16[4,128,128]{2,1,0:T(8,128)(2,1)S(1)}, bf16[4,128,128]{2,1,0:T(8,128)(2,1)S(1)}, u32[]{:S(2)}, u32[]{:S(2)}) collective-permute-start(bf16[4,128,128]{2,1,0:T(8,128)(2,1)S(1)} %get-tuple-element.95), channel_id=1, source_target_pairs={{0,24},{8,16},{16,8},{24,0},{1,25},{9,17},{17,9},{25,1},{2,26},{10... | collective-permute-start | bytes 393224 | tf_op jit(solution)/shard_map/ppermute | solution.py:64
  79.7 3.5 %lists.1 = (s32[16,42]{1,0:T(8,128)S(1)}, s32[16]{0:T(128)S(1)}) custom-call(s32[3]{0:T(128)S(1)} %copy-done.4, s32[8]{0:T(128)S(1)} %copy-done.6, s32[4,4,8]{2,1,0:T(4,128)S(1)} %bitcast.4), custom_call_target="tpu_custom_call" | custom-call | bytes 10500000 | tf_op jit(solution)/shard_map/lists/pallas_call | solution.py:229
  83.3 5.9 %totals.1 = (f32[32,128]{1,0:T(8,128)S(1)}, bf16[32,128,128]{2,1,0:T(8,128)(2,1)S(1)}) custom-call(s32[16,42]{1,0:T(8,128)S(1)} %get-tuple-element.59.by_key, s32[16]{0:T(128)S(1)} %get-tuple-element.60.n_key, bf16[16,128,128]{2,1,0:T(8,128)(2,1)S(1)} %shard_map.96.k_ref, bf16[16,128,128]{2,1,0:T(8,128)(2,1)S(1)} %shard_map.99.refs_0_, ...), custom_call_target="tpu_custom_call" | custom-call | bytes 21000000 | tf_op jit(solution)/shard_map/totals/pallas_call | solution.py:317
  89.1 0.1 collective-permute-start.20
  89.2 1.2 collective-permute-done.20.refs_3_
  90.4 0.1 query_rows.1
  90.5 8.6 %shard_map.103 = (bf16[2,2,128,128]{3,2,1,0:T(8,128)(2,1)S(1)}, bf16[2,2,128,128]{3,2,1,0:T(8,128)(2,1)S(1)}, bf16[2,2,128,128]{3,2,1,0:T(8,128)(2,1)S(1)}, bf16...) custom-call(s32[16,42]{1,0:T(8,128)S(1)} %get-tuple-element.59.by_key, s32[16]{0:T(128)S(1)} %get-tuple-element.60.n_key, ...), custom_call_target="tpu_custom_call" | custom-call | bytes 24500000 | tf_op jit(solution)/shard_map/pallas_call | solution.py:460
  99.2 9.1 %shard_map.104 = (bf16[2,2,128,128]{3,2,1,0:T(8,128)(2,1)S(1)}, bf16[2,2,128,128]{3,2,1,0:T(8,128)(2,1)S(1)}, bf16[2,2,128,128]{3,2,1,0:T(8,128)(2,1)S(1)}, bf16...) custom-call(s32[16,42]{1,0:T(8,128)S(1)} %get-tuple-element.59.by_key, ...), custom_call_target="tpu_custom_call" | custom-call | bytes 24500000 | tf_op jit(solution)/shard_map/pallas_call | solution.py:460
  108.3 0.2 collective-permute-start.27
  108.5 3.3 %collective-permute-start.34 = (bf16[2,2,128,128]{3,2,1,0:T(8,128)(2,1)S(1)}, bf16[2,2,128,128]{3,2,1,0:T(8,128)(2,1)S(1)}, u32[]{:S(2)}, u32[]{:S(2)}) collective-permute-start(bf16[2,2,128,128]{3,2,1,0:T(8,128)(2,1)S(1)} %get-tuple-element.110), channel_id=1, source_target_pairs={{0,2},{1,3},{2,0},{3,1},{4,6},{5,7},{6,4},{7,5},{8,10},{9,11},{10,... | collective-permute-start | bytes 393224 | tf_op jit(solution)/shard_map/ppermute | solution.py:69
  111.8 1.5 %collective-permute-start.36 = (bf16[2,2,128,128]{3,2,1,0:T(8,128)(2,1)S(1)}, bf16[2,2,128,128]{3,2,1,0:T(8,128)(2,1)S(1)}, u32[]{:S(2)}, u32[]{:S(2)}) collective-permute-start(bf16[2,2,128,128]{3,2,1,0:T(8,128)(2,1)S(1)} %get-tuple-element.112), channel_id=1, source_target_pairs={{0,6},{1,7},{2,4},{3,5},{4,2},{5,3},{6,0},{7,1},{8,14},{9,15},{10,... | collective-permute-start | bytes 393224 | tf_op jit(solution)/shard_map/ppermute | solution.py:69
  113.3 2.0 %collective-permute-start.31 = (bf16[2,2,128,128]{3,2,1,0:T(8,128)(2,1)S(1)}, bf16[2,2,128,128]{3,2,1,0:T(8,128)(2,1)S(1)}, u32[]{:S(2)}, u32[]{:S(2)}) collective-permute-start(bf16[2,2,128,128]{3,2,1,0:T(8,128)(2,1)S(1)} %get-tuple-element.106), channel_id=1, source_target_pairs={{0,2},{1,3},{2,0},{3,1},{4,6},{5,7},{6,4},{7,5},{8,10},{9,11},{10,... | collective-permute-start | bytes 393224 | tf_op jit(solution)/shard_map/ppermute | solution.py:69
  115.3 0.0 collective-permute-start.32
  115.3 0.2 pack.1
  115.5 0.5 collective-permute-done.34.refs_5_
  116.0 1.5 %collective-permute-start.33 = (bf16[2,2,128,128]{3,2,1,0:T(8,128)(2,1)S(1)}, bf16[2,2,128,128]{3,2,1,0:T(8,128)(2,1)S(1)}, u32[]{:S(2)}, u32[]{:S(2)}) collective-permute-start(bf16[2,2,128,128]{3,2,1,0:T(8,128)(2,1)S(1)} %get-tuple-element.108), channel_id=1, source_target_pairs={{0,6},{1,7},{2,4},{3,5},{4,2},{5,3},{6,0},{7,1},{8,14},{9,15},{10,... | collective-permute-start | bytes 393224 | tf_op jit(solution)/shard_map/ppermute | solution.py:69
  117.4 4.4 %collective-permute-done.35.refs_6_ = bf16[2,2,128,128]{3,2,1,0:T(8,128)(2,1)S(1)} collective-permute-done((bf16[2,2,128,128]{3,2,1,0:T(8,128)(2,1)S(1)}, bf16[2,2,128,128]{3,2,1,0:T(8,128)(2,1)S(1)}, u32[]{:S(2)}, u32[]{:S(2)}) %collective-permute-start.35) | collective-permute-done | bytes 131104 | tf_op jit(solution)/shard_map/ppermute | solution.py:69
  121.8 0.7 collective-permute-done.31.refs_1_
  122.5 2.8 %collective-permute-start.30 = (bf16[1,4,128,128]{3,2,1,0:T(8,128)(2,1)S(1)}, bf16[1,4,128,128]{3,2,1,0:T(8,128)(2,1)S(1)}, u32[]{:S(2)}, u32[]{:S(2)}) collective-permute-start(bf16[1,4,128,128]{3,2,1,0:T(8,128)(2,1)S(1)} %get-tuple-element.104), channel_id=1, source_target_pairs={{0,6},{1,7},{2,4},{3,5},{4,2},{5,3},{6,0},{7,1},{8,14},{9,15},{10,... | collective-permute-start | bytes 393224 | tf_op jit(solution)/shard_map/ppermute | solution.py:69
  125.3 2.1 %collective-permute-done.32.refs_2_ = bf16[2,2,128,128]{3,2,1,0:T(8,128)(2,1)S(1)} collective-permute-done((bf16[2,2,128,128]{3,2,1,0:T(8,128)(2,1)S(1)}, bf16[2,2,128,128]{3,2,1,0:T(8,128)(2,1)S(1)}, u32[]{:S(2)}, u32[]{:S(2)}) %collective-permute-start.32) | collective-permute-done | bytes 131104 | tf_op jit(solution)/shard_map/ppermute | solution.py:69
  127.4 1.7 %shard_map.106 = (bf16[512,512]{1,0:T(8,128)(2,1)}, bf16[512,512]{1,0:T(8,128)(2,1)}) custom-call(s32[3]{0:T(128)S(1)} %copy-done.4, bf16[2,2,128,128]{3,2,1,0:T(8,128)(2,1)S(1)} %get-tuple-element.105.refs_0_, bf16[2,2,128,128]{3,2,1,0:T(8,128)(2,1)S(1)} %collective-permute-done.31.refs_1_, bf16[2,2,128,128]{3,2,1,0:T(8,128)(2,1)S(1)} %collective-permute-done.32.refs_2_, ...), custom_call_target="tpu_custom_call" | custom-call | bytes 5250000 | tf_op jit(solution)/shard_map/pallas_call | solution.py:509
  129.1 2.2 %collective-permute-done.29.refs_2_ = bf16[1,4,128,128]{3,2,1,0:T(8,128)(2,1)S(1)} collective-permute-done((bf16[1,4,128,128]{3,2,1,0:T(8,128)(2,1)S(1)}, bf16[1,4,128,128]{3,2,1,0:T(8,128)(2,1)S(1)}, u32[]{:S(2)}, u32[]{:S(2)}) %collective-permute-start.29) | collective-permute-done | bytes 131104 | tf_op jit(solution)/shard_map/ppermute | solution.py:69
  131.3 1.4 %shard_map.105 = bf16[512,512]{1,0:T(8,128)(2,1)} custom-call(s32[3]{0:T(128)S(1)} %copy-done.4, bf16[1,4,128,128]{3,2,1,0:T(8,128)(2,1)S(1)} %get-tuple-element.101.refs_0_, bf16[1,4,128,128]{3,2,1,0:T(8,128)(2,1)S(1)} %collective-permute-done.28.refs_1_, bf16[1,4,128,128]{3,2,1,0:T(8,128)(2,1)S(1)} %collective-permute-done.29.refs_2_, ...), custom_call_target="tpu_custom_call" | custom-call | bytes 5250000 | tf_op jit(solution)/shard_map/pallas_call | solution.py:509
  (49 shorter events, 0.4 us)
Async XLA Ops:
  5.0 7.8 %collective-permute-start.13 = (bf16[4,136,128]{2,1,0:T(8,128)(2,1)}, bf16[4,136,128]{2,1,0:T(8,128)(2,1)S(1)}, u32[]{:S(2)}, u32[]{:S(2)}) collective-permute-start(bf16[4,136,128]{2,1,0:T(8,128)(2,1)} %get-tuple-element.79), channel_id=1, source_target_pairs={{0,2},{1,3},{2,0},{3,1},{4,6},{5,7},{6,4},{7,5},{8,10},{9,11},{10,... | collective-permute-start | bytes 417800 | tf_op jit(solution)/shard_map/ppermute | solution.py:69
  6.6 8.3 %collective-permute-start.14 = (bf16[4,136,128]{2,1,0:T(8,128)(2,1)}, bf16[4,136,128]{2,1,0:T(8,128)(2,1)S(1)}, u32[]{:S(2)}, u32[]{:S(2)}) collective-permute-start(bf16[4,136,128]{2,1,0:T(8,128)(2,1)} %get-tuple-element.80), channel_id=1, source_target_pairs={{0,4},{1,5},{2,6},{3,7},{4,0},{5,1},{6,2},{7,3},{8,12},{9,13},{10,... | collective-permute-start | bytes 417800 | tf_op jit(solution)/shard_map/ppermute | solution.py:69
  7.1 46.7 %copy-start.9 = (bf16[4,128,128]{2,1,0:T(8,128)(2,1)S(1)}, bf16[4,128,128]{2,1,0:T(8,128)(2,1)}, u32[]{:S(2)}) copy-start(bf16[4,128,128]{2,1,0:T(8,128)(2,1)} %get-tuple-element.91) | copy-start | bytes 393220
  7.1 49.1 %copy-start.8 = (bf16[4,128,128]{2,1,0:T(8,128)(2,1)S(1)}, bf16[4,128,128]{2,1,0:T(8,128)(2,1)}, u32[]{:S(2)}) copy-start(bf16[4,128,128]{2,1,0:T(8,128)(2,1)} %get-tuple-element.92) | copy-start | bytes 393220
  7.1 49.7 %copy-start.7 = (bf16[4,128,128]{2,1,0:T(8,128)(2,1)S(1)}, bf16[4,128,128]{2,1,0:T(8,128)(2,1)}, u32[]{:S(2)}) copy-start(bf16[4,128,128]{2,1,0:T(8,128)(2,1)} %get-tuple-element.93) | copy-start | bytes 393220
  7.1 7.8 %collective-permute-start.15 = (bf16[4,136,128]{2,1,0:T(8,128)(2,1)}, bf16[4,136,128]{2,1,0:T(8,128)(2,1)S(1)}, u32[]{:S(2)}, u32[]{:S(2)}) collective-permute-start(bf16[4,136,128]{2,1,0:T(8,128)(2,1)} %get-tuple-element.81), channel_id=1, source_target_pairs={{0,6},{1,7},{2,4},{3,5},{4,2},{5,3},{6,0},{7,1},{8,14},{9,15},{10,... | collective-permute-start | bytes 417800 | tf_op jit(solution)/shard_map/ppermute | solution.py:69
  11.2 10.8 %collective-permute-start.6 = (bf16[4,128,128]{2,1,0:T(8,128)(2,1)}, bf16[4,128,128]{2,1,0:T(8,128)(2,1)S(1)}, u32[]{:S(2)}, u32[]{:S(2)}) collective-permute-start(bf16[4,128,128]{2,1,0:T(8,128)(2,1)} %get-tuple-element.70), channel_id=1, source_target_pairs={{0,8},{8,0},{16,24},{24,16},{1,9},{9,1},{17,25},{25,17},{2,10},{10... | collective-permute-start | bytes 393224 | tf_op jit(solution)/shard_map/ppermute | solution.py:64
  14.9 0.9 copy-start
  15.8 53.5 %copy-start.1 = (bf16[4,128,128]{2,1,0:T(8,128)(2,1)S(1)}, bf16[4,128,128]{2,1,0:T(8,128)(2,1)}, u32[]{:S(2)}) copy-start(bf16[4,128,128]{2,1,0:T(8,128)(2,1)} %get-tuple-element.90.refs_0_) | copy-start | bytes 393220
  15.9 22.6 %collective-permute-start.16 = (bf16[4,136,128]{2,1,0:T(8,128)(2,1)S(1)}, bf16[4,136,128]{2,1,0:T(8,128)(2,1)S(1)}, u32[]{:S(2)}, u32[]{:S(2)}) collective-permute-start(bf16[4,136,128]{2,1,0:T(8,128)(2,1)S(1)} %get-tuple-element.83), channel_id=1, source_target_pairs={{0,8},{8,0},{16,24},{24,16},{1,9},{9,1},{17,25},{25,17},{2,10},{10... | collective-permute-start | bytes 417800 | tf_op jit(solution)/shard_map/ppermute | solution.py:64
  17.5 17.5 %collective-permute-start.7 = (bf16[4,128,128]{2,1,0:T(8,128)(2,1)}, bf16[4,128,128]{2,1,0:T(8,128)(2,1)S(1)}, u32[]{:S(2)}, u32[]{:S(2)}) collective-permute-start(bf16[4,128,128]{2,1,0:T(8,128)(2,1)} %get-tuple-element.71), channel_id=1, source_target_pairs={{0,16},{8,24},{16,0},{24,8},{1,17},{9,25},{17,1},{25,9},{2,18},{10... | collective-permute-start | bytes 393224 | tf_op jit(solution)/shard_map/ppermute | solution.py:64
  20.1 14.9 %collective-permute-start.8 = (bf16[4,128,128]{2,1,0:T(8,128)(2,1)}, bf16[4,128,128]{2,1,0:T(8,128)(2,1)S(1)}, u32[]{:S(2)}, u32[]{:S(2)}) collective-permute-start(bf16[4,128,128]{2,1,0:T(8,128)(2,1)} %get-tuple-element.72), channel_id=1, source_target_pairs={{0,24},{8,16},{16,8},{24,0},{1,25},{9,17},{17,9},{25,1},{2,26},{10... | collective-permute-start | bytes 393224 | tf_op jit(solution)/shard_map/ppermute | solution.py:64
  20.3 20.1 %collective-permute-start.17 = (bf16[4,136,128]{2,1,0:T(8,128)(2,1)S(1)}, bf16[4,136,128]{2,1,0:T(8,128)(2,1)S(1)}, u32[]{:S(2)}, u32[]{:S(2)}) collective-permute-start(bf16[4,136,128]{2,1,0:T(8,128)(2,1)S(1)} %get-tuple-element.84), channel_id=1, source_target_pairs={{0,16},{8,24},{16,0},{24,8},{1,17},{9,25},{17,1},{25,9},{2,18},{10... | collective-permute-start | bytes 417800 | tf_op jit(solution)/shard_map/ppermute | solution.py:64
  22.0 18.4 %collective-permute-start.18 = (bf16[4,136,128]{2,1,0:T(8,128)(2,1)S(1)}, bf16[4,136,128]{2,1,0:T(8,128)(2,1)S(1)}, u32[]{:S(2)}, u32[]{:S(2)}) collective-permute-start(bf16[4,136,128]{2,1,0:T(8,128)(2,1)S(1)} %get-tuple-element.85), channel_id=1, source_target_pairs={{0,24},{8,16},{16,8},{24,0},{1,25},{9,17},{17,9},{25,1},{2,26},{10... | collective-permute-start | bytes 417800 | tf_op jit(solution)/shard_map/ppermute | solution.py:64
  35.1 0.9 copy-start.2
  36.0 43.8 %copy-start.4 = (s32[3]{0:T(128)S(1)}, s32[3]{0:T(128)}, u32[]{:S(2)}) copy-start(s32[3]{0:T(128)} %pad_add_fusion.ids) | copy-start | bytes 40
  36.0 43.8 %copy-start.5 = (s32[8,4,4]{0,2,1:T(4,128)S(1)}, s32[8,4,4]{0,2,1:T(4,128)}, u32[]{:S(2)}) copy-start(s32[8,4,4]{0,2,1:T(4,128)} %param.13) | copy-start | bytes 1540
  36.0 43.8 %copy-start.6 = (s32[8]{0:T(128)S(1)}, s32[8]{0:T(128)}, u32[]{:S(2)}) copy-start(s32[8]{0:T(128)} %order.1) | copy-start | bytes 100
  36.0 5.0 %collective-permute-start.9 = (bf16[4,128,128]{2,1,0:T(8,128)(2,1)S(1)}, bf16[4,128,128]{2,1,0:T(8,128)(2,1)S(1)}, u32[]{:S(2)}, u32[]{:S(2)}) collective-permute-start(bf16[4,128,128]{2,1,0:T(8,128)(2,1)S(1)} %get-tuple-element.74), channel_id=1, source_target_pairs={{0,2},{1,3},{2,0},{3,1},{4,6},{5,7},{6,4},{7,5},{8,10},{9,11},{10,... | collective-permute-start | bytes 393224 | tf_op jit(solution)/shard_map/ppermute | solution.py:69
  37.2 5.0 %collective-permute-start.10 = (bf16[4,128,128]{2,1,0:T(8,128)(2,1)S(1)}, bf16[4,128,128]{2,1,0:T(8,128)(2,1)S(1)}, u32[]{:S(2)}, u32[]{:S(2)}) collective-permute-start(bf16[4,128,128]{2,1,0:T(8,128)(2,1)S(1)} %get-tuple-element.75), channel_id=1, source_target_pairs={{0,4},{1,5},{2,6},{3,7},{4,0},{5,1},{6,2},{7,3},{8,12},{9,13},{10,... | collective-permute-start | bytes 393224 | tf_op jit(solution)/shard_map/ppermute | solution.py:69
  38.5 5.9 %collective-permute-start.11 = (bf16[4,128,128]{2,1,0:T(8,128)(2,1)S(1)}, bf16[4,128,128]{2,1,0:T(8,128)(2,1)S(1)}, u32[]{:S(2)}, u32[]{:S(2)}) collective-permute-start(bf16[4,128,128]{2,1,0:T(8,128)(2,1)S(1)} %get-tuple-element.76), channel_id=1, source_target_pairs={{0,6},{1,7},{2,4},{3,5},{4,2},{5,3},{6,0},{7,1},{8,14},{9,15},{10,... | collective-permute-start | bytes 393224 | tf_op jit(solution)/shard_map/ppermute | solution.py:69
  40.5 49.9 %collective-permute-start.19 = (bf16[16,136,128]{2,1,0:T(8,128)(2,1)S(1)}, bf16[16,136,128]{2,1,0:T(8,128)(2,1)S(1)}, u32[]{:S(2)}, u32[]{:S(2)}) collective-permute-start(bf16[16,136,128]{2,1,0:T(8,128)(2,1)S(1)} %shard_map.101.refs_0_), channel_id=1, source_target_pairs={{0,1},{1,0},{2,3},{3,2},{4,5},{5,4},{6,7},{7,6},{8,9},{9,8},{10,11... | collective-permute-start | bytes 1671176 | tf_op jit(solution)/shard_map/ppermute | solution.py:69
  44.4 38.8 %collective-permute-start.12 = (bf16[16,128,128]{2,1,0:T(8,128)(2,1)S(1)}, bf16[16,128,128]{2,1,0:T(8,128)(2,1)S(1)}, u32[]{:S(2)}, u32[]{:S(2)}) collective-permute-start(bf16[16,128,128]{2,1,0:T(8,128)(2,1)S(1)} %shard_map.99.refs_0_), channel_id=1, source_target_pairs={{0,1},{1,0},{2,3},{3,2},{4,5},{5,4},{6,7},{7,6},{8,9},{9,8},{10,11... | collective-permute-start | bytes 1572872 | tf_op jit(solution)/shard_map/ppermute | solution.py:69
  47.1 6.6 %collective-permute-start = (bf16[4,128,128]{2,1,0:T(8,128)(2,1)}, bf16[4,128,128]{2,1,0:T(8,128)(2,1)S(1)}, u32[]{:S(2)}, u32[]{:S(2)}) collective-permute-start(bf16[4,128,128]{2,1,0:T(8,128)(2,1)} %get-tuple-element.62), channel_id=1, source_target_pairs={{0,2},{1,3},{2,0},{3,1},{4,6},{5,7},{6,4},{7,5},{8,10},{9,11},{10,... | collective-permute-start | bytes 393224 | tf_op jit(solution)/shard_map/ppermute | solution.py:69
  47.8 8.4 %collective-permute-start.1 = (bf16[4,128,128]{2,1,0:T(8,128)(2,1)}, bf16[4,128,128]{2,1,0:T(8,128)(2,1)S(1)}, u32[]{:S(2)}, u32[]{:S(2)}) collective-permute-start(bf16[4,128,128]{2,1,0:T(8,128)(2,1)} %get-tuple-element.63), channel_id=1, source_target_pairs={{0,4},{1,5},{2,6},{3,7},{4,0},{5,1},{6,2},{7,3},{8,12},{9,13},{10,... | collective-permute-start | bytes 393224 | tf_op jit(solution)/shard_map/ppermute | solution.py:69
  48.8 8.0 %collective-permute-start.2 = (bf16[4,128,128]{2,1,0:T(8,128)(2,1)}, bf16[4,128,128]{2,1,0:T(8,128)(2,1)S(1)}, u32[]{:S(2)}, u32[]{:S(2)}) collective-permute-start(bf16[4,128,128]{2,1,0:T(8,128)(2,1)} %get-tuple-element.64), channel_id=1, source_target_pairs={{0,6},{1,7},{2,4},{3,5},{4,2},{5,3},{6,0},{7,1},{8,14},{9,15},{10,... | collective-permute-start | bytes 393224 | tf_op jit(solution)/shard_map/ppermute | solution.py:69
  53.8 6.8 %collective-permute-start.21 = (bf16[4,128,128]{2,1,0:T(8,128)(2,1)S(1)}, bf16[4,128,128]{2,1,0:T(8,128)(2,1)S(1)}, u32[]{:S(2)}, u32[]{:S(2)}) collective-permute-start(bf16[4,128,128]{2,1,0:T(8,128)(2,1)S(1)} %copy-done.9), channel_id=1, source_target_pairs={{0,2},{1,3},{2,0},{3,1},{4,6},{5,7},{6,4},{7,5},{8,10},{9,11},{10,... | collective-permute-start | bytes 393224 | tf_op jit(solution)/shard_map/ppermute | solution.py:69
  56.2 7.8 %collective-permute-start.22 = (bf16[4,128,128]{2,1,0:T(8,128)(2,1)S(1)}, bf16[4,128,128]{2,1,0:T(8,128)(2,1)S(1)}, u32[]{:S(2)}, u32[]{:S(2)}) collective-permute-start(bf16[4,128,128]{2,1,0:T(8,128)(2,1)S(1)} %copy-done.8), channel_id=1, source_target_pairs={{0,4},{1,5},{2,6},{3,7},{4,0},{5,1},{6,2},{7,3},{8,12},{9,13},{10,... | collective-permute-start | bytes 393224 | tf_op jit(solution)/shard_map/ppermute | solution.py:69
  56.8 11.4 %collective-permute-start.23 = (bf16[4,128,128]{2,1,0:T(8,128)(2,1)S(1)}, bf16[4,128,128]{2,1,0:T(8,128)(2,1)S(1)}, u32[]{:S(2)}, u32[]{:S(2)}) collective-permute-start(bf16[4,128,128]{2,1,0:T(8,128)(2,1)S(1)} %copy-done.7), channel_id=1, source_target_pairs={{0,6},{1,7},{2,4},{3,5},{4,2},{5,3},{6,0},{7,1},{8,14},{9,15},{10,... | collective-permute-start | bytes 393224 | tf_op jit(solution)/shard_map/ppermute | solution.py:69
  59.6 0.9 copy-start.3
  60.6 8.8 %collective-permute-start.3 = (bf16[4,128,128]{2,1,0:T(8,128)(2,1)S(1)}, bf16[4,128,128]{2,1,0:T(8,128)(2,1)S(1)}, u32[]{:S(2)}, u32[]{:S(2)}) collective-permute-start(bf16[4,128,128]{2,1,0:T(8,128)(2,1)S(1)} %get-tuple-element.66), channel_id=1, source_target_pairs={{0,8},{8,0},{16,24},{24,16},{1,9},{9,1},{17,25},{25,17},{2,10},{10... | collective-permute-start | bytes 393224 | tf_op jit(solution)/shard_map/ppermute | solution.py:64
  64.0 14.3 %collective-permute-start.4 = (bf16[4,128,128]{2,1,0:T(8,128)(2,1)S(1)}, bf16[4,128,128]{2,1,0:T(8,128)(2,1)S(1)}, u32[]{:S(2)}, u32[]{:S(2)}) collective-permute-start(bf16[4,128,128]{2,1,0:T(8,128)(2,1)S(1)} %get-tuple-element.67), channel_id=1, source_target_pairs={{0,16},{8,24},{16,0},{24,8},{1,17},{9,25},{17,1},{25,9},{2,18},{10... | collective-permute-start | bytes 393224 | tf_op jit(solution)/shard_map/ppermute | solution.py:64
  68.2 10.1 %collective-permute-start.5 = (bf16[4,128,128]{2,1,0:T(8,128)(2,1)S(1)}, bf16[4,128,128]{2,1,0:T(8,128)(2,1)S(1)}, u32[]{:S(2)}, u32[]{:S(2)}) collective-permute-start(bf16[4,128,128]{2,1,0:T(8,128)(2,1)S(1)} %get-tuple-element.68), channel_id=1, source_target_pairs={{0,24},{8,16},{16,8},{24,0},{1,25},{9,17},{17,9},{25,1},{2,26},{10... | collective-permute-start | bytes 393224 | tf_op jit(solution)/shard_map/ppermute | solution.py:64
  69.4 21.1 %collective-permute-start.26 = (bf16[4,128,128]{2,1,0:T(8,128)(2,1)S(1)}, bf16[4,128,128]{2,1,0:T(8,128)(2,1)S(1)}, u32[]{:S(2)}, u32[]{:S(2)}) collective-permute-start(bf16[4,128,128]{2,1,0:T(8,128)(2,1)S(1)} %get-tuple-element.97), channel_id=1, source_target_pairs={{0,8},{8,0},{16,24},{24,16},{1,9},{9,1},{17,25},{25,17},{2,10},{10... | collective-permute-start | bytes 393224 | tf_op jit(solution)/shard_map/ppermute | solution.py:64
  78.3 20.8 %collective-permute-start.24 = (bf16[4,128,128]{2,1,0:T(8,128)(2,1)S(1)}, bf16[4,128,128]{2,1,0:T(8,128)(2,1)S(1)}, u32[]{:S(2)}, u32[]{:S(2)}) collective-permute-start(bf16[4,128,128]{2,1,0:T(8,128)(2,1)S(1)} %get-tuple-element.94), channel_id=1, source_target_pairs={{0,16},{8,24},{16,0},{24,8},{1,17},{9,25},{17,1},{25,9},{2,18},{10... | collective-permute-start | bytes 393224 | tf_op jit(solution)/shard_map/ppermute | solution.py:64
  78.3 20.8 %collective-permute-start.25 = (bf16[4,128,128]{2,1,0:T(8,128)(2,1)S(1)}, bf16[4,128,128]{2,1,0:T(8,128)(2,1)S(1)}, u32[]{:S(2)}, u32[]{:S(2)}) collective-permute-start(bf16[4,128,128]{2,1,0:T(8,128)(2,1)S(1)} %get-tuple-element.95), channel_id=1, source_target_pairs={{0,24},{8,16},{16,8},{24,0},{1,25},{9,17},{17,9},{25,1},{2,26},{10... | collective-permute-start | bytes 393224 | tf_op jit(solution)/shard_map/ppermute | solution.py:64
  89.1 1.2 collective-permute-start.20
  108.3 7.0 %collective-permute-start.27 = (f32[16,128,128]{2,1,0:T(8,128)S(1)}, f32[16,128,128]{2,1,0:T(8,128)S(1)}, u32[]{:S(2)}, u32[]{:S(2)}) collective-permute-start(f32[16,128,128]{2,1,0:T(8,128)S(1)} %get-tuple-element.100), channel_id=1, source_target_pairs={{0,1},{1,0},{2,3},{3,2},{4,5},{5,4},{6,7},{7,6},{8,9},{9,8},{10,11... | collective-permute-start | bytes 3145736 | tf_op jit(solution)/shard_map/ppermute | solution.py:69
  108.5 7.5 %collective-permute-start.34 = (bf16[2,2,128,128]{3,2,1,0:T(8,128)(2,1)S(1)}, bf16[2,2,128,128]{3,2,1,0:T(8,128)(2,1)S(1)}, u32[]{:S(2)}, u32[]{:S(2)}) collective-permute-start(bf16[2,2,128,128]{3,2,1,0:T(8,128)(2,1)S(1)} %get-tuple-element.110), channel_id=1, source_target_pairs={{0,2},{1,3},{2,0},{3,1},{4,6},{5,7},{6,4},{7,5},{8,10},{9,11},{10,... | collective-permute-start | bytes 393224 | tf_op jit(solution)/shard_map/ppermute | solution.py:69
  111.8 10.0 %collective-permute-start.35 = (bf16[2,2,128,128]{3,2,1,0:T(8,128)(2,1)S(1)}, bf16[2,2,128,128]{3,2,1,0:T(8,128)(2,1)S(1)}, u32[]{:S(2)}, u32[]{:S(2)}) collective-permute-start(bf16[2,2,128,128]{3,2,1,0:T(8,128)(2,1)S(1)} %get-tuple-element.111), channel_id=1, source_target_pairs={{0,4},{1,5},{2,6},{3,7},{4,0},{5,1},{6,2},{7,3},{8,12},{9,13},{10,... | collective-permute-start | bytes 393224 | tf_op jit(solution)/shard_map/ppermute | solution.py:69
  111.8 10.0 %collective-permute-start.36 = (bf16[2,2,128,128]{3,2,1,0:T(8,128)(2,1)S(1)}, bf16[2,2,128,128]{3,2,1,0:T(8,128)(2,1)S(1)}, u32[]{:S(2)}, u32[]{:S(2)}) collective-permute-start(bf16[2,2,128,128]{3,2,1,0:T(8,128)(2,1)S(1)} %get-tuple-element.112), channel_id=1, source_target_pairs={{0,6},{1,7},{2,4},{3,5},{4,2},{5,3},{6,0},{7,1},{8,14},{9,15},{10,... | collective-permute-start | bytes 393224 | tf_op jit(solution)/shard_map/ppermute | solution.py:69
  113.3 9.2 %collective-permute-start.31 = (bf16[2,2,128,128]{3,2,1,0:T(8,128)(2,1)S(1)}, bf16[2,2,128,128]{3,2,1,0:T(8,128)(2,1)S(1)}, u32[]{:S(2)}, u32[]{:S(2)}) collective-permute-start(bf16[2,2,128,128]{3,2,1,0:T(8,128)(2,1)S(1)} %get-tuple-element.106), channel_id=1, source_target_pairs={{0,2},{1,3},{2,0},{3,1},{4,6},{5,7},{6,4},{7,5},{8,10},{9,11},{10,... | collective-permute-start | bytes 393224 | tf_op jit(solution)/shard_map/ppermute | solution.py:69
  115.3 12.1 %collective-permute-start.32 = (bf16[2,2,128,128]{3,2,1,0:T(8,128)(2,1)S(1)}, bf16[2,2,128,128]{3,2,1,0:T(8,128)(2,1)S(1)}, u32[]{:S(2)}, u32[]{:S(2)}) collective-permute-start(bf16[2,2,128,128]{3,2,1,0:T(8,128)(2,1)S(1)} %get-tuple-element.107), channel_id=1, source_target_pairs={{0,4},{1,5},{2,6},{3,7},{4,0},{5,1},{6,2},{7,3},{8,12},{9,13},{10,... | collective-permute-start | bytes 393224 | tf_op jit(solution)/shard_map/ppermute | solution.py:69
  116.0 11.4 %collective-permute-start.33 = (bf16[2,2,128,128]{3,2,1,0:T(8,128)(2,1)S(1)}, bf16[2,2,128,128]{3,2,1,0:T(8,128)(2,1)S(1)}, u32[]{:S(2)}, u32[]{:S(2)}) collective-permute-start(bf16[2,2,128,128]{3,2,1,0:T(8,128)(2,1)S(1)} %get-tuple-element.108), channel_id=1, source_target_pairs={{0,6},{1,7},{2,4},{3,5},{4,2},{5,3},{6,0},{7,1},{8,14},{9,15},{10,... | collective-permute-start | bytes 393224 | tf_op jit(solution)/shard_map/ppermute | solution.py:69
  121.8 7.3 %collective-permute-start.28 = (bf16[1,4,128,128]{3,2,1,0:T(8,128)(2,1)S(1)}, bf16[1,4,128,128]{3,2,1,0:T(8,128)(2,1)S(1)}, u32[]{:S(2)}, u32[]{:S(2)}) collective-permute-start(bf16[1,4,128,128]{3,2,1,0:T(8,128)(2,1)S(1)} %get-tuple-element.102), channel_id=1, source_target_pairs={{0,2},{1,3},{2,0},{3,1},{4,6},{5,7},{6,4},{7,5},{8,10},{9,11},{10,... | collective-permute-start | bytes 393224 | tf_op jit(solution)/shard_map/ppermute | solution.py:69
  121.8 9.5 %collective-permute-start.29 = (bf16[1,4,128,128]{3,2,1,0:T(8,128)(2,1)S(1)}, bf16[1,4,128,128]{3,2,1,0:T(8,128)(2,1)S(1)}, u32[]{:S(2)}, u32[]{:S(2)}) collective-permute-start(bf16[1,4,128,128]{3,2,1,0:T(8,128)(2,1)S(1)} %get-tuple-element.103), channel_id=1, source_target_pairs={{0,4},{1,5},{2,6},{3,7},{4,0},{5,1},{6,2},{7,3},{8,12},{9,13},{10,... | collective-permute-start | bytes 393224 | tf_op jit(solution)/shard_map/ppermute | solution.py:69
  122.5 8.8 %collective-permute-start.30 = (bf16[1,4,128,128]{3,2,1,0:T(8,128)(2,1)S(1)}, bf16[1,4,128,128]{3,2,1,0:T(8,128)(2,1)S(1)}, u32[]{:S(2)}, u32[]{:S(2)}) collective-permute-start(bf16[1,4,128,128]{3,2,1,0:T(8,128)(2,1)S(1)} %get-tuple-element.104), channel_id=1, source_target_pairs={{0,6},{1,7},{2,4},{3,5},{4,2},{5,3},{6,0},{7,1},{8,14},{9,15},{10,... | collective-permute-start | bytes 393224 | tf_op jit(solution)/shard_map/ppermute | solution.py:69

commit v2 on v0

--- a/solution.py
+++ b/solution.py
@@ -504,16 +504,22 @@
 
 def assemble_kernel(plan, spans, n, ids, *refs):
     na, rows, hd = plan.na, plan.rows, HEAD_DIM
-    refs = list(refs)
-    outs = refs[na * len(spans) :]
-    for span in spans:
+    pieces, outs, sems = refs[: na * len(spans)], refs[na * len(spans) : -1], refs[-1]
+    copies = []
+    for g, span in enumerate(spans):
         for s in range(na):
-            piece = refs.pop(0)
             cols = pl.ds(pl.multiple_of((ids[1] ^ s) * hd, hd), hd)
             for w in range(n):
                 for x, r in enumerate(span):
                     place = pl.ds(pl.multiple_of((ids[0] ^ r) * rows, rows), rows)
-                    outs[w][place, cols] = piece[w, x]
+                    source = pieces[g * na + s].at[w, x]
+                    copies.append(
+                        pltpu.make_async_copy(source, outs[w].at[place, cols], sems.at[w, r, s])
+                    )
+    for copy in copies:
+        copy.start()
+    for copy in copies:
+        copy.wait()
 
 
 def assemble(plan, ids, spans, groups):
@@ -523,7 +529,8 @@
         functools.partial(assemble_kernel, plan, spans, n),
         out_shape=[sds((plan.nz * plan.rows, plan.na * HEAD_DIM), BF16)] * n,
         in_specs=[SMEM] + [VMEM] * len(pieces),
-        out_specs=[VMEM] * n,
+        out_specs=[HBM] * n,
+        scratch_shapes=[pltpu.SemaphoreType.DMA((n, plan.nz, plan.na))],
         cost_estimate=lasts(1.5),
         compiler_params=within(*pieces, *pieces),
     )(ids, *pieces)

time: 114 us -> 114 us (level)
  no operation moved by 1% of the time
where the time goes in v2:
time: 114 us
  waiting for transfers between devices  39.6 us (35%)
  starting transfers between devices  37.5 us (33%)
  Pallas kernels  35.9 us (31%)
    ppermute x19, waiting for transfers between devices, over_frame(): return lax.ppermute(value, 'frame', [(i, i ^ step) for i in range(count)])  28.3 us
    ppermute x19, starting transfers between devices, over_frame(): return lax.ppermute(value, 'frame', [(i, i ^ step) for i in range(count)])  18.8 us
    pallas_call x2, Pallas kernels, grads(): pl.pallas_call(functools.partial(grads_kernel, plan, span, first, last),...  17.7 us
    ppermute x6, waiting for transfers between devices, over_head(): return lax.ppermute(value, 'head', [(i, i ^ step) for i in range(count)])  11.3 us
    ppermute x6, starting transfers between devices, over_head(): return lax.ppermute(value, 'head', [(i, i ^ step) for i in range(count)])  10.3 us
    all_to_all x1, starting transfers between devices, local(): lax.all_to_all(prep(plan, queries, key_states), ('frame', 'head'), 0, 0,...  8.34 us
    pallas_call x1, Pallas kernels, totals(): pl.pallas_call(functools.partial(totals_kernel, plan), out_shape=[sds((pl...  5.88 us
    pallas_call x1, Pallas kernels, lists(): pl.pallas_call(functools.partial(lists_kernel, plan), out_shape=[sds((own...  3.47 us
  transfers between devices with their start and end apart: 26, of which 15 were waited for; matrix products, arithmetic and copies ran while one was open for 0% of the time, Pallas kernels for 20%

profile of v2, /device:TPU:0, one launch (start us, length us, event | category | flops | bytes accessed | tf_op | source)
XLA Modules:
  0.0 114.0 jit_solution(5503519745165153258)
XLA Ops:
  0.7 2.5 %prep.1 = bf16[16,256,128]{2,1,0:T(8,128)(2,1)} custom-call(bf16[128,2048]{1,0:T(8,128)(2,1)} %q_ref.1, bf16[128,2048]{1,0:T(8,128)(2,1)} %k_ref.1), custom_call_target="tpu_custom_call" | custom-call | bytes 5250000 | tf_op jit(solution)/shard_map/prep/pallas_call | solution.py:98
  3.2 8.3 %all-to-all-start = ((bf16[16,256,128]{2,1,0:T(8,128)(2,1)}), bf16[16,256,128]{2,1,0:T(8,128)(2,1)S(1)}, u32[]{:S(2)}, u32[]{:S(2)}) async-start(bf16[16,256,128]{2,1,0:T(8,128)(2,1)} %prep.1), calls=%async_computation | async-start | bytes 2097152 | tf_op jit(solution)/shard_map/all_to_all | solution.py:563
  11.5 0.1 pad_add_fusion.ids
  11.6 0.0 copy-start.3
  11.6 0.0 copy-start.4
  11.6 2.1 %prep_rest.1 = (bf16[4,136,128]{2,1,0:T(8,128)(2,1)S(1)}, bf16[4,136,128]{2,1,0:T(8,128)(2,1)S(1)}, bf16[4,136,128]{2,1,0:T(8,128)(2,1)S(1)}, bf16[4,136,128]{2,...) custom-call(s32[3]{0:T(128)S(1)} %pad_add_fusion.ids, ...), custom_call_target="tpu_custom_call" | custom-call | bytes 7000000 | tf_op jit(solution)/shard_map/prep_rest/pallas_call | solution.py:158
  13.7 2.0 %collective-permute-start.1 = (bf16[4,136,128]{2,1,0:T(8,128)(2,1)S(1)}, bf16[4,136,128]{2,1,0:T(8,128)(2,1)S(1)}, u32[]{:S(2)}, u32[]{:S(2)}) collective-permute-start(bf16[4,136,128]{2,1,0:T(8,128)(2,1)S(1)} %get-tuple-element.51), channel_id=1, source_target_pairs={{0,2},{1,3},{2,0},{3,1},{4,6},{5,7},{6,4},{7,5},{8,10},{9,11},{10,... | collective-permute-start | bytes 417800 | tf_op jit(solution)/shard_map/ppermute | solution.py:69
  15.7 1.5 %collective-permute-start.2 = (bf16[4,136,128]{2,1,0:T(8,128)(2,1)S(1)}, bf16[4,136,128]{2,1,0:T(8,128)(2,1)S(1)}, u32[]{:S(2)}, u32[]{:S(2)}) collective-permute-start(bf16[4,136,128]{2,1,0:T(8,128)(2,1)S(1)} %get-tuple-element.52), channel_id=1, source_target_pairs={{0,4},{1,5},{2,6},{3,7},{4,0},{5,1},{6,2},{7,3},{8,12},{9,13},{10,... | collective-permute-start | bytes 417800 | tf_op jit(solution)/shard_map/ppermute | solution.py:69
  17.2 0.1 collective-permute-start.3
  17.3 9.3 %collective-permute-done.1.refs_1_ = bf16[4,136,128]{2,1,0:T(8,128)(2,1)S(1)} collective-permute-done((bf16[4,136,128]{2,1,0:T(8,128)(2,1)S(1)}, bf16[4,136,128]{2,1,0:T(8,128)(2,1)S(1)}, u32[]{:S(2)}, u32[]{:S(2)}) %collective-permute-start.1) | collective-permute-done | bytes 139296 | tf_op jit(solution)/shard_map/ppermute | solution.py:69
  26.5 1.5 %collective-permute-done.2.refs_2_ = bf16[4,136,128]{2,1,0:T(8,128)(2,1)S(1)} collective-permute-done((bf16[4,136,128]{2,1,0:T(8,128)(2,1)S(1)}, bf16[4,136,128]{2,1,0:T(8,128)(2,1)S(1)}, u32[]{:S(2)}, u32[]{:S(2)}) %collective-permute-start.2) | collective-permute-done | bytes 139296 | tf_op jit(solution)/shard_map/ppermute | solution.py:69
  28.0 2.4 %collective-permute-done.3.refs_3_ = bf16[4,136,128]{2,1,0:T(8,128)(2,1)S(1)} collective-permute-done((bf16[4,136,128]{2,1,0:T(8,128)(2,1)S(1)}, bf16[4,136,128]{2,1,0:T(8,128)(2,1)S(1)}, u32[]{:S(2)}, u32[]{:S(2)}) %collective-permute-start.3) | collective-permute-done | bytes 139296 | tf_op jit(solution)/shard_map/ppermute | solution.py:69
  30.5 0.1 collective-permute-start.4
  30.6 5.2 %collective-permute-start.5 = (bf16[4,136,128]{2,1,0:T(8,128)(2,1)S(1)}, bf16[4,136,128]{2,1,0:T(8,128)(2,1)S(1)}, u32[]{:S(2)}, u32[]{:S(2)}) collective-permute-start(bf16[4,136,128]{2,1,0:T(8,128)(2,1)S(1)} %get-tuple-element.56), channel_id=1, source_target_pairs={{0,16},{8,24},{16,0},{24,8},{1,17},{9,25},{17,1},{25,9},{2,18},{10... | collective-permute-start | bytes 417800 | tf_op jit(solution)/shard_map/ppermute | solution.py:64
  35.8 0.0 collective-permute-start.6
  35.8 0.6 collective-permute-done.4.refs_1_
  36.4 10.7 %collective-permute-done.5.refs_2_ = bf16[4,136,128]{2,1,0:T(8,128)(2,1)S(1)} collective-permute-done((bf16[4,136,128]{2,1,0:T(8,128)(2,1)S(1)}, bf16[4,136,128]{2,1,0:T(8,128)(2,1)S(1)}, u32[]{:S(2)}, u32[]{:S(2)}) %collective-permute-start.5) | collective-permute-done | bytes 139296 | tf_op jit(solution)/shard_map/ppermute | solution.py:64
  47.1 0.0 collective-permute-done.6.refs_3_
  47.2 0.1 collective-permute-start.7
  47.2 0.0 all-to-all-done.x_ref
  47.3 0.6 part.1
  47.9 0.6 collective-permute-start
  48.4 1.5 %collective-permute-start.9 = (bf16[4,128,128]{2,1,0:T(8,128)(2,1)S(1)}, bf16[4,128,128]{2,1,0:T(8,128)(2,1)S(1)}, u32[]{:S(2)}, u32[]{:S(2)}) collective-permute-start(bf16[4,128,128]{2,1,0:T(8,128)(2,1)S(1)} %get-tuple-element.63), channel_id=1, source_target_pairs={{0,2},{1,3},{2,0},{3,1},{4,6},{5,7},{6,4},{7,5},{8,10},{9,11},{10,... | collective-permute-start | bytes 393224 | tf_op jit(solution)/shard_map/ppermute | solution.py:69
  49.9 1.5 %collective-permute-start.10 = (bf16[4,128,128]{2,1,0:T(8,128)(2,1)S(1)}, bf16[4,128,128]{2,1,0:T(8,128)(2,1)S(1)}, u32[]{:S(2)}, u32[]{:S(2)}) collective-permute-start(bf16[4,128,128]{2,1,0:T(8,128)(2,1)S(1)} %get-tuple-element.64), channel_id=1, source_target_pairs={{0,4},{1,5},{2,6},{3,7},{4,0},{5,1},{6,2},{7,3},{8,12},{9,13},{10,... | collective-permute-start | bytes 393224 | tf_op jit(solution)/shard_map/ppermute | solution.py:69
  51.4 0.6 collective-permute-start.11
  51.9 2.4 %collective-permute-done.9.refs_1_ = bf16[4,128,128]{2,1,0:T(8,128)(2,1)S(1)} collective-permute-done((bf16[4,128,128]{2,1,0:T(8,128)(2,1)S(1)}, bf16[4,128,128]{2,1,0:T(8,128)(2,1)S(1)}, u32[]{:S(2)}, u32[]{:S(2)}) %collective-permute-start.9) | collective-permute-done | bytes 131104 | tf_op jit(solution)/shard_map/ppermute | solution.py:69
  54.3 3.6 %collective-permute-done.10.refs_2_ = bf16[4,128,128]{2,1,0:T(8,128)(2,1)S(1)} collective-permute-done((bf16[4,128,128]{2,1,0:T(8,128)(2,1)S(1)}, bf16[4,128,128]{2,1,0:T(8,128)(2,1)S(1)}, u32[]{:S(2)}, u32[]{:S(2)}) %collective-permute-start.10) | collective-permute-done | bytes 131104 | tf_op jit(solution)/shard_map/ppermute | solution.py:69
  57.9 0.0 collective-permute-done.11.refs_3_
  57.9 2.6 %collective-permute-start.14 = (bf16[4,128,128]{2,1,0:T(8,128)(2,1)S(1)}, bf16[4,128,128]{2,1,0:T(8,128)(2,1)S(1)}, u32[]{:S(2)}, u32[]{:S(2)}) collective-permute-start(bf16[4,128,128]{2,1,0:T(8,128)(2,1)S(1)} %get-tuple-element.69), channel_id=1, source_target_pairs={{0,8},{8,0},{16,24},{24,16},{1,9},{9,1},{17,25},{25,17},{2,10},{10... | collective-permute-start | bytes 393224 | tf_op jit(solution)/shard_map/ppermute | solution.py:64
  60.6 0.1 collective-permute-start.12
  60.7 2.3 %collective-permute-start.13 = (bf16[4,128,128]{2,1,0:T(8,128)(2,1)S(1)}, bf16[4,128,128]{2,1,0:T(8,128)(2,1)S(1)}, u32[]{:S(2)}, u32[]{:S(2)}) collective-permute-start(bf16[4,128,128]{2,1,0:T(8,128)(2,1)S(1)} %get-tuple-element.67), channel_id=1, source_target_pairs={{0,24},{8,16},{16,8},{24,0},{1,25},{9,17},{17,9},{25,1},{2,26},{10... | collective-permute-start | bytes 393224 | tf_op jit(solution)/shard_map/ppermute | solution.py:64
  63.0 3.5 %lists.1 = (s32[16,42]{1,0:T(8,128)S(1)}, s32[16]{0:T(128)S(1)}) custom-call(s32[3]{0:T(128)S(1)} %pad_add_fusion.ids, s32[8]{0:T(128)S(1)} %copy-done.4, s32[4,4,8]{2,1,0:T(4,128)S(1)} %bitcast.4), custom_call_target="tpu_custom_call" | custom-call | bytes 10500000 | tf_op jit(solution)/shard_map/lists/pallas_call | solution.py:242
  66.5 5.9 %totals.1 = (f32[32,128]{1,0:T(8,128)S(1)}, bf16[32,128,128]{2,1,0:T(8,128)(2,1)S(1)}) custom-call(s32[16,42]{1,0:T(8,128)S(1)} %get-tuple-element.45.by_key, s32[16]{0:T(128)S(1)} %get-tuple-element.46.n_key, bf16[16,128,128]{2,1,0:T(8,128)(2,1)S(1)} %get-tuple-element.47.k_ref, bf16[16,128,128]{2,1,0:T(8,128)(2,1)S(1)} %get-tuple-element.48.refs_0_, ...), custom_call_target="tpu_custom_call" | custom-call | bytes 21000000 | tf_op jit(solution)/shard_map/totals/pallas_call | solution.py:330
  72.4 0.1 collective-permute-start.8
  72.5 0.0 collective-permute-done.7.refs_1_
  72.5 1.2 %collective-permute-done.8.refs_3_ = f32[32,128]{1,0:T(8,128)S(1)} collective-permute-done((f32[32,128]{1,0:T(8,128)S(1)}, f32[32,128]{1,0:T(8,128)S(1)}, u32[]{:S(2)}, u32[]{:S(2)}) %collective-permute-start.8) | collective-permute-done | bytes 16416 | tf_op jit(solution)/shard_map/ppermute | solution.py:69
  73.6 0.1 query_rows.1
  73.7 0.0 collective-permute-done.14.refs_1_
  73.7 8.6 %shard_map.97 = (bf16[2,2,128,128]{3,2,1,0:T(8,128)(2,1)S(1)}, bf16[2,2,128,128]{3,2,1,0:T(8,128)(2,1)S(1)}, bf16[2,2,128,128]{3,2,1,0:T(8,128)(2,1)S(1)}, bf16[...) custom-call(s32[16,42]{1,0:T(8,128)S(1)} %get-tuple-element.45.by_key, s32[16]{0:T(128)S(1)} %get-tuple-element.46.n_key, ...), custom_call_target="tpu_custom_call" | custom-call | bytes 24500000 | tf_op jit(solution)/shard_map/pallas_call | solution.py:473
  82.4 0.0 collective-permute-done.12.refs_0_
  82.4 9.1 %shard_map.98 = (bf16[2,2,128,128]{3,2,1,0:T(8,128)(2,1)S(1)}, bf16[2,2,128,128]{3,2,1,0:T(8,128)(2,1)S(1)}, bf16[2,2,128,128]{3,2,1,0:T(8,128)(2,1)S(1)}, bf16[...) custom-call(s32[16,42]{1,0:T(8,128)S(1)} %get-tuple-element.45.by_key, ...), custom_call_target="tpu_custom_call" | custom-call | bytes 24500000 | tf_op jit(solution)/shard_map/pallas_call | solution.py:473
  91.5 0.2 collective-permute-start.15
  91.7 1.2 %collective-permute-start.22 = (bf16[2,2,128,128]{3,2,1,0:T(8,128)(2,1)S(1)}, bf16[2,2,128,128]{3,2,1,0:T(8,128)(2,1)S(1)}, u32[]{:S(2)}, u32[]{:S(2)}) collective-permute-start(bf16[2,2,128,128]{3,2,1,0:T(8,128)(2,1)S(1)} %get-tuple-element.82), channel_id=1, source_target_pairs={{0,2},{1,3},{2,0},{3,1},{4,6},{5,7},{6,4},{7,5},{8,10},{9,11},{10,... | collective-permute-start | bytes 393224 | tf_op jit(solution)/shard_map/ppermute | solution.py:69
  92.9 0.8 collective-permute-start.23
  93.8 1.5 %collective-permute-start.24 = (bf16[2,2,128,128]{3,2,1,0:T(8,128)(2,1)S(1)}, bf16[2,2,128,128]{3,2,1,0:T(8,128)(2,1)S(1)}, u32[]{:S(2)}, u32[]{:S(2)}) collective-permute-start(bf16[2,2,128,128]{3,2,1,0:T(8,128)(2,1)S(1)} %get-tuple-element.84), channel_id=1, source_target_pairs={{0,6},{1,7},{2,4},{3,5},{4,2},{5,3},{6,0},{7,1},{8,14},{9,15},{10,... | collective-permute-start | bytes 393224 | tf_op jit(solution)/shard_map/ppermute | solution.py:69
  95.2 1.2 %collective-permute-start.19 = (bf16[2,2,128,128]{3,2,1,0:T(8,128)(2,1)S(1)}, bf16[2,2,128,128]{3,2,1,0:T(8,128)(2,1)S(1)}, u32[]{:S(2)}, u32[]{:S(2)}) collective-permute-start(bf16[2,2,128,128]{3,2,1,0:T(8,128)(2,1)S(1)} %get-tuple-element.78), channel_id=1, source_target_pairs={{0,2},{1,3},{2,0},{3,1},{4,6},{5,7},{6,4},{7,5},{8,10},{9,11},{10,... | collective-permute-start | bytes 393224 | tf_op jit(solution)/shard_map/ppermute | solution.py:69
  96.4 0.0 collective-permute-done.15.refs_1_
  96.4 0.8 collective-permute-start.20
  97.3 0.2 pack.1
  97.4 0.7 collective-permute-done.22.refs_5_
  98.1 1.3 %collective-permute-start.21 = (bf16[2,2,128,128]{3,2,1,0:T(8,128)(2,1)S(1)}, bf16[2,2,128,128]{3,2,1,0:T(8,128)(2,1)S(1)}, u32[]{:S(2)}, u32[]{:S(2)}) collective-permute-start(bf16[2,2,128,128]{3,2,1,0:T(8,128)(2,1)S(1)} %get-tuple-element.80), channel_id=1, source_target_pairs={{0,6},{1,7},{2,4},{3,5},{4,2},{5,3},{6,0},{7,1},{8,14},{9,15},{10,... | collective-permute-start | bytes 393224 | tf_op jit(solution)/shard_map/ppermute | solution.py:69
  99.4 1.9 %collective-permute-done.23.refs_6_ = bf16[2,2,128,128]{3,2,1,0:T(8,128)(2,1)S(1)} collective-permute-done((bf16[2,2,128,128]{3,2,1,0:T(8,128)(2,1)S(1)}, bf16[2,2,128,128]{3,2,1,0:T(8,128)(2,1)S(1)}, u32[]{:S(2)}, u32[]{:S(2)}) %collective-permute-start.23) | collective-permute-done | bytes 131104 | tf_op jit(solution)/shard_map/ppermute | solution.py:69
  101.3 1.1 collective-permute-start.16
  102.4 0.0 collective-permute-done.24.refs_7_
  102.4 1.8 %collective-permute-start.17 = (bf16[1,4,128,128]{3,2,1,0:T(8,128)(2,1)S(1)}, bf16[1,4,128,128]{3,2,1,0:T(8,128)(2,1)S(1)}, u32[]{:S(2)}, u32[]{:S(2)}) collective-permute-start(bf16[1,4,128,128]{3,2,1,0:T(8,128)(2,1)S(1)} %get-tuple-element.75), channel_id=1, source_target_pairs={{0,4},{1,5},{2,6},{3,7},{4,0},{5,1},{6,2},{7,3},{8,12},{9,13},{10,... | collective-permute-start | bytes 393224 | tf_op jit(solution)/shard_map/ppermute | solution.py:69
  104.2 0.0 collective-permute-done.19.refs_1_
  104.2 1.2 %collective-permute-start.18 = (bf16[1,4,128,128]{3,2,1,0:T(8,128)(2,1)S(1)}, bf16[1,4,128,128]{3,2,1,0:T(8,128)(2,1)S(1)}, u32[]{:S(2)}, u32[]{:S(2)}) collective-permute-start(bf16[1,4,128,128]{3,2,1,0:T(8,128)(2,1)S(1)} %get-tuple-element.76), channel_id=1, source_target_pairs={{0,6},{1,7},{2,4},{3,5},{4,2},{5,3},{6,0},{7,1},{8,14},{9,15},{10,... | collective-permute-start | bytes 393224 | tf_op jit(solution)/shard_map/ppermute | solution.py:69
  105.3 1.5 %collective-permute-done.20.refs_2_ = bf16[2,2,128,128]{3,2,1,0:T(8,128)(2,1)S(1)} collective-permute-done((bf16[2,2,128,128]{3,2,1,0:T(8,128)(2,1)S(1)}, bf16[2,2,128,128]{3,2,1,0:T(8,128)(2,1)S(1)}, u32[]{:S(2)}, u32[]{:S(2)}) %collective-permute-start.20) | collective-permute-done | bytes 131104 | tf_op jit(solution)/shard_map/ppermute | solution.py:69
  106.9 0.7 collective-permute-done.21.refs_3_
  107.5 1.8 %shard_map.100 = (bf16[512,512]{1,0:T(8,128)(2,1)}, bf16[512,512]{1,0:T(8,128)(2,1)}) custom-call(s32[3]{0:T(128)S(1)} %pad_add_fusion.ids, bf16[2,2,128,128]{3,2,1,0:T(8,128)(2,1)S(1)} %get-tuple-element.77.refs_0_, bf16[2,2,128,128]{3,2,1,0:T(8,128)(2,1)S(1)} %collective-permute-done.19.refs_1_, ...), custom_call_target="tpu_custom_call" | custom-call | bytes 5250000 | tf_op jit(solution)/shard_map/pallas_call | solution.py:528
  109.3 0.1 collective-permute-done.16.refs_1_
  109.4 0.7 collective-permute-done.17.refs_2_
  110.1 2.4 %collective-permute-done.18.refs_3_ = bf16[1,4,128,128]{3,2,1,0:T(8,128)(2,1)S(1)} collective-permute-done((bf16[1,4,128,128]{3,2,1,0:T(8,128)(2,1)S(1)}, bf16[1,4,128,128]{3,2,1,0:T(8,128)(2,1)S(1)}, u32[]{:S(2)}, u32[]{:S(2)}) %collective-permute-start.18) | collective-permute-done | bytes 131104 | tf_op jit(solution)/shard_map/ppermute | solution.py:69
  112.5 1.5 %shard_map.99 = bf16[512,512]{1,0:T(8,128)(2,1)} custom-call(s32[3]{0:T(128)S(1)} %pad_add_fusion.ids, bf16[1,4,128,128]{3,2,1,0:T(8,128)(2,1)S(1)} %get-tuple-element.73.refs_0_, bf16[1,4,128,128]{3,2,1,0:T(8,128)(2,1)S(1)} %collective-permute-done.16.refs_1_, bf16[1,4,128,128]{3,2,1,0:T(8,128)(2,1)S(1)} %collective-permute-done.17.refs_2_, ...), custom_call_target="tpu_custom_call" | custom-call | bytes 5250000 | tf_op jit(solution)/shard_map/pallas_call | solution.py:528
  (13 shorter events, 0.1 us)
Async XLA Ops:
  0.6 11.0 %copy-start = (bf16[128,2048]{1,0:T(8,128)(2,1)S(1)}, bf16[128,2048]{1,0:T(8,128)(2,1)}, u32[]{:S(2)}) copy-start(bf16[128,2048]{1,0:T(8,128)(2,1)} %g_ref.1) | copy-start | bytes 1572868
  0.6 11.0 %copy-start.1 = (bf16[128,2048]{1,0:T(8,128)(2,1)S(1)}, bf16[128,2048]{1,0:T(8,128)(2,1)}, u32[]{:S(2)}) copy-start(bf16[128,2048]{1,0:T(8,128)(2,1)} %o_ref.1) | copy-start | bytes 1572868
  0.7 11.0 %copy-start.2 = (bf16[128,2048]{1,0:T(8,128)(2,1)S(1)}, bf16[128,2048]{1,0:T(8,128)(2,1)}, u32[]{:S(2)}) copy-start(bf16[128,2048]{1,0:T(8,128)(2,1)} %v_ref.1) | copy-start | bytes 1572868
  3.2 44.1 %all-to-all-start = ((bf16[16,256,128]{2,1,0:T(8,128)(2,1)}), bf16[16,256,128]{2,1,0:T(8,128)(2,1)S(1)}, u32[]{:S(2)}, u32[]{:S(2)}) async-start(bf16[16,256,128]{2,1,0:T(8,128)(2,1)} %prep.1), calls=%async_computation | async-start | bytes 2097152 | tf_op jit(solution)/shard_map/all_to_all | solution.py:563
  11.6 51.4 %copy-start.3 = (s32[8,4,4]{0,2,1:T(4,128)S(1)}, s32[8,4,4]{0,2,1:T(4,128)}, u32[]{:S(2)}) copy-start(s32[8,4,4]{0,2,1:T(4,128)} %param.13) | copy-start | bytes 1540
  11.6 51.4 %copy-start.4 = (s32[8]{0:T(128)S(1)}, s32[8]{0:T(128)}, u32[]{:S(2)}) copy-start(s32[8]{0:T(128)} %order.1) | copy-start | bytes 100
  13.7 12.8 %collective-permute-start.1 = (bf16[4,136,128]{2,1,0:T(8,128)(2,1)S(1)}, bf16[4,136,128]{2,1,0:T(8,128)(2,1)S(1)}, u32[]{:S(2)}, u32[]{:S(2)}) collective-permute-start(bf16[4,136,128]{2,1,0:T(8,128)(2,1)S(1)} %get-tuple-element.51), channel_id=1, source_target_pairs={{0,2},{1,3},{2,0},{3,1},{4,6},{5,7},{6,4},{7,5},{8,10},{9,11},{10,... | collective-permute-start | bytes 417800 | tf_op jit(solution)/shard_map/ppermute | solution.py:69
  15.7 12.3 %collective-permute-start.2 = (bf16[4,136,128]{2,1,0:T(8,128)(2,1)S(1)}, bf16[4,136,128]{2,1,0:T(8,128)(2,1)S(1)}, u32[]{:S(2)}, u32[]{:S(2)}) collective-permute-start(bf16[4,136,128]{2,1,0:T(8,128)(2,1)S(1)} %get-tuple-element.52), channel_id=1, source_target_pairs={{0,4},{1,5},{2,6},{3,7},{4,0},{5,1},{6,2},{7,3},{8,12},{9,13},{10,... | collective-permute-start | bytes 417800 | tf_op jit(solution)/shard_map/ppermute | solution.py:69
  17.2 13.3 %collective-permute-start.3 = (bf16[4,136,128]{2,1,0:T(8,128)(2,1)S(1)}, bf16[4,136,128]{2,1,0:T(8,128)(2,1)S(1)}, u32[]{:S(2)}, u32[]{:S(2)}) collective-permute-start(bf16[4,136,128]{2,1,0:T(8,128)(2,1)S(1)} %get-tuple-element.53), channel_id=1, source_target_pairs={{0,6},{1,7},{2,4},{3,5},{4,2},{5,3},{6,0},{7,1},{8,14},{9,15},{10,... | collective-permute-start | bytes 417800 | tf_op jit(solution)/shard_map/ppermute | solution.py:69
  30.5 5.9 %collective-permute-start.4 = (bf16[4,136,128]{2,1,0:T(8,128)(2,1)S(1)}, bf16[4,136,128]{2,1,0:T(8,128)(2,1)S(1)}, u32[]{:S(2)}, u32[]{:S(2)}) collective-permute-start(bf16[4,136,128]{2,1,0:T(8,128)(2,1)S(1)} %get-tuple-element.55), channel_id=1, source_target_pairs={{0,8},{8,0},{16,24},{24,16},{1,9},{9,1},{17,25},{25,17},{2,10},{10... | collective-permute-start | bytes 417800 | tf_op jit(solution)/shard_map/ppermute | solution.py:64
  30.6 16.5 %collective-permute-start.5 = (bf16[4,136,128]{2,1,0:T(8,128)(2,1)S(1)}, bf16[4,136,128]{2,1,0:T(8,128)(2,1)S(1)}, u32[]{:S(2)}, u32[]{:S(2)}) collective-permute-start(bf16[4,136,128]{2,1,0:T(8,128)(2,1)S(1)} %get-tuple-element.56), channel_id=1, source_target_pairs={{0,16},{8,24},{16,0},{24,8},{1,17},{9,25},{17,1},{25,9},{2,18},{10... | collective-permute-start | bytes 417800 | tf_op jit(solution)/shard_map/ppermute | solution.py:64
  35.8 11.3 %collective-permute-start.6 = (bf16[4,136,128]{2,1,0:T(8,128)(2,1)S(1)}, bf16[4,136,128]{2,1,0:T(8,128)(2,1)S(1)}, u32[]{:S(2)}, u32[]{:S(2)}) collective-permute-start(bf16[4,136,128]{2,1,0:T(8,128)(2,1)S(1)} %get-tuple-element.57), channel_id=1, source_target_pairs={{0,24},{8,16},{16,8},{24,0},{1,25},{9,17},{17,9},{25,1},{2,26},{10... | collective-permute-start | bytes 417800 | tf_op jit(solution)/shard_map/ppermute | solution.py:64
  47.2 25.3 %collective-permute-start.7 = (bf16[16,136,128]{2,1,0:T(8,128)(2,1)S(1)}, bf16[16,136,128]{2,1,0:T(8,128)(2,1)S(1)}, u32[]{:S(2)}, u32[]{:S(2)}) collective-permute-start(bf16[16,136,128]{2,1,0:T(8,128)(2,1)S(1)} %shard_map.95.refs_0_), channel_id=1, source_target_pairs={{0,1},{1,0},{2,3},{3,2},{4,5},{5,4},{6,7},{7,6},{8,9},{9,8},{10,11... | collective-permute-start | bytes 1671176 | tf_op jit(solution)/shard_map/ppermute | solution.py:69
  47.9 18.6 %collective-permute-start = (bf16[16,128,128]{2,1,0:T(8,128)(2,1)S(1)}, bf16[16,128,128]{2,1,0:T(8,128)(2,1)S(1)}, u32[]{:S(2)}, u32[]{:S(2)}) collective-permute-start(bf16[16,128,128]{2,1,0:T(8,128)(2,1)S(1)} %get-tuple-element.48.refs_0_), channel_id=1, source_target_pairs={{0,1},{1,0},{2,3},{3,2},{4,5},{5,4},{6,7},{7,6},{8,9},{9,8},{10,11... | collective-permute-start | bytes 1572872 | tf_op jit(solution)/shard_map/ppermute | solution.py:69
  48.4 5.9 %collective-permute-start.9 = (bf16[4,128,128]{2,1,0:T(8,128)(2,1)S(1)}, bf16[4,128,128]{2,1,0:T(8,128)(2,1)S(1)}, u32[]{:S(2)}, u32[]{:S(2)}) collective-permute-start(bf16[4,128,128]{2,1,0:T(8,128)(2,1)S(1)} %get-tuple-element.63), channel_id=1, source_target_pairs={{0,2},{1,3},{2,0},{3,1},{4,6},{5,7},{6,4},{7,5},{8,10},{9,11},{10,... | collective-permute-start | bytes 393224 | tf_op jit(solution)/shard_map/ppermute | solution.py:69
  49.9 8.0 %collective-permute-start.10 = (bf16[4,128,128]{2,1,0:T(8,128)(2,1)S(1)}, bf16[4,128,128]{2,1,0:T(8,128)(2,1)S(1)}, u32[]{:S(2)}, u32[]{:S(2)}) collective-permute-start(bf16[4,128,128]{2,1,0:T(8,128)(2,1)S(1)} %get-tuple-element.64), channel_id=1, source_target_pairs={{0,4},{1,5},{2,6},{3,7},{4,0},{5,1},{6,2},{7,3},{8,12},{9,13},{10,... | collective-permute-start | bytes 393224 | tf_op jit(solution)/shard_map/ppermute | solution.py:69
  51.4 6.5 %collective-permute-start.11 = (bf16[4,128,128]{2,1,0:T(8,128)(2,1)S(1)}, bf16[4,128,128]{2,1,0:T(8,128)(2,1)S(1)}, u32[]{:S(2)}, u32[]{:S(2)}) collective-permute-start(bf16[4,128,128]{2,1,0:T(8,128)(2,1)S(1)} %get-tuple-element.65), channel_id=1, source_target_pairs={{0,6},{1,7},{2,4},{3,5},{4,2},{5,3},{6,0},{7,1},{8,14},{9,15},{10,... | collective-permute-start | bytes 393224 | tf_op jit(solution)/shard_map/ppermute | solution.py:69
  57.9 15.8 %collective-permute-start.14 = (bf16[4,128,128]{2,1,0:T(8,128)(2,1)S(1)}, bf16[4,128,128]{2,1,0:T(8,128)(2,1)S(1)}, u32[]{:S(2)}, u32[]{:S(2)}) collective-permute-start(bf16[4,128,128]{2,1,0:T(8,128)(2,1)S(1)} %get-tuple-element.69), channel_id=1, source_target_pairs={{0,8},{8,0},{16,24},{24,16},{1,9},{9,1},{17,25},{25,17},{2,10},{10... | collective-permute-start | bytes 393224 | tf_op jit(solution)/shard_map/ppermute | solution.py:64
  60.6 21.8 %collective-permute-start.12 = (bf16[4,128,128]{2,1,0:T(8,128)(2,1)S(1)}, bf16[4,128,128]{2,1,0:T(8,128)(2,1)S(1)}, u32[]{:S(2)}, u32[]{:S(2)}) collective-permute-start(bf16[4,128,128]{2,1,0:T(8,128)(2,1)S(1)} %get-tuple-element.66), channel_id=1, source_target_pairs={{0,16},{8,24},{16,0},{24,8},{1,17},{9,25},{17,1},{25,9},{2,18},{10... | collective-permute-start | bytes 393224 | tf_op jit(solution)/shard_map/ppermute | solution.py:64
  60.7 21.7 %collective-permute-start.13 = (bf16[4,128,128]{2,1,0:T(8,128)(2,1)S(1)}, bf16[4,128,128]{2,1,0:T(8,128)(2,1)S(1)}, u32[]{:S(2)}, u32[]{:S(2)}) collective-permute-start(bf16[4,128,128]{2,1,0:T(8,128)(2,1)S(1)} %get-tuple-element.67), channel_id=1, source_target_pairs={{0,24},{8,16},{16,8},{24,0},{1,25},{9,17},{17,9},{25,1},{2,26},{10... | collective-permute-start | bytes 393224 | tf_op jit(solution)/shard_map/ppermute | solution.py:64
  72.4 1.2 %collective-permute-start.8 = (f32[32,128]{1,0:T(8,128)S(1)}, f32[32,128]{1,0:T(8,128)S(1)}, u32[]{:S(2)}, u32[]{:S(2)}) collective-permute-start(f32[32,128]{1,0:T(8,128)S(1)} %get-tuple-element.58.refs_2_), channel_id=1, source_target_pairs={{0,1},{1,0},{2,3},{3,2},{4,5},{5,4},{6,7},{7,6},{8,9},{9,8},{10,11... | collective-permute-start | bytes 49160 | tf_op jit(solution)/shard_map/ppermute | solution.py:69
  91.5 4.9 %collective-permute-start.15 = (f32[16,128,128]{2,1,0:T(8,128)S(1)}, f32[16,128,128]{2,1,0:T(8,128)S(1)}, u32[]{:S(2)}, u32[]{:S(2)}) collective-permute-start(f32[16,128,128]{2,1,0:T(8,128)S(1)} %get-tuple-element.72), channel_id=1, source_target_pairs={{0,1},{1,0},{2,3},{3,2},{4,5},{5,4},{6,7},{7,6},{8,9},{9,8},{10,11... | collective-permute-start | bytes 3145736 | tf_op jit(solution)/shard_map/ppermute | solution.py:69
  91.7 6.4 %collective-permute-start.22 = (bf16[2,2,128,128]{3,2,1,0:T(8,128)(2,1)S(1)}, bf16[2,2,128,128]{3,2,1,0:T(8,128)(2,1)S(1)}, u32[]{:S(2)}, u32[]{:S(2)}) collective-permute-start(bf16[2,2,128,128]{3,2,1,0:T(8,128)(2,1)S(1)} %get-tuple-element.82), channel_id=1, source_target_pairs={{0,2},{1,3},{2,0},{3,1},{4,6},{5,7},{6,4},{7,5},{8,10},{9,11},{10,... | collective-permute-start | bytes 393224 | tf_op jit(solution)/shard_map/ppermute | solution.py:69
  92.9 8.4 %collective-permute-start.23 = (bf16[2,2,128,128]{3,2,1,0:T(8,128)(2,1)S(1)}, bf16[2,2,128,128]{3,2,1,0:T(8,128)(2,1)S(1)}, u32[]{:S(2)}, u32[]{:S(2)}) collective-permute-start(bf16[2,2,128,128]{3,2,1,0:T(8,128)(2,1)S(1)} %get-tuple-element.83), channel_id=1, source_target_pairs={{0,4},{1,5},{2,6},{3,7},{4,0},{5,1},{6,2},{7,3},{8,12},{9,13},{10,... | collective-permute-start | bytes 393224 | tf_op jit(solution)/shard_map/ppermute | solution.py:69
  93.8 8.7 %collective-permute-start.24 = (bf16[2,2,128,128]{3,2,1,0:T(8,128)(2,1)S(1)}, bf16[2,2,128,128]{3,2,1,0:T(8,128)(2,1)S(1)}, u32[]{:S(2)}, u32[]{:S(2)}) collective-permute-start(bf16[2,2,128,128]{3,2,1,0:T(8,128)(2,1)S(1)} %get-tuple-element.84), channel_id=1, source_target_pairs={{0,6},{1,7},{2,4},{3,5},{4,2},{5,3},{6,0},{7,1},{8,14},{9,15},{10,... | collective-permute-start | bytes 393224 | tf_op jit(solution)/shard_map/ppermute | solution.py:69
  95.2 9.0 %collective-permute-start.19 = (bf16[2,2,128,128]{3,2,1,0:T(8,128)(2,1)S(1)}, bf16[2,2,128,128]{3,2,1,0:T(8,128)(2,1)S(1)}, u32[]{:S(2)}, u32[]{:S(2)}) collective-permute-start(bf16[2,2,128,128]{3,2,1,0:T(8,128)(2,1)S(1)} %get-tuple-element.78), channel_id=1, source_target_pairs={{0,2},{1,3},{2,0},{3,1},{4,6},{5,7},{6,4},{7,5},{8,10},{9,11},{10,... | collective-permute-start | bytes 393224 | tf_op jit(solution)/shard_map/ppermute | solution.py:69
  96.4 10.5 %collective-permute-start.20 = (bf16[2,2,128,128]{3,2,1,0:T(8,128)(2,1)S(1)}, bf16[2,2,128,128]{3,2,1,0:T(8,128)(2,1)S(1)}, u32[]{:S(2)}, u32[]{:S(2)}) collective-permute-start(bf16[2,2,128,128]{3,2,1,0:T(8,128)(2,1)S(1)} %get-tuple-element.79), channel_id=1, source_target_pairs={{0,4},{1,5},{2,6},{3,7},{4,0},{5,1},{6,2},{7,3},{8,12},{9,13},{10,... | collective-permute-start | bytes 393224 | tf_op jit(solution)/shard_map/ppermute | solution.py:69
  98.1 9.4 %collective-permute-start.21 = (bf16[2,2,128,128]{3,2,1,0:T(8,128)(2,1)S(1)}, bf16[2,2,128,128]{3,2,1,0:T(8,128)(2,1)S(1)}, u32[]{:S(2)}, u32[]{:S(2)}) collective-permute-start(bf16[2,2,128,128]{3,2,1,0:T(8,128)(2,1)S(1)} %get-tuple-element.80), channel_id=1, source_target_pairs={{0,6},{1,7},{2,4},{3,5},{4,2},{5,3},{6,0},{7,1},{8,14},{9,15},{10,... | collective-permute-start | bytes 393224 | tf_op jit(solution)/shard_map/ppermute | solution.py:69
  101.3 8.1 %collective-permute-start.16 = (bf16[1,4,128,128]{3,2,1,0:T(8,128)(2,1)S(1)}, bf16[1,4,128,128]{3,2,1,0:T(8,128)(2,1)S(1)}, u32[]{:S(2)}, u32[]{:S(2)}) collective-permute-start(bf16[1,4,128,128]{3,2,1,0:T(8,128)(2,1)S(1)} %get-tuple-element.74), channel_id=1, source_target_pairs={{0,2},{1,3},{2,0},{3,1},{4,6},{5,7},{6,4},{7,5},{8,10},{9,11},{10,... | collective-permute-start | bytes 393224 | tf_op jit(solution)/shard_map/ppermute | solution.py:69
  102.4 7.7 %collective-permute-start.17 = (bf16[1,4,128,128]{3,2,1,0:T(8,128)(2,1)S(1)}, bf16[1,4,128,128]{3,2,1,0:T(8,128)(2,1)S(1)}, u32[]{:S(2)}, u32[]{:S(2)}) collective-permute-start(bf16[1,4,128,128]{3,2,1,0:T(8,128)(2,1)S(1)} %get-tuple-element.75), channel_id=1, source_target_pairs={{0,4},{1,5},{2,6},{3,7},{4,0},{5,1},{6,2},{7,3},{8,12},{9,13},{10,... | collective-permute-start | bytes 393224 | tf_op jit(solution)/shard_map/ppermute | solution.py:69
  104.2 8.3 %collective-permute-start.18 = (bf16[1,4,128,128]{3,2,1,0:T(8,128)(2,1)S(1)}, bf16[1,4,128,128]{3,2,1,0:T(8,128)(2,1)S(1)}, u32[]{:S(2)}, u32[]{:S(2)}) collective-permute-start(bf16[1,4,128,128]{3,2,1,0:T(8,128)(2,1)S(1)} %get-tuple-element.76), channel_id=1, source_target_pairs={{0,6},{1,7},{2,4},{3,5},{4,2},{5,3},{6,0},{7,1},{8,14},{9,15},{10,... | collective-permute-start | bytes 393224 | tf_op jit(solution)/shard_map/ppermute | solution.py:69

commit v3 on v0

--- a/solution.py
+++ b/solution.py
@@ -379,6 +379,7 @@
     v_refs = take(width)
     if not first:
         (dq_before,) = take(1)
+    kv_before = [] if first else take(na)
     kv_outs = take(na)
     dq_outs = take(nb if last else 1)
     dk_all, dv_all = take(2)
@@ -449,10 +450,13 @@
 
     lax.fori_loop(0, na, away, 0)
 
+    done = 0 if first else kv_before[0].shape[1]
     for s, out in enumerate(kv_outs):
+        if done:
+            out[:, :done] = kv_before[s][...]
         for x in range(width):
-            out[0, x] = (scale * dk_all[s * width + x]).astype(BF16)
-            out[1, x] = dv_all[s * width + x].astype(BF16)
+            out[0, done + x] = (scale * dk_all[s * width + x]).astype(BF16)
+            out[1, done + x] = dv_all[s * width + x].astype(BF16)
     if last:
         for t in range(nb):
 
@@ -463,12 +467,13 @@
             lax.fori_loop(0, own, drain, 0)
 
 
-def grads(plan, span, tables, queries, out_grads, lse, delta, keys, values, dq_before, last):
+def grads(plan, span, tables, queries, out_grads, lse, delta, keys, values, dq_before, kv_before, last):
     nb, na, own, rows, total = plan.nb, plan.na, plan.own, plan.rows, plan.total
     hd, width, first = HEAD_DIM, len(span), dq_before is None
-    kv = [sds((2, width, rows, hd), BF16)] * na
+    done = 0 if first else kv_before[0].shape[1]
+    kv = [sds((2, done + width, rows, hd), BF16)] * na
     dq = [sds((own, rows, hd), F32)] * nb if last else [sds((total, rows, hd), F32)]
-    before = [] if first else [dq_before]
+    before = [] if first else [dq_before, *kv_before]
     partial = sds((own, rows, hd), F32)
     outs = pl.pallas_call(
         functools.partial(grads_kernel, plan, span, first, last),
@@ -567,17 +572,17 @@
     lse_part, q_all = totals(plan, by_key, n_key, keys, swapped([q_own] * nb))
     lse, delta, g_all = query_rows(plan, swapped([g_own] * nb), swapped([lse_part] * nb))
     spans = [range(0, 2), range(2, nz)]
-    kv_home, dq = [], None
+    kv, dq = [], None
     for place, span in enumerate(spans):
         last = place == len(spans) - 1
         kv, dq_parts = grads(
             plan, span, (by_key, n_key), q_all, g_all, lse, delta, keys,
-            [values[r] for r in span], dq, last,
+            [values[r] for r in span], dq, kv, last,
         )
         dq = dq_parts[0]
-        kv_home.append(frame_stage(kv))
+    kv_home = frame_stage(kv)
     dq_home = frame_stage(pack(plan, swapped(dq_parts)))
-    grad_key, grad_value = assemble(plan, ids, spans, kv_home)
+    grad_key, grad_value = assemble(plan, ids, [range(nz)], [kv_home])
     (grad_query,) = assemble(plan, ids, [range(nz)], [dq_home])
     return grad_query, grad_key, grad_value
 

time: 114 us -> 114 us (level)
  starting transfers between devices: 37.5 us -> 33.7 us
  waiting for transfers between devices: 39.7 us -> 43.5 us
    ppermute x19 -> x16, starting transfers between devices: 18.8 us -> 15 us  [over_frame(): return lax.ppermute(value, 'frame', [(i, i ^ step) for i in range(count)])]
    ppermute x19 -> x16, waiting for transfers between devices: 28.4 us -> 32.1 us  [over_frame(): return lax.ppermute(value, 'frame', [(i, i ^ step) for i in range(count)])]
  transfers between devices with their start and end apart: 26 -> 23, of which waited for: 15 -> 12; matrix products, arithmetic and copies ran while one was open for 0% -> 0% of each run, Pallas kernels for 20% -> 20%
where the time goes in v3:
time: 114 us
  waiting for transfers between devices  43.5 us (38%)
  Pallas kernels  35.8 us (31%)
  starting transfers between devices  33.7 us (30%)
    ppermute x16, waiting for transfers between devices, over_frame(): return lax.ppermute(value, 'frame', [(i, i ^ step) for i in range(count)])  32.1 us
    pallas_call x2, Pallas kernels, grads(): pl.pallas_call(functools.partial(grads_kernel, plan, span, first, last),...  17.8 us
    ppermute x16, starting transfers between devices, over_frame(): return lax.ppermute(value, 'frame', [(i, i ^ step) for i in range(count)])  15 us
    ppermute x6, waiting for transfers between devices, over_head(): return lax.ppermute(value, 'head', [(i, i ^ step) for i in range(count)])  11.3 us
    ppermute x6, starting transfers between devices, over_head(): return lax.ppermute(value, 'head', [(i, i ^ step) for i in range(count)])  10.3 us
    all_to_all x1, starting transfers between devices, local(): lax.all_to_all(prep(plan, queries, key_states), ('frame', 'head'), 0, 0,...  8.34 us
    pallas_call x1, Pallas kernels, totals(): pl.pallas_call(functools.partial(totals_kernel, plan), out_shape=[sds((pl...  5.87 us
    pallas_call x1, Pallas kernels, lists(): pl.pallas_call(functools.partial(lists_kernel, plan), out_shape=[sds((own...  3.47 us
  transfers between devices with their start and end apart: 23, of which 12 were waited for; matrix products, arithmetic and copies ran while one was open for 0% of the time, Pallas kernels for 20%

profile of v3, /device:TPU:0, one launch (start us, length us, event | category | flops | bytes accessed | tf_op | source)
XLA Modules:
  0.0 113.9 jit_solution(6433402804121875512)
XLA Ops:
  0.6 0.0 copy-start
  0.6 0.0 copy-start.1
  0.7 2.5 %prep.1 = bf16[16,256,128]{2,1,0:T(8,128)(2,1)} custom-call(bf16[128,2048]{1,0:T(8,128)(2,1)} %q_ref.1, bf16[128,2048]{1,0:T(8,128)(2,1)} %k_ref.1), custom_call_target="tpu_custom_call" | custom-call | bytes 5250000 | tf_op jit(solution)/shard_map/prep/pallas_call | solution.py:98
  3.1 8.3 %all-to-all-start = ((bf16[16,256,128]{2,1,0:T(8,128)(2,1)}), bf16[16,256,128]{2,1,0:T(8,128)(2,1)S(1)}, u32[]{:S(2)}, u32[]{:S(2)}) async-start(bf16[16,256,128]{2,1,0:T(8,128)(2,1)} %prep.1), calls=%async_computation | async-start | bytes 2097152 | tf_op jit(solution)/shard_map/all_to_all | solution.py:561
  11.5 0.1 pad_add_fusion.ids
  11.6 0.0 copy-done
  11.6 0.0 copy-start.3
  11.6 0.0 copy-start.4
  11.6 2.1 %prep_rest.1 = (bf16[4,136,128]{2,1,0:T(8,128)(2,1)S(1)}, bf16[4,136,128]{2,1,0:T(8,128)(2,1)S(1)}, bf16[4,136,128]{2,1,0:T(8,128)(2,1)S(1)}, bf16[4,136,128]{2,...) custom-call(s32[3]{0:T(128)S(1)} %pad_add_fusion.ids, ...), custom_call_target="tpu_custom_call" | custom-call | bytes 7000000 | tf_op jit(solution)/shard_map/prep_rest/pallas_call | solution.py:158
  13.7 2.0 %collective-permute-start.1 = (bf16[4,136,128]{2,1,0:T(8,128)(2,1)S(1)}, bf16[4,136,128]{2,1,0:T(8,128)(2,1)S(1)}, u32[]{:S(2)}, u32[]{:S(2)}) collective-permute-start(bf16[4,136,128]{2,1,0:T(8,128)(2,1)S(1)} %get-tuple-element.51), channel_id=1, source_target_pairs={{0,2},{1,3},{2,0},{3,1},{4,6},{5,7},{6,4},{7,5},{8,10},{9,11},{10,... | collective-permute-start | bytes 417800 | tf_op jit(solution)/shard_map/ppermute | solution.py:69
  15.7 1.5 %collective-permute-start.2 = (bf16[4,136,128]{2,1,0:T(8,128)(2,1)S(1)}, bf16[4,136,128]{2,1,0:T(8,128)(2,1)S(1)}, u32[]{:S(2)}, u32[]{:S(2)}) collective-permute-start(bf16[4,136,128]{2,1,0:T(8,128)(2,1)S(1)} %get-tuple-element.52), channel_id=1, source_target_pairs={{0,4},{1,5},{2,6},{3,7},{4,0},{5,1},{6,2},{7,3},{8,12},{9,13},{10,... | collective-permute-start | bytes 417800 | tf_op jit(solution)/shard_map/ppermute | solution.py:69
  17.1 0.1 collective-permute-start.3
  17.3 9.3 %collective-permute-done.1.refs_1_ = bf16[4,136,128]{2,1,0:T(8,128)(2,1)S(1)} collective-permute-done((bf16[4,136,128]{2,1,0:T(8,128)(2,1)S(1)}, bf16[4,136,128]{2,1,0:T(8,128)(2,1)S(1)}, u32[]{:S(2)}, u32[]{:S(2)}) %collective-permute-start.1) | collective-permute-done | bytes 139296 | tf_op jit(solution)/shard_map/ppermute | solution.py:69
  26.5 1.5 %collective-permute-done.2.refs_2_ = bf16[4,136,128]{2,1,0:T(8,128)(2,1)S(1)} collective-permute-done((bf16[4,136,128]{2,1,0:T(8,128)(2,1)S(1)}, bf16[4,136,128]{2,1,0:T(8,128)(2,1)S(1)}, u32[]{:S(2)}, u32[]{:S(2)}) %collective-permute-start.2) | collective-permute-done | bytes 139296 | tf_op jit(solution)/shard_map/ppermute | solution.py:69
  28.0 2.4 %collective-permute-done.3.refs_3_ = bf16[4,136,128]{2,1,0:T(8,128)(2,1)S(1)} collective-permute-done((bf16[4,136,128]{2,1,0:T(8,128)(2,1)S(1)}, bf16[4,136,128]{2,1,0:T(8,128)(2,1)S(1)}, u32[]{:S(2)}, u32[]{:S(2)}) %collective-permute-start.3) | collective-permute-done | bytes 139296 | tf_op jit(solution)/shard_map/ppermute | solution.py:69
  30.5 0.1 collective-permute-start.4
  30.6 5.2 %collective-permute-start.5 = (bf16[4,136,128]{2,1,0:T(8,128)(2,1)S(1)}, bf16[4,136,128]{2,1,0:T(8,128)(2,1)S(1)}, u32[]{:S(2)}, u32[]{:S(2)}) collective-permute-start(bf16[4,136,128]{2,1,0:T(8,128)(2,1)S(1)} %get-tuple-element.56), channel_id=1, source_target_pairs={{0,16},{8,24},{16,0},{24,8},{1,17},{9,25},{17,1},{25,9},{2,18},{10... | collective-permute-start | bytes 417800 | tf_op jit(solution)/shard_map/ppermute | solution.py:64
  35.8 0.0 collective-permute-start.6
  35.8 0.6 collective-permute-done.4.refs_1_
  36.4 10.7 %collective-permute-done.5.refs_2_ = bf16[4,136,128]{2,1,0:T(8,128)(2,1)S(1)} collective-permute-done((bf16[4,136,128]{2,1,0:T(8,128)(2,1)S(1)}, bf16[4,136,128]{2,1,0:T(8,128)(2,1)S(1)}, u32[]{:S(2)}, u32[]{:S(2)}) %collective-permute-start.5) | collective-permute-done | bytes 139296 | tf_op jit(solution)/shard_map/ppermute | solution.py:64
  47.1 0.0 collective-permute-done.6.refs_3_
  47.1 0.1 collective-permute-start.7
  47.2 0.0 all-to-all-done.x_ref
  47.2 0.6 part.1
  47.9 0.6 collective-permute-start
  48.4 1.5 %collective-permute-start.9 = (bf16[4,128,128]{2,1,0:T(8,128)(2,1)S(1)}, bf16[4,128,128]{2,1,0:T(8,128)(2,1)S(1)}, u32[]{:S(2)}, u32[]{:S(2)}) collective-permute-start(bf16[4,128,128]{2,1,0:T(8,128)(2,1)S(1)} %get-tuple-element.63), channel_id=1, source_target_pairs={{0,2},{1,3},{2,0},{3,1},{4,6},{5,7},{6,4},{7,5},{8,10},{9,11},{10,... | collective-permute-start | bytes 393224 | tf_op jit(solution)/shard_map/ppermute | solution.py:69
  49.9 1.5 %collective-permute-start.10 = (bf16[4,128,128]{2,1,0:T(8,128)(2,1)S(1)}, bf16[4,128,128]{2,1,0:T(8,128)(2,1)S(1)}, u32[]{:S(2)}, u32[]{:S(2)}) collective-permute-start(bf16[4,128,128]{2,1,0:T(8,128)(2,1)S(1)} %get-tuple-element.64), channel_id=1, source_target_pairs={{0,4},{1,5},{2,6},{3,7},{4,0},{5,1},{6,2},{7,3},{8,12},{9,13},{10,... | collective-permute-start | bytes 393224 | tf_op jit(solution)/shard_map/ppermute | solution.py:69
  51.3 0.6 collective-permute-start.11
  51.9 2.4 %collective-permute-done.9.refs_1_ = bf16[4,128,128]{2,1,0:T(8,128)(2,1)S(1)} collective-permute-done((bf16[4,128,128]{2,1,0:T(8,128)(2,1)S(1)}, bf16[4,128,128]{2,1,0:T(8,128)(2,1)S(1)}, u32[]{:S(2)}, u32[]{:S(2)}) %collective-permute-start.9) | collective-permute-done | bytes 131104 | tf_op jit(solution)/shard_map/ppermute | solution.py:69
  54.3 3.6 %collective-permute-done.10.refs_2_ = bf16[4,128,128]{2,1,0:T(8,128)(2,1)S(1)} collective-permute-done((bf16[4,128,128]{2,1,0:T(8,128)(2,1)S(1)}, bf16[4,128,128]{2,1,0:T(8,128)(2,1)S(1)}, u32[]{:S(2)}, u32[]{:S(2)}) %collective-permute-start.10) | collective-permute-done | bytes 131104 | tf_op jit(solution)/shard_map/ppermute | solution.py:69
  57.9 0.0 collective-permute-done.11.refs_3_
  57.9 2.6 %collective-permute-start.14 = (bf16[4,128,128]{2,1,0:T(8,128)(2,1)S(1)}, bf16[4,128,128]{2,1,0:T(8,128)(2,1)S(1)}, u32[]{:S(2)}, u32[]{:S(2)}) collective-permute-start(bf16[4,128,128]{2,1,0:T(8,128)(2,1)S(1)} %get-tuple-element.69), channel_id=1, source_target_pairs={{0,8},{8,0},{16,24},{24,16},{1,9},{9,1},{17,25},{25,17},{2,10},{10... | collective-permute-start | bytes 393224 | tf_op jit(solution)/shard_map/ppermute | solution.py:64
  60.5 0.1 collective-permute-start.12
  60.7 2.3 %collective-permute-start.13 = (bf16[4,128,128]{2,1,0:T(8,128)(2,1)S(1)}, bf16[4,128,128]{2,1,0:T(8,128)(2,1)S(1)}, u32[]{:S(2)}, u32[]{:S(2)}) collective-permute-start(bf16[4,128,128]{2,1,0:T(8,128)(2,1)S(1)} %get-tuple-element.67), channel_id=1, source_target_pairs={{0,24},{8,16},{16,8},{24,0},{1,25},{9,17},{17,9},{25,1},{2,26},{10... | collective-permute-start | bytes 393224 | tf_op jit(solution)/shard_map/ppermute | solution.py:64
  63.0 0.0 copy-done.4
  63.0 3.5 %lists.1 = (s32[16,42]{1,0:T(8,128)S(1)}, s32[16]{0:T(128)S(1)}) custom-call(s32[3]{0:T(128)S(1)} %pad_add_fusion.ids, s32[8]{0:T(128)S(1)} %copy-done.4, s32[4,4,8]{2,1,0:T(4,128)S(1)} %bitcast.4), custom_call_target="tpu_custom_call" | custom-call | bytes 10500000 | tf_op jit(solution)/shard_map/lists/pallas_call | solution.py:242
  66.5 0.0 collective-permute-done.refs_1_
  66.5 5.9 %totals.1 = (f32[32,128]{1,0:T(8,128)S(1)}, bf16[32,128,128]{2,1,0:T(8,128)(2,1)S(1)}) custom-call(s32[16,42]{1,0:T(8,128)S(1)} %get-tuple-element.45.by_key, s32[16]{0:T(128)S(1)} %get-tuple-element.46.n_key, bf16[16,128,128]{2,1,0:T(8,128)(2,1)S(1)} %get-tuple-element.47.k_ref, bf16[16,128,128]{2,1,0:T(8,128)(2,1)S(1)} %get-tuple-element.48.refs_0_, ...), custom_call_target="tpu_custom_call" | custom-call | bytes 21000000 | tf_op jit(solution)/shard_map/totals/pallas_call | solution.py:330
  72.4 0.1 collective-permute-start.8
  72.4 0.0 collective-permute-done.7.refs_1_
  72.5 1.2 %collective-permute-done.8.refs_3_ = f32[32,128]{1,0:T(8,128)S(1)} collective-permute-done((f32[32,128]{1,0:T(8,128)S(1)}, f32[32,128]{1,0:T(8,128)S(1)}, u32[]{:S(2)}, u32[]{:S(2)}) %collective-permute-start.8) | collective-permute-done | bytes 16416 | tf_op jit(solution)/shard_map/ppermute | solution.py:69
  73.6 0.1 query_rows.1
  73.7 0.0 collective-permute-done.14.refs_1_
  73.7 8.6 %shard_map.97 = (bf16[2,2,128,128]{3,2,1,0:T(8,128)(2,1)S(1)}, bf16[2,2,128,128]{3,2,1,0:T(8,128)(2,1)S(1)}, bf16[2,2,128,128]{3,2,1,0:T(8,128)(2,1)S(1)}, bf16[...) custom-call(s32[16,42]{1,0:T(8,128)S(1)} %get-tuple-element.45.by_key, s32[16]{0:T(128)S(1)} %get-tuple-element.46.n_key, ...), custom_call_target="tpu_custom_call" | custom-call | bytes 24500000 | tf_op jit(solution)/shard_map/pallas_call | solution.py:478
  82.4 0.0 collective-permute-done.12.refs_0_
  82.4 0.0 collective-permute-done.13.refs_1_
  82.4 9.1 %shard_map.98 = (bf16[2,4,128,128]{3,2,1,0:T(8,128)(2,1)S(1)}, bf16[2,4,128,128]{3,2,1,0:T(8,128)(2,1)S(1)}, bf16[2,4,128,128]{3,2,1,0:T(8,128)(2,1)S(1)}, bf16[...) custom-call(s32[16,42]{1,0:T(8,128)S(1)} %get-tuple-element.45.by_key, ...), custom_call_target="tpu_custom_call" | custom-call | bytes 24500000 | tf_op jit(solution)/shard_map/pallas_call | solution.py:478
  91.5 0.2 collective-permute-start.15
  91.8 1.2 %collective-permute-start.19 = (bf16[2,4,128,128]{3,2,1,0:T(8,128)(2,1)S(1)}, bf16[2,4,128,128]{3,2,1,0:T(8,128)(2,1)S(1)}, u32[]{:S(2)}, u32[]{:S(2)}) collective-permute-start(bf16[2,4,128,128]{3,2,1,0:T(8,128)(2,1)S(1)} %get-tuple-element.82), channel_id=1, source_target_pairs={{0,2},{1,3},{2,0},{3,1},{4,6},{5,7},{6,4},{7,5},{8,10},{9,11},{10,... | collective-permute-start | bytes 786440 | tf_op jit(solution)/shard_map/ppermute | solution.py:69
  92.9 0.9 collective-permute-start.20
  93.8 1.5 %collective-permute-start.21 = (bf16[2,4,128,128]{3,2,1,0:T(8,128)(2,1)S(1)}, bf16[2,4,128,128]{3,2,1,0:T(8,128)(2,1)S(1)}, u32[]{:S(2)}, u32[]{:S(2)}) collective-permute-start(bf16[2,4,128,128]{3,2,1,0:T(8,128)(2,1)S(1)} %get-tuple-element.84), channel_id=1, source_target_pairs={{0,6},{1,7},{2,4},{3,5},{4,2},{5,3},{6,0},{7,1},{8,14},{9,15},{10,... | collective-permute-start | bytes 786440 | tf_op jit(solution)/shard_map/ppermute | solution.py:69
  95.3 0.0 collective-permute-done.15.refs_1_
  95.3 0.2 pack.1
  95.4 1.2 %collective-permute-start.16 = (bf16[1,4,128,128]{3,2,1,0:T(8,128)(2,1)S(1)}, bf16[1,4,128,128]{3,2,1,0:T(8,128)(2,1)S(1)}, u32[]{:S(2)}, u32[]{:S(2)}) collective-permute-start(bf16[1,4,128,128]{3,2,1,0:T(8,128)(2,1)S(1)} %get-tuple-element.78), channel_id=1, source_target_pairs={{0,2},{1,3},{2,0},{3,1},{4,6},{5,7},{6,4},{7,5},{8,10},{9,11},{10,... | collective-permute-start | bytes 393224 | tf_op jit(solution)/shard_map/ppermute | solution.py:69
  96.7 0.9 collective-permute-start.17
  97.5 3.4 %collective-permute-done.19.refs_1_ = bf16[2,4,128,128]{3,2,1,0:T(8,128)(2,1)S(1)} collective-permute-done((bf16[2,4,128,128]{3,2,1,0:T(8,128)(2,1)S(1)}, bf16[2,4,128,128]{3,2,1,0:T(8,128)(2,1)S(1)}, u32[]{:S(2)}, u32[]{:S(2)}) %collective-permute-start.19) | collective-permute-done | bytes 262176 | tf_op jit(solution)/shard_map/ppermute | solution.py:69
  100.9 1.5 %collective-permute-start.18 = (bf16[1,4,128,128]{3,2,1,0:T(8,128)(2,1)S(1)}, bf16[1,4,128,128]{3,2,1,0:T(8,128)(2,1)S(1)}, u32[]{:S(2)}, u32[]{:S(2)}) collective-permute-start(bf16[1,4,128,128]{3,2,1,0:T(8,128)(2,1)S(1)} %get-tuple-element.80), channel_id=1, source_target_pairs={{0,6},{1,7},{2,4},{3,5},{4,2},{5,3},{6,0},{7,1},{8,14},{9,15},{10,... | collective-permute-start | bytes 393224 | tf_op jit(solution)/shard_map/ppermute | solution.py:69
  102.4 5.3 %collective-permute-done.20.refs_2_ = bf16[2,4,128,128]{3,2,1,0:T(8,128)(2,1)S(1)} collective-permute-done((bf16[2,4,128,128]{3,2,1,0:T(8,128)(2,1)S(1)}, bf16[2,4,128,128]{3,2,1,0:T(8,128)(2,1)S(1)}, u32[]{:S(2)}, u32[]{:S(2)}) %collective-permute-start.20) | collective-permute-done | bytes 262176 | tf_op jit(solution)/shard_map/ppermute | solution.py:69
  107.7 0.0 collective-permute-done.21.refs_3_
  107.7 1.7 %shard_map.100 = (bf16[512,512]{1,0:T(8,128)(2,1)}, bf16[512,512]{1,0:T(8,128)(2,1)}) custom-call(s32[3]{0:T(128)S(1)} %pad_add_fusion.ids, bf16[2,4,128,128]{3,2,1,0:T(8,128)(2,1)S(1)} %get-tuple-element.81.refs_0_, bf16[2,4,128,128]{3,2,1,0:T(8,128)(2,1)S(1)} %collective-permute-done.19.refs_1_, ...), custom_call_target="tpu_custom_call" | custom-call | bytes 5250000 | tf_op jit(solution)/shard_map/pallas_call | solution.py:527
  109.4 0.0 collective-permute-done.16.refs_1_
  109.4 0.8 collective-permute-done.17.refs_2_
  110.2 2.3 %collective-permute-done.18.refs_3_ = bf16[1,4,128,128]{3,2,1,0:T(8,128)(2,1)S(1)} collective-permute-done((bf16[1,4,128,128]{3,2,1,0:T(8,128)(2,1)S(1)}, bf16[1,4,128,128]{3,2,1,0:T(8,128)(2,1)S(1)}, u32[]{:S(2)}, u32[]{:S(2)}) %collective-permute-start.18) | collective-permute-done | bytes 131104 | tf_op jit(solution)/shard_map/ppermute | solution.py:69
  112.5 1.4 %shard_map.99 = bf16[512,512]{1,0:T(8,128)(2,1)} custom-call(s32[3]{0:T(128)S(1)} %pad_add_fusion.ids, bf16[1,4,128,128]{3,2,1,0:T(8,128)(2,1)S(1)} %get-tuple-element.77.refs_0_, bf16[1,4,128,128]{3,2,1,0:T(8,128)(2,1)S(1)} %collective-permute-done.16.refs_1_, bf16[1,4,128,128]{3,2,1,0:T(8,128)(2,1)S(1)} %collective-permute-done.17.refs_2_, ...), custom_call_target="tpu_custom_call" | custom-call | bytes 5250000 | tf_op jit(solution)/shard_map/pallas_call | solution.py:527
  (7 shorter events, 0.1 us)
Async XLA Ops:
  0.6 11.0 %copy-start = (bf16[128,2048]{1,0:T(8,128)(2,1)S(1)}, bf16[128,2048]{1,0:T(8,128)(2,1)}, u32[]{:S(2)}) copy-start(bf16[128,2048]{1,0:T(8,128)(2,1)} %g_ref.1) | copy-start | bytes 1572868
  0.6 10.9 %copy-start.1 = (bf16[128,2048]{1,0:T(8,128)(2,1)S(1)}, bf16[128,2048]{1,0:T(8,128)(2,1)}, u32[]{:S(2)}) copy-start(bf16[128,2048]{1,0:T(8,128)(2,1)} %o_ref.1) | copy-start | bytes 1572868
  0.7 10.9 %copy-start.2 = (bf16[128,2048]{1,0:T(8,128)(2,1)S(1)}, bf16[128,2048]{1,0:T(8,128)(2,1)}, u32[]{:S(2)}) copy-start(bf16[128,2048]{1,0:T(8,128)(2,1)} %v_ref.1) | copy-start | bytes 1572868
  3.1 44.1 %all-to-all-start = ((bf16[16,256,128]{2,1,0:T(8,128)(2,1)}), bf16[16,256,128]{2,1,0:T(8,128)(2,1)S(1)}, u32[]{:S(2)}, u32[]{:S(2)}) async-start(bf16[16,256,128]{2,1,0:T(8,128)(2,1)} %prep.1), calls=%async_computation | async-start | bytes 2097152 | tf_op jit(solution)/shard_map/all_to_all | solution.py:561
  11.6 51.4 %copy-start.3 = (s32[8,4,4]{0,2,1:T(4,128)S(1)}, s32[8,4,4]{0,2,1:T(4,128)}, u32[]{:S(2)}) copy-start(s32[8,4,4]{0,2,1:T(4,128)} %param.13) | copy-start | bytes 1540
  11.6 51.4 %copy-start.4 = (s32[8]{0:T(128)S(1)}, s32[8]{0:T(128)}, u32[]{:S(2)}) copy-start(s32[8]{0:T(128)} %order.1) | copy-start | bytes 100
  13.7 12.8 %collective-permute-start.1 = (bf16[4,136,128]{2,1,0:T(8,128)(2,1)S(1)}, bf16[4,136,128]{2,1,0:T(8,128)(2,1)S(1)}, u32[]{:S(2)}, u32[]{:S(2)}) collective-permute-start(bf16[4,136,128]{2,1,0:T(8,128)(2,1)S(1)} %get-tuple-element.51), channel_id=1, source_target_pairs={{0,2},{1,3},{2,0},{3,1},{4,6},{5,7},{6,4},{7,5},{8,10},{9,11},{10,... | collective-permute-start | bytes 417800 | tf_op jit(solution)/shard_map/ppermute | solution.py:69
  15.7 12.3 %collective-permute-start.2 = (bf16[4,136,128]{2,1,0:T(8,128)(2,1)S(1)}, bf16[4,136,128]{2,1,0:T(8,128)(2,1)S(1)}, u32[]{:S(2)}, u32[]{:S(2)}) collective-permute-start(bf16[4,136,128]{2,1,0:T(8,128)(2,1)S(1)} %get-tuple-element.52), channel_id=1, source_target_pairs={{0,4},{1,5},{2,6},{3,7},{4,0},{5,1},{6,2},{7,3},{8,12},{9,13},{10,... | collective-permute-start | bytes 417800 | tf_op jit(solution)/shard_map/ppermute | solution.py:69
  17.1 13.3 %collective-permute-start.3 = (bf16[4,136,128]{2,1,0:T(8,128)(2,1)S(1)}, bf16[4,136,128]{2,1,0:T(8,128)(2,1)S(1)}, u32[]{:S(2)}, u32[]{:S(2)}) collective-permute-start(bf16[4,136,128]{2,1,0:T(8,128)(2,1)S(1)} %get-tuple-element.53), channel_id=1, source_target_pairs={{0,6},{1,7},{2,4},{3,5},{4,2},{5,3},{6,0},{7,1},{8,14},{9,15},{10,... | collective-permute-start | bytes 417800 | tf_op jit(solution)/shard_map/ppermute | solution.py:69
  30.5 5.9 %collective-permute-start.4 = (bf16[4,136,128]{2,1,0:T(8,128)(2,1)S(1)}, bf16[4,136,128]{2,1,0:T(8,128)(2,1)S(1)}, u32[]{:S(2)}, u32[]{:S(2)}) collective-permute-start(bf16[4,136,128]{2,1,0:T(8,128)(2,1)S(1)} %get-tuple-element.55), channel_id=1, source_target_pairs={{0,8},{8,0},{16,24},{24,16},{1,9},{9,1},{17,25},{25,17},{2,10},{10... | collective-permute-start | bytes 417800 | tf_op jit(solution)/shard_map/ppermute | solution.py:64
  30.6 16.5 %collective-permute-start.5 = (bf16[4,136,128]{2,1,0:T(8,128)(2,1)S(1)}, bf16[4,136,128]{2,1,0:T(8,128)(2,1)S(1)}, u32[]{:S(2)}, u32[]{:S(2)}) collective-permute-start(bf16[4,136,128]{2,1,0:T(8,128)(2,1)S(1)} %get-tuple-element.56), channel_id=1, source_target_pairs={{0,16},{8,24},{16,0},{24,8},{1,17},{9,25},{17,1},{25,9},{2,18},{10... | collective-permute-start | bytes 417800 | tf_op jit(solution)/shard_map/ppermute | solution.py:64
  35.8 11.3 %collective-permute-start.6 = (bf16[4,136,128]{2,1,0:T(8,128)(2,1)S(1)}, bf16[4,136,128]{2,1,0:T(8,128)(2,1)S(1)}, u32[]{:S(2)}, u32[]{:S(2)}) collective-permute-start(bf16[4,136,128]{2,1,0:T(8,128)(2,1)S(1)} %get-tuple-element.57), channel_id=1, source_target_pairs={{0,24},{8,16},{16,8},{24,0},{1,25},{9,17},{17,9},{25,1},{2,26},{10... | collective-permute-start | bytes 417800 | tf_op jit(solution)/shard_map/ppermute | solution.py:64
  47.1 25.3 %collective-permute-start.7 = (bf16[16,136,128]{2,1,0:T(8,128)(2,1)S(1)}, bf16[16,136,128]{2,1,0:T(8,128)(2,1)S(1)}, u32[]{:S(2)}, u32[]{:S(2)}) collective-permute-start(bf16[16,136,128]{2,1,0:T(8,128)(2,1)S(1)} %shard_map.95.refs_0_), channel_id=1, source_target_pairs={{0,1},{1,0},{2,3},{3,2},{4,5},{5,4},{6,7},{7,6},{8,9},{9,8},{10,11... | collective-permute-start | bytes 1671176 | tf_op jit(solution)/shard_map/ppermute | solution.py:69
  47.9 18.6 %collective-permute-start = (bf16[16,128,128]{2,1,0:T(8,128)(2,1)S(1)}, bf16[16,128,128]{2,1,0:T(8,128)(2,1)S(1)}, u32[]{:S(2)}, u32[]{:S(2)}) collective-permute-start(bf16[16,128,128]{2,1,0:T(8,128)(2,1)S(1)} %get-tuple-element.48.refs_0_), channel_id=1, source_target_pairs={{0,1},{1,0},{2,3},{3,2},{4,5},{5,4},{6,7},{7,6},{8,9},{9,8},{10,11... | collective-permute-start | bytes 1572872 | tf_op jit(solution)/shard_map/ppermute | solution.py:69
  48.4 5.9 %collective-permute-start.9 = (bf16[4,128,128]{2,1,0:T(8,128)(2,1)S(1)}, bf16[4,128,128]{2,1,0:T(8,128)(2,1)S(1)}, u32[]{:S(2)}, u32[]{:S(2)}) collective-permute-start(bf16[4,128,128]{2,1,0:T(8,128)(2,1)S(1)} %get-tuple-element.63), channel_id=1, source_target_pairs={{0,2},{1,3},{2,0},{3,1},{4,6},{5,7},{6,4},{7,5},{8,10},{9,11},{10,... | collective-permute-start | bytes 393224 | tf_op jit(solution)/shard_map/ppermute | solution.py:69
  49.9 8.0 %collective-permute-start.10 = (bf16[4,128,128]{2,1,0:T(8,128)(2,1)S(1)}, bf16[4,128,128]{2,1,0:T(8,128)(2,1)S(1)}, u32[]{:S(2)}, u32[]{:S(2)}) collective-permute-start(bf16[4,128,128]{2,1,0:T(8,128)(2,1)S(1)} %get-tuple-element.64), channel_id=1, source_target_pairs={{0,4},{1,5},{2,6},{3,7},{4,0},{5,1},{6,2},{7,3},{8,12},{9,13},{10,... | collective-permute-start | bytes 393224 | tf_op jit(solution)/shard_map/ppermute | solution.py:69
  51.3 6.5 %collective-permute-start.11 = (bf16[4,128,128]{2,1,0:T(8,128)(2,1)S(1)}, bf16[4,128,128]{2,1,0:T(8,128)(2,1)S(1)}, u32[]{:S(2)}, u32[]{:S(2)}) collective-permute-start(bf16[4,128,128]{2,1,0:T(8,128)(2,1)S(1)} %get-tuple-element.65), channel_id=1, source_target_pairs={{0,6},{1,7},{2,4},{3,5},{4,2},{5,3},{6,0},{7,1},{8,14},{9,15},{10,... | collective-permute-start | bytes 393224 | tf_op jit(solution)/shard_map/ppermute | solution.py:69
  57.9 15.8 %collective-permute-start.14 = (bf16[4,128,128]{2,1,0:T(8,128)(2,1)S(1)}, bf16[4,128,128]{2,1,0:T(8,128)(2,1)S(1)}, u32[]{:S(2)}, u32[]{:S(2)}) collective-permute-start(bf16[4,128,128]{2,1,0:T(8,128)(2,1)S(1)} %get-tuple-element.69), channel_id=1, source_target_pairs={{0,8},{8,0},{16,24},{24,16},{1,9},{9,1},{17,25},{25,17},{2,10},{10... | collective-permute-start | bytes 393224 | tf_op jit(solution)/shard_map/ppermute | solution.py:64
  60.5 21.8 %collective-permute-start.12 = (bf16[4,128,128]{2,1,0:T(8,128)(2,1)S(1)}, bf16[4,128,128]{2,1,0:T(8,128)(2,1)S(1)}, u32[]{:S(2)}, u32[]{:S(2)}) collective-permute-start(bf16[4,128,128]{2,1,0:T(8,128)(2,1)S(1)} %get-tuple-element.66), channel_id=1, source_target_pairs={{0,16},{8,24},{16,0},{24,8},{1,17},{9,25},{17,1},{25,9},{2,18},{10... | collective-permute-start | bytes 393224 | tf_op jit(solution)/shard_map/ppermute | solution.py:64
  60.7 21.7 %collective-permute-start.13 = (bf16[4,128,128]{2,1,0:T(8,128)(2,1)S(1)}, bf16[4,128,128]{2,1,0:T(8,128)(2,1)S(1)}, u32[]{:S(2)}, u32[]{:S(2)}) collective-permute-start(bf16[4,128,128]{2,1,0:T(8,128)(2,1)S(1)} %get-tuple-element.67), channel_id=1, source_target_pairs={{0,24},{8,16},{16,8},{24,0},{1,25},{9,17},{17,9},{25,1},{2,26},{10... | collective-permute-start | bytes 393224 | tf_op jit(solution)/shard_map/ppermute | solution.py:64
  72.4 1.2 %collective-permute-start.8 = (f32[32,128]{1,0:T(8,128)S(1)}, f32[32,128]{1,0:T(8,128)S(1)}, u32[]{:S(2)}, u32[]{:S(2)}) collective-permute-start(f32[32,128]{1,0:T(8,128)S(1)} %get-tuple-element.58.refs_2_), channel_id=1, source_target_pairs={{0,1},{1,0},{2,3},{3,2},{4,5},{5,4},{6,7},{7,6},{8,9},{9,8},{10,11... | collective-permute-start | bytes 49160 | tf_op jit(solution)/shard_map/ppermute | solution.py:69
  91.5 3.7 %collective-permute-start.15 = (f32[16,128,128]{2,1,0:T(8,128)S(1)}, f32[16,128,128]{2,1,0:T(8,128)S(1)}, u32[]{:S(2)}, u32[]{:S(2)}) collective-permute-start(f32[16,128,128]{2,1,0:T(8,128)S(1)} %get-tuple-element.76), channel_id=1, source_target_pairs={{0,1},{1,0},{2,3},{3,2},{4,5},{5,4},{6,7},{7,6},{8,9},{9,8},{10,11... | collective-permute-start | bytes 3145736 | tf_op jit(solution)/shard_map/ppermute | solution.py:69
  91.8 9.2 %collective-permute-start.19 = (bf16[2,4,128,128]{3,2,1,0:T(8,128)(2,1)S(1)}, bf16[2,4,128,128]{3,2,1,0:T(8,128)(2,1)S(1)}, u32[]{:S(2)}, u32[]{:S(2)}) collective-permute-start(bf16[2,4,128,128]{3,2,1,0:T(8,128)(2,1)S(1)} %get-tuple-element.82), channel_id=1, source_target_pairs={{0,2},{1,3},{2,0},{3,1},{4,6},{5,7},{6,4},{7,5},{8,10},{9,11},{10,... | collective-permute-start | bytes 786440 | tf_op jit(solution)/shard_map/ppermute | solution.py:69
  92.9 14.8 %collective-permute-start.20 = (bf16[2,4,128,128]{3,2,1,0:T(8,128)(2,1)S(1)}, bf16[2,4,128,128]{3,2,1,0:T(8,128)(2,1)S(1)}, u32[]{:S(2)}, u32[]{:S(2)}) collective-permute-start(bf16[2,4,128,128]{3,2,1,0:T(8,128)(2,1)S(1)} %get-tuple-element.83), channel_id=1, source_target_pairs={{0,4},{1,5},{2,6},{3,7},{4,0},{5,1},{6,2},{7,3},{8,12},{9,13},{10,... | collective-permute-start | bytes 786440 | tf_op jit(solution)/shard_map/ppermute | solution.py:69
  93.8 13.9 %collective-permute-start.21 = (bf16[2,4,128,128]{3,2,1,0:T(8,128)(2,1)S(1)}, bf16[2,4,128,128]{3,2,1,0:T(8,128)(2,1)S(1)}, u32[]{:S(2)}, u32[]{:S(2)}) collective-permute-start(bf16[2,4,128,128]{3,2,1,0:T(8,128)(2,1)S(1)} %get-tuple-element.84), channel_id=1, source_target_pairs={{0,6},{1,7},{2,4},{3,5},{4,2},{5,3},{6,0},{7,1},{8,14},{9,15},{10,... | collective-permute-start | bytes 786440 | tf_op jit(solution)/shard_map/ppermute | solution.py:69
  95.4 14.0 %collective-permute-start.16 = (bf16[1,4,128,128]{3,2,1,0:T(8,128)(2,1)S(1)}, bf16[1,4,128,128]{3,2,1,0:T(8,128)(2,1)S(1)}, u32[]{:S(2)}, u32[]{:S(2)}) collective-permute-start(bf16[1,4,128,128]{3,2,1,0:T(8,128)(2,1)S(1)} %get-tuple-element.78), channel_id=1, source_target_pairs={{0,2},{1,3},{2,0},{3,1},{4,6},{5,7},{6,4},{7,5},{8,10},{9,11},{10,... | collective-permute-start | bytes 393224 | tf_op jit(solution)/shard_map/ppermute | solution.py:69
  96.7 13.5 %collective-permute-start.17 = (bf16[1,4,128,128]{3,2,1,0:T(8,128)(2,1)S(1)}, bf16[1,4,128,128]{3,2,1,0:T(8,128)(2,1)S(1)}, u32[]{:S(2)}, u32[]{:S(2)}) collective-permute-start(bf16[1,4,128,128]{3,2,1,0:T(8,128)(2,1)S(1)} %get-tuple-element.79), channel_id=1, source_target_pairs={{0,4},{1,5},{2,6},{3,7},{4,0},{5,1},{6,2},{7,3},{8,12},{9,13},{10,... | collective-permute-start | bytes 393224 | tf_op jit(solution)/shard_map/ppermute | solution.py:69
  100.9 11.6 %collective-permute-start.18 = (bf16[1,4,128,128]{3,2,1,0:T(8,128)(2,1)S(1)}, bf16[1,4,128,128]{3,2,1,0:T(8,128)(2,1)S(1)}, u32[]{:S(2)}, u32[]{:S(2)}) collective-permute-start(bf16[1,4,128,128]{3,2,1,0:T(8,128)(2,1)S(1)} %get-tuple-element.80), channel_id=1, source_target_pairs={{0,6},{1,7},{2,4},{3,5},{4,2},{5,3},{6,0},{7,1},{8,14},{9,15},{10,... | collective-permute-start | bytes 393224 | tf_op jit(solution)/shard_map/ppermute | solution.py:69

commit v4 on v0

--- a/solution.py
+++ b/solution.py
@@ -415,9 +415,9 @@
 
     lax.fori_loop(0, na, diagonal, 0)
 
-    def terms(s, x, j, start):
+    def terms(s, x, j, start, size):
         k, v = k_ref[j], v_refs[x][s]
-        chosen = picks(by_key, j, n_key[j], start, KEY_GROUP)
+        chosen = picks(by_key, j, n_key[j], start, size)
         q = jnp.concatenate([q_ref[i] for i, _ in chosen], axis=0)
         g = jnp.concatenate([g_ref[i] for i, _ in chosen], axis=0)
         lse = jnp.concatenate([jnp.where(ok, lse_ref[pl.ds(i, 1), :], -NEG) for i, ok in chosen], axis=1)
@@ -436,15 +436,22 @@
             dq_all[i] += dq[u * rows : (u + 1) * rows]
 
     def away(s, carry):
-        for x, found in [(x, terms(s, x, s * nz + r, 0)) for x, r in enumerate(span)]:
-            add(s, x, found)
+        most = functools.reduce(jnp.maximum, [n_key[s * nz + r] for r in span])
+
+        def together(size):
+            for x, found in [(x, terms(s, x, s * nz + r, 0, size)) for x, r in enumerate(span)]:
+                add(s, x, found)
+
+        pl.when((most > 0) & (most <= KEY_GROUP))(lambda: together(KEY_GROUP))
+        pl.when(most > KEY_GROUP)(lambda: together(WIDE_GROUP))
         for x, r in enumerate(span):
+            left = jnp.maximum(n_key[s * nz + r] - WIDE_GROUP, 0)
 
             def group(step, carry, x=x, r=r):
-                add(s, x, terms(s, x, s * nz + r, step * KEY_GROUP))
+                add(s, x, terms(s, x, s * nz + r, WIDE_GROUP + step * KEY_GROUP, KEY_GROUP))
                 return carry
 
-            lax.fori_loop(1, steps(n_key[s * nz + r], KEY_GROUP), group, 0)
+            lax.fori_loop(0, steps(left, KEY_GROUP), group, 0)
         return carry
 
     lax.fori_loop(0, na, away, 0)

time: 114 us -> 113 us (level)
  Pallas kernels: 35.8 us -> 34.2 us
    pallas_call x2, Pallas kernels: 17.7 us -> 16.2 us  [grads(): pl.pallas_call(functools.partial(grads_kernel, plan, span, first, last),...]
where the time goes in v4:
time: 113 us; the launch traced here: 112 us
  waiting for transfers between devices  39.7 us (35%)
  starting transfers between devices  37.5 us (33%)
  Pallas kernels  34.2 us (30%)
    ppermute x19, waiting for transfers between devices, over_frame(): return lax.ppermute(value, 'frame', [(i, i ^ step) for i in range(count)])  28.4 us
    ppermute x19, starting transfers between devices, over_frame(): return lax.ppermute(value, 'frame', [(i, i ^ step) for i in range(count)])  18.8 us
    pallas_call x2, Pallas kernels, grads(): pl.pallas_call(functools.partial(grads_kernel, plan, span, first, last),...  16.2 us
    ppermute x6, waiting for transfers between devices, over_head(): return lax.ppermute(value, 'head', [(i, i ^ step) for i in range(count)])  11.3 us
    ppermute x6, starting transfers between devices, over_head(): return lax.ppermute(value, 'head', [(i, i ^ step) for i in range(count)])  10.3 us
    all_to_all x1, starting transfers between devices, local(): lax.all_to_all(prep(plan, queries, key_states), ('frame', 'head'), 0, 0,...  8.34 us
    pallas_call x1, Pallas kernels, totals(): pl.pallas_call(functools.partial(totals_kernel, plan), out_shape=[sds((pl...  5.88 us
    pallas_call x1, Pallas kernels, lists(): pl.pallas_call(functools.partial(lists_kernel, plan), out_shape=[sds((own...  3.47 us
  transfers between devices with their start and end apart: 26, of which 15 were waited for; matrix products, arithmetic and copies ran while one was open for 0% of the time, Pallas kernels for 20%

profile of v4, /device:TPU:0, one launch (start us, length us, event | category | flops | bytes accessed | tf_op | source)
XLA Modules:
  0.0 112.4 jit_solution(14754483006599774664)
XLA Ops:
  0.7 2.5 %prep.1 = bf16[16,256,128]{2,1,0:T(8,128)(2,1)} custom-call(bf16[128,2048]{1,0:T(8,128)(2,1)} %q_ref.1, bf16[128,2048]{1,0:T(8,128)(2,1)} %k_ref.1), custom_call_target="tpu_custom_call" | custom-call | bytes 5250000 | tf_op jit(solution)/shard_map/prep/pallas_call | solution.py:98
  3.2 8.3 %all-to-all-start = ((bf16[16,256,128]{2,1,0:T(8,128)(2,1)}), bf16[16,256,128]{2,1,0:T(8,128)(2,1)S(1)}, u32[]{:S(2)}, u32[]{:S(2)}) async-start(bf16[16,256,128]{2,1,0:T(8,128)(2,1)} %prep.1), calls=%async_computation | async-start | bytes 2097152 | tf_op jit(solution)/shard_map/all_to_all | solution.py:563
  11.5 0.1 pad_add_fusion.ids
  11.6 0.0 copy-start.3
  11.6 0.0 copy-start.4
  11.6 2.1 %prep_rest.1 = (bf16[4,136,128]{2,1,0:T(8,128)(2,1)S(1)}, bf16[4,136,128]{2,1,0:T(8,128)(2,1)S(1)}, bf16[4,136,128]{2,1,0:T(8,128)(2,1)S(1)}, bf16[4,136,128]{2,...) custom-call(s32[3]{0:T(128)S(1)} %pad_add_fusion.ids, ...), custom_call_target="tpu_custom_call" | custom-call | bytes 7000000 | tf_op jit(solution)/shard_map/prep_rest/pallas_call | solution.py:158
  13.7 2.0 %collective-permute-start.1 = (bf16[4,136,128]{2,1,0:T(8,128)(2,1)S(1)}, bf16[4,136,128]{2,1,0:T(8,128)(2,1)S(1)}, u32[]{:S(2)}, u32[]{:S(2)}) collective-permute-start(bf16[4,136,128]{2,1,0:T(8,128)(2,1)S(1)} %get-tuple-element.51), channel_id=1, source_target_pairs={{0,2},{1,3},{2,0},{3,1},{4,6},{5,7},{6,4},{7,5},{8,10},{9,11},{10,... | collective-permute-start | bytes 417800 | tf_op jit(solution)/shard_map/ppermute | solution.py:69
  15.7 1.5 %collective-permute-start.2 = (bf16[4,136,128]{2,1,0:T(8,128)(2,1)S(1)}, bf16[4,136,128]{2,1,0:T(8,128)(2,1)S(1)}, u32[]{:S(2)}, u32[]{:S(2)}) collective-permute-start(bf16[4,136,128]{2,1,0:T(8,128)(2,1)S(1)} %get-tuple-element.52), channel_id=1, source_target_pairs={{0,4},{1,5},{2,6},{3,7},{4,0},{5,1},{6,2},{7,3},{8,12},{9,13},{10,... | collective-permute-start | bytes 417800 | tf_op jit(solution)/shard_map/ppermute | solution.py:69
  17.2 0.1 collective-permute-start.3
  17.3 9.3 %collective-permute-done.1.refs_1_ = bf16[4,136,128]{2,1,0:T(8,128)(2,1)S(1)} collective-permute-done((bf16[4,136,128]{2,1,0:T(8,128)(2,1)S(1)}, bf16[4,136,128]{2,1,0:T(8,128)(2,1)S(1)}, u32[]{:S(2)}, u32[]{:S(2)}) %collective-permute-start.1) | collective-permute-done | bytes 139296 | tf_op jit(solution)/shard_map/ppermute | solution.py:69
  26.5 1.5 %collective-permute-done.2.refs_2_ = bf16[4,136,128]{2,1,0:T(8,128)(2,1)S(1)} collective-permute-done((bf16[4,136,128]{2,1,0:T(8,128)(2,1)S(1)}, bf16[4,136,128]{2,1,0:T(8,128)(2,1)S(1)}, u32[]{:S(2)}, u32[]{:S(2)}) %collective-permute-start.2) | collective-permute-done | bytes 139296 | tf_op jit(solution)/shard_map/ppermute | solution.py:69
  28.0 2.4 %collective-permute-done.3.refs_3_ = bf16[4,136,128]{2,1,0:T(8,128)(2,1)S(1)} collective-permute-done((bf16[4,136,128]{2,1,0:T(8,128)(2,1)S(1)}, bf16[4,136,128]{2,1,0:T(8,128)(2,1)S(1)}, u32[]{:S(2)}, u32[]{:S(2)}) %collective-permute-start.3) | collective-permute-done | bytes 139296 | tf_op jit(solution)/shard_map/ppermute | solution.py:69
  30.5 0.1 collective-permute-start.4
  30.6 5.2 %collective-permute-start.5 = (bf16[4,136,128]{2,1,0:T(8,128)(2,1)S(1)}, bf16[4,136,128]{2,1,0:T(8,128)(2,1)S(1)}, u32[]{:S(2)}, u32[]{:S(2)}) collective-permute-start(bf16[4,136,128]{2,1,0:T(8,128)(2,1)S(1)} %get-tuple-element.56), channel_id=1, source_target_pairs={{0,16},{8,24},{16,0},{24,8},{1,17},{9,25},{17,1},{25,9},{2,18},{10... | collective-permute-start | bytes 417800 | tf_op jit(solution)/shard_map/ppermute | solution.py:64
  35.8 0.0 collective-permute-start.6
  35.8 0.6 collective-permute-done.4.refs_1_
  36.4 10.7 %collective-permute-done.5.refs_2_ = bf16[4,136,128]{2,1,0:T(8,128)(2,1)S(1)} collective-permute-done((bf16[4,136,128]{2,1,0:T(8,128)(2,1)S(1)}, bf16[4,136,128]{2,1,0:T(8,128)(2,1)S(1)}, u32[]{:S(2)}, u32[]{:S(2)}) %collective-permute-start.5) | collective-permute-done | bytes 139296 | tf_op jit(solution)/shard_map/ppermute | solution.py:64
  47.1 0.0 collective-permute-done.6.refs_3_
  47.2 0.1 collective-permute-start.7
  47.2 0.0 all-to-all-done.x_ref
  47.3 0.6 part.1
  47.9 0.6 collective-permute-start
  48.4 1.5 %collective-permute-start.9 = (bf16[4,128,128]{2,1,0:T(8,128)(2,1)S(1)}, bf16[4,128,128]{2,1,0:T(8,128)(2,1)S(1)}, u32[]{:S(2)}, u32[]{:S(2)}) collective-permute-start(bf16[4,128,128]{2,1,0:T(8,128)(2,1)S(1)} %get-tuple-element.63), channel_id=1, source_target_pairs={{0,2},{1,3},{2,0},{3,1},{4,6},{5,7},{6,4},{7,5},{8,10},{9,11},{10,... | collective-permute-start | bytes 393224 | tf_op jit(solution)/shard_map/ppermute | solution.py:69
  49.9 1.5 %collective-permute-start.10 = (bf16[4,128,128]{2,1,0:T(8,128)(2,1)S(1)}, bf16[4,128,128]{2,1,0:T(8,128)(2,1)S(1)}, u32[]{:S(2)}, u32[]{:S(2)}) collective-permute-start(bf16[4,128,128]{2,1,0:T(8,128)(2,1)S(1)} %get-tuple-element.64), channel_id=1, source_target_pairs={{0,4},{1,5},{2,6},{3,7},{4,0},{5,1},{6,2},{7,3},{8,12},{9,13},{10,... | collective-permute-start | bytes 393224 | tf_op jit(solution)/shard_map/ppermute | solution.py:69
  51.4 0.6 collective-permute-start.11
  51.9 2.4 %collective-permute-done.9.refs_1_ = bf16[4,128,128]{2,1,0:T(8,128)(2,1)S(1)} collective-permute-done((bf16[4,128,128]{2,1,0:T(8,128)(2,1)S(1)}, bf16[4,128,128]{2,1,0:T(8,128)(2,1)S(1)}, u32[]{:S(2)}, u32[]{:S(2)}) %collective-permute-start.9) | collective-permute-done | bytes 131104 | tf_op jit(solution)/shard_map/ppermute | solution.py:69
  54.3 3.6 %collective-permute-done.10.refs_2_ = bf16[4,128,128]{2,1,0:T(8,128)(2,1)S(1)} collective-permute-done((bf16[4,128,128]{2,1,0:T(8,128)(2,1)S(1)}, bf16[4,128,128]{2,1,0:T(8,128)(2,1)S(1)}, u32[]{:S(2)}, u32[]{:S(2)}) %collective-permute-start.10) | collective-permute-done | bytes 131104 | tf_op jit(solution)/shard_map/ppermute | solution.py:69
  57.9 0.0 collective-permute-done.11.refs_3_
  57.9 2.6 %collective-permute-start.14 = (bf16[4,128,128]{2,1,0:T(8,128)(2,1)S(1)}, bf16[4,128,128]{2,1,0:T(8,128)(2,1)S(1)}, u32[]{:S(2)}, u32[]{:S(2)}) collective-permute-start(bf16[4,128,128]{2,1,0:T(8,128)(2,1)S(1)} %get-tuple-element.69), channel_id=1, source_target_pairs={{0,8},{8,0},{16,24},{24,16},{1,9},{9,1},{17,25},{25,17},{2,10},{10... | collective-permute-start | bytes 393224 | tf_op jit(solution)/shard_map/ppermute | solution.py:64
  60.6 0.1 collective-permute-start.12
  60.7 2.3 %collective-permute-start.13 = (bf16[4,128,128]{2,1,0:T(8,128)(2,1)S(1)}, bf16[4,128,128]{2,1,0:T(8,128)(2,1)S(1)}, u32[]{:S(2)}, u32[]{:S(2)}) collective-permute-start(bf16[4,128,128]{2,1,0:T(8,128)(2,1)S(1)} %get-tuple-element.67), channel_id=1, source_target_pairs={{0,24},{8,16},{16,8},{24,0},{1,25},{9,17},{17,9},{25,1},{2,26},{10... | collective-permute-start | bytes 393224 | tf_op jit(solution)/shard_map/ppermute | solution.py:64
  63.0 3.5 %lists.1 = (s32[16,42]{1,0:T(8,128)S(1)}, s32[16]{0:T(128)S(1)}) custom-call(s32[3]{0:T(128)S(1)} %pad_add_fusion.ids, s32[8]{0:T(128)S(1)} %copy-done.4, s32[4,4,8]{2,1,0:T(4,128)S(1)} %bitcast.4), custom_call_target="tpu_custom_call" | custom-call | bytes 10500000 | tf_op jit(solution)/shard_map/lists/pallas_call | solution.py:242
  66.5 5.9 %totals.1 = (f32[32,128]{1,0:T(8,128)S(1)}, bf16[32,128,128]{2,1,0:T(8,128)(2,1)S(1)}) custom-call(s32[16,42]{1,0:T(8,128)S(1)} %get-tuple-element.45.by_key, s32[16]{0:T(128)S(1)} %get-tuple-element.46.n_key, bf16[16,128,128]{2,1,0:T(8,128)(2,1)S(1)} %get-tuple-element.47.k_ref, bf16[16,128,128]{2,1,0:T(8,128)(2,1)S(1)} %get-tuple-element.48.refs_0_, ...), custom_call_target="tpu_custom_call" | custom-call | bytes 21000000 | tf_op jit(solution)/shard_map/totals/pallas_call | solution.py:330
  72.4 0.1 collective-permute-start.8
  72.5 0.0 collective-permute-done.7.refs_1_
  72.5 1.2 %collective-permute-done.8.refs_3_ = f32[32,128]{1,0:T(8,128)S(1)} collective-permute-done((f32[32,128]{1,0:T(8,128)S(1)}, f32[32,128]{1,0:T(8,128)S(1)}, u32[]{:S(2)}, u32[]{:S(2)}) %collective-permute-start.8) | collective-permute-done | bytes 16416 | tf_op jit(solution)/shard_map/ppermute | solution.py:69
  73.6 0.1 query_rows.1
  73.7 0.0 collective-permute-done.14.refs_1_
  73.7 7.9 %shard_map.97 = (bf16[2,2,128,128]{3,2,1,0:T(8,128)(2,1)S(1)}, bf16[2,2,128,128]{3,2,1,0:T(8,128)(2,1)S(1)}, bf16[2,2,128,128]{3,2,1,0:T(8,128)(2,1)S(1)}, bf16[...) custom-call(s32[16,42]{1,0:T(8,128)S(1)} %get-tuple-element.45.by_key, s32[16]{0:T(128)S(1)} %get-tuple-element.46.n_key, ...), custom_call_target="tpu_custom_call" | custom-call | bytes 24500000 | tf_op jit(solution)/shard_map/pallas_call | solution.py:480
  81.6 0.0 collective-permute-done.12.refs_0_
  81.6 0.0 collective-permute-done.13.refs_1_
  81.6 8.3 %shard_map.98 = (bf16[2,2,128,128]{3,2,1,0:T(8,128)(2,1)S(1)}, bf16[2,2,128,128]{3,2,1,0:T(8,128)(2,1)S(1)}, bf16[2,2,128,128]{3,2,1,0:T(8,128)(2,1)S(1)}, bf16[...) custom-call(s32[16,42]{1,0:T(8,128)S(1)} %get-tuple-element.45.by_key, ...), custom_call_target="tpu_custom_call" | custom-call | bytes 24500000 | tf_op jit(solution)/shard_map/pallas_call | solution.py:480
  89.9 0.2 collective-permute-start.15
  90.2 1.2 %collective-permute-start.22 = (bf16[2,2,128,128]{3,2,1,0:T(8,128)(2,1)S(1)}, bf16[2,2,128,128]{3,2,1,0:T(8,128)(2,1)S(1)}, u32[]{:S(2)}, u32[]{:S(2)}) collective-permute-start(bf16[2,2,128,128]{3,2,1,0:T(8,128)(2,1)S(1)} %get-tuple-element.82), channel_id=1, source_target_pairs={{0,2},{1,3},{2,0},{3,1},{4,6},{5,7},{6,4},{7,5},{8,10},{9,11},{10,... | collective-permute-start | bytes 393224 | tf_op jit(solution)/shard_map/ppermute | solution.py:69
  91.3 0.8 collective-permute-start.23
  92.2 1.5 %collective-permute-start.24 = (bf16[2,2,128,128]{3,2,1,0:T(8,128)(2,1)S(1)}, bf16[2,2,128,128]{3,2,1,0:T(8,128)(2,1)S(1)}, u32[]{:S(2)}, u32[]{:S(2)}) collective-permute-start(bf16[2,2,128,128]{3,2,1,0:T(8,128)(2,1)S(1)} %get-tuple-element.84), channel_id=1, source_target_pairs={{0,6},{1,7},{2,4},{3,5},{4,2},{5,3},{6,0},{7,1},{8,14},{9,15},{10,... | collective-permute-start | bytes 393224 | tf_op jit(solution)/shard_map/ppermute | solution.py:69
  93.7 1.2 %collective-permute-start.19 = (bf16[2,2,128,128]{3,2,1,0:T(8,128)(2,1)S(1)}, bf16[2,2,128,128]{3,2,1,0:T(8,128)(2,1)S(1)}, u32[]{:S(2)}, u32[]{:S(2)}) collective-permute-start(bf16[2,2,128,128]{3,2,1,0:T(8,128)(2,1)S(1)} %get-tuple-element.78), channel_id=1, source_target_pairs={{0,2},{1,3},{2,0},{3,1},{4,6},{5,7},{6,4},{7,5},{8,10},{9,11},{10,... | collective-permute-start | bytes 393224 | tf_op jit(solution)/shard_map/ppermute | solution.py:69
  94.8 0.0 collective-permute-done.15.refs_1_
  94.8 0.8 collective-permute-start.20
  95.7 0.2 pack.1
  95.9 0.7 collective-permute-done.22.refs_5_
  96.5 1.3 %collective-permute-start.21 = (bf16[2,2,128,128]{3,2,1,0:T(8,128)(2,1)S(1)}, bf16[2,2,128,128]{3,2,1,0:T(8,128)(2,1)S(1)}, u32[]{:S(2)}, u32[]{:S(2)}) collective-permute-start(bf16[2,2,128,128]{3,2,1,0:T(8,128)(2,1)S(1)} %get-tuple-element.80), channel_id=1, source_target_pairs={{0,6},{1,7},{2,4},{3,5},{4,2},{5,3},{6,0},{7,1},{8,14},{9,15},{10,... | collective-permute-start | bytes 393224 | tf_op jit(solution)/shard_map/ppermute | solution.py:69
  97.8 1.9 %collective-permute-done.23.refs_6_ = bf16[2,2,128,128]{3,2,1,0:T(8,128)(2,1)S(1)} collective-permute-done((bf16[2,2,128,128]{3,2,1,0:T(8,128)(2,1)S(1)}, bf16[2,2,128,128]{3,2,1,0:T(8,128)(2,1)S(1)}, u32[]{:S(2)}, u32[]{:S(2)}) %collective-permute-start.23) | collective-permute-done | bytes 131104 | tf_op jit(solution)/shard_map/ppermute | solution.py:69
  99.7 1.1 collective-permute-start.16
  100.8 0.0 collective-permute-done.24.refs_7_
  100.8 1.8 %collective-permute-start.17 = (bf16[1,4,128,128]{3,2,1,0:T(8,128)(2,1)S(1)}, bf16[1,4,128,128]{3,2,1,0:T(8,128)(2,1)S(1)}, u32[]{:S(2)}, u32[]{:S(2)}) collective-permute-start(bf16[1,4,128,128]{3,2,1,0:T(8,128)(2,1)S(1)} %get-tuple-element.75), channel_id=1, source_target_pairs={{0,4},{1,5},{2,6},{3,7},{4,0},{5,1},{6,2},{7,3},{8,12},{9,13},{10,... | collective-permute-start | bytes 393224 | tf_op jit(solution)/shard_map/ppermute | solution.py:69
  102.6 1.2 %collective-permute-start.18 = (bf16[1,4,128,128]{3,2,1,0:T(8,128)(2,1)S(1)}, bf16[1,4,128,128]{3,2,1,0:T(8,128)(2,1)S(1)}, u32[]{:S(2)}, u32[]{:S(2)}) collective-permute-start(bf16[1,4,128,128]{3,2,1,0:T(8,128)(2,1)S(1)} %get-tuple-element.76), channel_id=1, source_target_pairs={{0,6},{1,7},{2,4},{3,5},{4,2},{5,3},{6,0},{7,1},{8,14},{9,15},{10,... | collective-permute-start | bytes 393224 | tf_op jit(solution)/shard_map/ppermute | solution.py:69
  103.8 1.5 %collective-permute-done.20.refs_2_ = bf16[2,2,128,128]{3,2,1,0:T(8,128)(2,1)S(1)} collective-permute-done((bf16[2,2,128,128]{3,2,1,0:T(8,128)(2,1)S(1)}, bf16[2,2,128,128]{3,2,1,0:T(8,128)(2,1)S(1)}, u32[]{:S(2)}, u32[]{:S(2)}) %collective-permute-start.20) | collective-permute-done | bytes 131104 | tf_op jit(solution)/shard_map/ppermute | solution.py:69
  105.3 0.7 collective-permute-done.21.refs_3_
  106.0 1.7 %shard_map.100 = (bf16[512,512]{1,0:T(8,128)(2,1)}, bf16[512,512]{1,0:T(8,128)(2,1)}) custom-call(s32[3]{0:T(128)S(1)} %pad_add_fusion.ids, bf16[2,2,128,128]{3,2,1,0:T(8,128)(2,1)S(1)} %get-tuple-element.77.refs_0_, bf16[2,2,128,128]{3,2,1,0:T(8,128)(2,1)S(1)} %collective-permute-done.19.refs_1_, ...), custom_call_target="tpu_custom_call" | custom-call | bytes 5250000 | tf_op jit(solution)/shard_map/pallas_call | solution.py:529
  107.7 0.2 collective-permute-done.16.refs_1_
  107.9 0.7 collective-permute-done.17.refs_2_
  108.6 2.4 %collective-permute-done.18.refs_3_ = bf16[1,4,128,128]{3,2,1,0:T(8,128)(2,1)S(1)} collective-permute-done((bf16[1,4,128,128]{3,2,1,0:T(8,128)(2,1)S(1)}, bf16[1,4,128,128]{3,2,1,0:T(8,128)(2,1)S(1)}, u32[]{:S(2)}, u32[]{:S(2)}) %collective-permute-start.18) | collective-permute-done | bytes 131104 | tf_op jit(solution)/shard_map/ppermute | solution.py:69
  110.9 1.4 %shard_map.99 = bf16[512,512]{1,0:T(8,128)(2,1)} custom-call(s32[3]{0:T(128)S(1)} %pad_add_fusion.ids, bf16[1,4,128,128]{3,2,1,0:T(8,128)(2,1)S(1)} %get-tuple-element.73.refs_0_, bf16[1,4,128,128]{3,2,1,0:T(8,128)(2,1)S(1)} %collective-permute-done.16.refs_1_, bf16[1,4,128,128]{3,2,1,0:T(8,128)(2,1)S(1)} %collective-permute-done.17.refs_2_, ...), custom_call_target="tpu_custom_call" | custom-call | bytes 5250000 | tf_op jit(solution)/shard_map/pallas_call | solution.py:529
  (13 shorter events, 0.1 us)
Async XLA Ops:
  0.6 11.0 %copy-start = (bf16[128,2048]{1,0:T(8,128)(2,1)S(1)}, bf16[128,2048]{1,0:T(8,128)(2,1)}, u32[]{:S(2)}) copy-start(bf16[128,2048]{1,0:T(8,128)(2,1)} %g_ref.1) | copy-start | bytes 1572868
  0.6 11.0 %copy-start.1 = (bf16[128,2048]{1,0:T(8,128)(2,1)S(1)}, bf16[128,2048]{1,0:T(8,128)(2,1)}, u32[]{:S(2)}) copy-start(bf16[128,2048]{1,0:T(8,128)(2,1)} %o_ref.1) | copy-start | bytes 1572868
  0.7 11.0 %copy-start.2 = (bf16[128,2048]{1,0:T(8,128)(2,1)S(1)}, bf16[128,2048]{1,0:T(8,128)(2,1)}, u32[]{:S(2)}) copy-start(bf16[128,2048]{1,0:T(8,128)(2,1)} %v_ref.1) | copy-start | bytes 1572868
  3.2 44.1 %all-to-all-start = ((bf16[16,256,128]{2,1,0:T(8,128)(2,1)}), bf16[16,256,128]{2,1,0:T(8,128)(2,1)S(1)}, u32[]{:S(2)}, u32[]{:S(2)}) async-start(bf16[16,256,128]{2,1,0:T(8,128)(2,1)} %prep.1), calls=%async_computation | async-start | bytes 2097152 | tf_op jit(solution)/shard_map/all_to_all | solution.py:563
  11.6 51.4 %copy-start.3 = (s32[8,4,4]{0,2,1:T(4,128)S(1)}, s32[8,4,4]{0,2,1:T(4,128)}, u32[]{:S(2)}) copy-start(s32[8,4,4]{0,2,1:T(4,128)} %param.13) | copy-start | bytes 1540
  11.6 51.4 %copy-start.4 = (s32[8]{0:T(128)S(1)}, s32[8]{0:T(128)}, u32[]{:S(2)}) copy-start(s32[8]{0:T(128)} %order.1) | copy-start | bytes 100
  13.7 12.8 %collective-permute-start.1 = (bf16[4,136,128]{2,1,0:T(8,128)(2,1)S(1)}, bf16[4,136,128]{2,1,0:T(8,128)(2,1)S(1)}, u32[]{:S(2)}, u32[]{:S(2)}) collective-permute-start(bf16[4,136,128]{2,1,0:T(8,128)(2,1)S(1)} %get-tuple-element.51), channel_id=1, source_target_pairs={{0,2},{1,3},{2,0},{3,1},{4,6},{5,7},{6,4},{7,5},{8,10},{9,11},{10,... | collective-permute-start | bytes 417800 | tf_op jit(solution)/shard_map/ppermute | solution.py:69
  15.7 12.3 %collective-permute-start.2 = (bf16[4,136,128]{2,1,0:T(8,128)(2,1)S(1)}, bf16[4,136,128]{2,1,0:T(8,128)(2,1)S(1)}, u32[]{:S(2)}, u32[]{:S(2)}) collective-permute-start(bf16[4,136,128]{2,1,0:T(8,128)(2,1)S(1)} %get-tuple-element.52), channel_id=1, source_target_pairs={{0,4},{1,5},{2,6},{3,7},{4,0},{5,1},{6,2},{7,3},{8,12},{9,13},{10,... | collective-permute-start | bytes 417800 | tf_op jit(solution)/shard_map/ppermute | solution.py:69
  17.2 13.3 %collective-permute-start.3 = (bf16[4,136,128]{2,1,0:T(8,128)(2,1)S(1)}, bf16[4,136,128]{2,1,0:T(8,128)(2,1)S(1)}, u32[]{:S(2)}, u32[]{:S(2)}) collective-permute-start(bf16[4,136,128]{2,1,0:T(8,128)(2,1)S(1)} %get-tuple-element.53), channel_id=1, source_target_pairs={{0,6},{1,7},{2,4},{3,5},{4,2},{5,3},{6,0},{7,1},{8,14},{9,15},{10,... | collective-permute-start | bytes 417800 | tf_op jit(solution)/shard_map/ppermute | solution.py:69
  30.5 5.9 %collective-permute-start.4 = (bf16[4,136,128]{2,1,0:T(8,128)(2,1)S(1)}, bf16[4,136,128]{2,1,0:T(8,128)(2,1)S(1)}, u32[]{:S(2)}, u32[]{:S(2)}) collective-permute-start(bf16[4,136,128]{2,1,0:T(8,128)(2,1)S(1)} %get-tuple-element.55), channel_id=1, source_target_pairs={{0,8},{8,0},{16,24},{24,16},{1,9},{9,1},{17,25},{25,17},{2,10},{10... | collective-permute-start | bytes 417800 | tf_op jit(solution)/shard_map/ppermute | solution.py:64
  30.6 16.5 %collective-permute-start.5 = (bf16[4,136,128]{2,1,0:T(8,128)(2,1)S(1)}, bf16[4,136,128]{2,1,0:T(8,128)(2,1)S(1)}, u32[]{:S(2)}, u32[]{:S(2)}) collective-permute-start(bf16[4,136,128]{2,1,0:T(8,128)(2,1)S(1)} %get-tuple-element.56), channel_id=1, source_target_pairs={{0,16},{8,24},{16,0},{24,8},{1,17},{9,25},{17,1},{25,9},{2,18},{10... | collective-permute-start | bytes 417800 | tf_op jit(solution)/shard_map/ppermute | solution.py:64
  35.8 11.3 %collective-permute-start.6 = (bf16[4,136,128]{2,1,0:T(8,128)(2,1)S(1)}, bf16[4,136,128]{2,1,0:T(8,128)(2,1)S(1)}, u32[]{:S(2)}, u32[]{:S(2)}) collective-permute-start(bf16[4,136,128]{2,1,0:T(8,128)(2,1)S(1)} %get-tuple-element.57), channel_id=1, source_target_pairs={{0,24},{8,16},{16,8},{24,0},{1,25},{9,17},{17,9},{25,1},{2,26},{10... | collective-permute-start | bytes 417800 | tf_op jit(solution)/shard_map/ppermute | solution.py:64
  47.2 25.3 %collective-permute-start.7 = (bf16[16,136,128]{2,1,0:T(8,128)(2,1)S(1)}, bf16[16,136,128]{2,1,0:T(8,128)(2,1)S(1)}, u32[]{:S(2)}, u32[]{:S(2)}) collective-permute-start(bf16[16,136,128]{2,1,0:T(8,128)(2,1)S(1)} %shard_map.95.refs_0_), channel_id=1, source_target_pairs={{0,1},{1,0},{2,3},{3,2},{4,5},{5,4},{6,7},{7,6},{8,9},{9,8},{10,11... | collective-permute-start | bytes 1671176 | tf_op jit(solution)/shard_map/ppermute | solution.py:69
  47.9 18.6 %collective-permute-start = (bf16[16,128,128]{2,1,0:T(8,128)(2,1)S(1)}, bf16[16,128,128]{2,1,0:T(8,128)(2,1)S(1)}, u32[]{:S(2)}, u32[]{:S(2)}) collective-permute-start(bf16[16,128,128]{2,1,0:T(8,128)(2,1)S(1)} %get-tuple-element.48.refs_0_), channel_id=1, source_target_pairs={{0,1},{1,0},{2,3},{3,2},{4,5},{5,4},{6,7},{7,6},{8,9},{9,8},{10,11... | collective-permute-start | bytes 1572872 | tf_op jit(solution)/shard_map/ppermute | solution.py:69
  48.4 5.9 %collective-permute-start.9 = (bf16[4,128,128]{2,1,0:T(8,128)(2,1)S(1)}, bf16[4,128,128]{2,1,0:T(8,128)(2,1)S(1)}, u32[]{:S(2)}, u32[]{:S(2)}) collective-permute-start(bf16[4,128,128]{2,1,0:T(8,128)(2,1)S(1)} %get-tuple-element.63), channel_id=1, source_target_pairs={{0,2},{1,3},{2,0},{3,1},{4,6},{5,7},{6,4},{7,5},{8,10},{9,11},{10,... | collective-permute-start | bytes 393224 | tf_op jit(solution)/shard_map/ppermute | solution.py:69
  49.9 8.0 %collective-permute-start.10 = (bf16[4,128,128]{2,1,0:T(8,128)(2,1)S(1)}, bf16[4,128,128]{2,1,0:T(8,128)(2,1)S(1)}, u32[]{:S(2)}, u32[]{:S(2)}) collective-permute-start(bf16[4,128,128]{2,1,0:T(8,128)(2,1)S(1)} %get-tuple-element.64), channel_id=1, source_target_pairs={{0,4},{1,5},{2,6},{3,7},{4,0},{5,1},{6,2},{7,3},{8,12},{9,13},{10,... | collective-permute-start | bytes 393224 | tf_op jit(solution)/shard_map/ppermute | solution.py:69
  51.4 6.5 %collective-permute-start.11 = (bf16[4,128,128]{2,1,0:T(8,128)(2,1)S(1)}, bf16[4,128,128]{2,1,0:T(8,128)(2,1)S(1)}, u32[]{:S(2)}, u32[]{:S(2)}) collective-permute-start(bf16[4,128,128]{2,1,0:T(8,128)(2,1)S(1)} %get-tuple-element.65), channel_id=1, source_target_pairs={{0,6},{1,7},{2,4},{3,5},{4,2},{5,3},{6,0},{7,1},{8,14},{9,15},{10,... | collective-permute-start | bytes 393224 | tf_op jit(solution)/shard_map/ppermute | solution.py:69
  57.9 15.8 %collective-permute-start.14 = (bf16[4,128,128]{2,1,0:T(8,128)(2,1)S(1)}, bf16[4,128,128]{2,1,0:T(8,128)(2,1)S(1)}, u32[]{:S(2)}, u32[]{:S(2)}) collective-permute-start(bf16[4,128,128]{2,1,0:T(8,128)(2,1)S(1)} %get-tuple-element.69), channel_id=1, source_target_pairs={{0,8},{8,0},{16,24},{24,16},{1,9},{9,1},{17,25},{25,17},{2,10},{10... | collective-permute-start | bytes 393224 | tf_op jit(solution)/shard_map/ppermute | solution.py:64
  60.6 21.0 %collective-permute-start.12 = (bf16[4,128,128]{2,1,0:T(8,128)(2,1)S(1)}, bf16[4,128,128]{2,1,0:T(8,128)(2,1)S(1)}, u32[]{:S(2)}, u32[]{:S(2)}) collective-permute-start(bf16[4,128,128]{2,1,0:T(8,128)(2,1)S(1)} %get-tuple-element.66), channel_id=1, source_target_pairs={{0,16},{8,24},{16,0},{24,8},{1,17},{9,25},{17,1},{25,9},{2,18},{10... | collective-permute-start | bytes 393224 | tf_op jit(solution)/shard_map/ppermute | solution.py:64
  60.7 20.9 %collective-permute-start.13 = (bf16[4,128,128]{2,1,0:T(8,128)(2,1)S(1)}, bf16[4,128,128]{2,1,0:T(8,128)(2,1)S(1)}, u32[]{:S(2)}, u32[]{:S(2)}) collective-permute-start(bf16[4,128,128]{2,1,0:T(8,128)(2,1)S(1)} %get-tuple-element.67), channel_id=1, source_target_pairs={{0,24},{8,16},{16,8},{24,0},{1,25},{9,17},{17,9},{25,1},{2,26},{10... | collective-permute-start | bytes 393224 | tf_op jit(solution)/shard_map/ppermute | solution.py:64
  72.4 1.2 %collective-permute-start.8 = (f32[32,128]{1,0:T(8,128)S(1)}, f32[32,128]{1,0:T(8,128)S(1)}, u32[]{:S(2)}, u32[]{:S(2)}) collective-permute-start(f32[32,128]{1,0:T(8,128)S(1)} %get-tuple-element.58.refs_2_), channel_id=1, source_target_pairs={{0,1},{1,0},{2,3},{3,2},{4,5},{5,4},{6,7},{7,6},{8,9},{9,8},{10,11... | collective-permute-start | bytes 49160 | tf_op jit(solution)/shard_map/ppermute | solution.py:69
  89.9 4.9 %collective-permute-start.15 = (f32[16,128,128]{2,1,0:T(8,128)S(1)}, f32[16,128,128]{2,1,0:T(8,128)S(1)}, u32[]{:S(2)}, u32[]{:S(2)}) collective-permute-start(f32[16,128,128]{2,1,0:T(8,128)S(1)} %get-tuple-element.72), channel_id=1, source_target_pairs={{0,1},{1,0},{2,3},{3,2},{4,5},{5,4},{6,7},{7,6},{8,9},{9,8},{10,11... | collective-permute-start | bytes 3145736 | tf_op jit(solution)/shard_map/ppermute | solution.py:69
  90.2 6.4 %collective-permute-start.22 = (bf16[2,2,128,128]{3,2,1,0:T(8,128)(2,1)S(1)}, bf16[2,2,128,128]{3,2,1,0:T(8,128)(2,1)S(1)}, u32[]{:S(2)}, u32[]{:S(2)}) collective-permute-start(bf16[2,2,128,128]{3,2,1,0:T(8,128)(2,1)S(1)} %get-tuple-element.82), channel_id=1, source_target_pairs={{0,2},{1,3},{2,0},{3,1},{4,6},{5,7},{6,4},{7,5},{8,10},{9,11},{10,... | collective-permute-start | bytes 393224 | tf_op jit(solution)/shard_map/ppermute | solution.py:69
  91.3 8.4 %collective-permute-start.23 = (bf16[2,2,128,128]{3,2,1,0:T(8,128)(2,1)S(1)}, bf16[2,2,128,128]{3,2,1,0:T(8,128)(2,1)S(1)}, u32[]{:S(2)}, u32[]{:S(2)}) collective-permute-start(bf16[2,2,128,128]{3,2,1,0:T(8,128)(2,1)S(1)} %get-tuple-element.83), channel_id=1, source_target_pairs={{0,4},{1,5},{2,6},{3,7},{4,0},{5,1},{6,2},{7,3},{8,12},{9,13},{10,... | collective-permute-start | bytes 393224 | tf_op jit(solution)/shard_map/ppermute | solution.py:69
  92.2 8.6 %collective-permute-start.24 = (bf16[2,2,128,128]{3,2,1,0:T(8,128)(2,1)S(1)}, bf16[2,2,128,128]{3,2,1,0:T(8,128)(2,1)S(1)}, u32[]{:S(2)}, u32[]{:S(2)}) collective-permute-start(bf16[2,2,128,128]{3,2,1,0:T(8,128)(2,1)S(1)} %get-tuple-element.84), channel_id=1, source_target_pairs={{0,6},{1,7},{2,4},{3,5},{4,2},{5,3},{6,0},{7,1},{8,14},{9,15},{10,... | collective-permute-start | bytes 393224 | tf_op jit(solution)/shard_map/ppermute | solution.py:69
  93.7 8.9 %collective-permute-start.19 = (bf16[2,2,128,128]{3,2,1,0:T(8,128)(2,1)S(1)}, bf16[2,2,128,128]{3,2,1,0:T(8,128)(2,1)S(1)}, u32[]{:S(2)}, u32[]{:S(2)}) collective-permute-start(bf16[2,2,128,128]{3,2,1,0:T(8,128)(2,1)S(1)} %get-tuple-element.78), channel_id=1, source_target_pairs={{0,2},{1,3},{2,0},{3,1},{4,6},{5,7},{6,4},{7,5},{8,10},{9,11},{10,... | collective-permute-start | bytes 393224 | tf_op jit(solution)/shard_map/ppermute | solution.py:69
  94.8 10.5 %collective-permute-start.20 = (bf16[2,2,128,128]{3,2,1,0:T(8,128)(2,1)S(1)}, bf16[2,2,128,128]{3,2,1,0:T(8,128)(2,1)S(1)}, u32[]{:S(2)}, u32[]{:S(2)}) collective-permute-start(bf16[2,2,128,128]{3,2,1,0:T(8,128)(2,1)S(1)} %get-tuple-element.79), channel_id=1, source_target_pairs={{0,4},{1,5},{2,6},{3,7},{4,0},{5,1},{6,2},{7,3},{8,12},{9,13},{10,... | collective-permute-start | bytes 393224 | tf_op jit(solution)/shard_map/ppermute | solution.py:69
  96.5 9.4 %collective-permute-start.21 = (bf16[2,2,128,128]{3,2,1,0:T(8,128)(2,1)S(1)}, bf16[2,2,128,128]{3,2,1,0:T(8,128)(2,1)S(1)}, u32[]{:S(2)}, u32[]{:S(2)}) collective-permute-start(bf16[2,2,128,128]{3,2,1,0:T(8,128)(2,1)S(1)} %get-tuple-element.80), channel_id=1, source_target_pairs={{0,6},{1,7},{2,4},{3,5},{4,2},{5,3},{6,0},{7,1},{8,14},{9,15},{10,... | collective-permute-start | bytes 393224 | tf_op jit(solution)/shard_map/ppermute | solution.py:69
  99.7 8.1 %collective-permute-start.16 = (bf16[1,4,128,128]{3,2,1,0:T(8,128)(2,1)S(1)}, bf16[1,4,128,128]{3,2,1,0:T(8,128)(2,1)S(1)}, u32[]{:S(2)}, u32[]{:S(2)}) collective-permute-start(bf16[1,4,128,128]{3,2,1,0:T(8,128)(2,1)S(1)} %get-tuple-element.74), channel_id=1, source_target_pairs={{0,2},{1,3},{2,0},{3,1},{4,6},{5,7},{6,4},{7,5},{8,10},{9,11},{10,... | collective-permute-start | bytes 393224 | tf_op jit(solution)/shard_map/ppermute | solution.py:69
  100.8 7.8 %collective-permute-start.17 = (bf16[1,4,128,128]{3,2,1,0:T(8,128)(2,1)S(1)}, bf16[1,4,128,128]{3,2,1,0:T(8,128)(2,1)S(1)}, u32[]{:S(2)}, u32[]{:S(2)}) collective-permute-start(bf16[1,4,128,128]{3,2,1,0:T(8,128)(2,1)S(1)} %get-tuple-element.75), channel_id=1, source_target_pairs={{0,4},{1,5},{2,6},{3,7},{4,0},{5,1},{6,2},{7,3},{8,12},{9,13},{10,... | collective-permute-start | bytes 393224 | tf_op jit(solution)/shard_map/ppermute | solution.py:69
  102.6 8.3 %collective-permute-start.18 = (bf16[1,4,128,128]{3,2,1,0:T(8,128)(2,1)S(1)}, bf16[1,4,128,128]{3,2,1,0:T(8,128)(2,1)S(1)}, u32[]{:S(2)}, u32[]{:S(2)}) collective-permute-start(bf16[1,4,128,128]{3,2,1,0:T(8,128)(2,1)S(1)} %get-tuple-element.76), channel_id=1, source_target_pairs={{0,6},{1,7},{2,4},{3,5},{4,2},{5,3},{6,0},{7,1},{8,14},{9,15},{10,... | collective-permute-start | bytes 393224 | tf_op jit(solution)/shard_map/ppermute | solution.py:69

commit v5 on v4

--- a/solution.py
+++ b/solution.py
@@ -289,8 +289,8 @@
 
     lax.fori_loop(0, na, near, 0)
 
-    def local(j, start):
-        chosen = picks(by_key, j, n_key[j], start, WIDE_GROUP)
+    def local(j, start, size):
+        chosen = picks(by_key, j, n_key[j], start, size)
         places = [pl.ds(jnp.where(ok, i, total), 1) for i, ok in chosen]
         q = jnp.concatenate([q_ref[i] for i, _ in chosen], axis=0)
         scores = scale * dot(k_ref[j], q, NT)
@@ -308,15 +308,22 @@
             sums[place, :] = new_mass[:, u * rows : (u + 1) * rows]
 
     def away(m, carry):
-        for found in [local(m * TOGETHER + u, 0) for u in range(TOGETHER)]:
-            merge(*found)
+        blocks = [m * TOGETHER + u for u in range(TOGETHER)]
+        most = functools.reduce(jnp.maximum, [n_key[j] for j in blocks])
+
+        def together(size):
+            for found in [local(j, 0, size) for j in blocks]:
+                merge(*found)
+
+        pl.when((most > 0) & (most <= KEY_GROUP))(lambda: together(KEY_GROUP))
+        pl.when(most > KEY_GROUP)(lambda: together(WIDE_GROUP))
         return carry
 
     lax.fori_loop(0, own // TOGETHER, away, 0)
 
     def rest(j, carry):
         def group(step, carry):
-            merge(*local(j, step * WIDE_GROUP))
+            merge(*local(j, step * WIDE_GROUP, WIDE_GROUP))
             return carry
 
         return lax.fori_loop(1, steps(n_key[j], WIDE_GROUP), group, carry)
@@ -442,8 +449,10 @@
             for x, found in [(x, terms(s, x, s * nz + r, 0, size)) for x, r in enumerate(span)]:
                 add(s, x, found)
 
-        pl.when((most > 0) & (most <= KEY_GROUP))(lambda: together(KEY_GROUP))
-        pl.when(most > KEY_GROUP)(lambda: together(WIDE_GROUP))
+        pl.when((most > 0) & (most < KEY_GROUP))(lambda: together(KEY_GROUP - 1))
+        pl.when(most == KEY_GROUP)(lambda: together(KEY_GROUP))
+        pl.when(most == KEY_GROUP + 1)(lambda: together(KEY_GROUP + 1))
+        pl.when(most > KEY_GROUP + 1)(lambda: together(WIDE_GROUP))
         for x, r in enumerate(span):
             left = jnp.maximum(n_key[s * nz + r] - WIDE_GROUP, 0)
 

time: 113 us -> 113 us (level)
  transfers between devices with their start and end apart: 26 -> 26, of which waited for: 15 -> 15; matrix products, arithmetic and copies ran while one was open for 0% -> 0% of each run, Pallas kernels for 20% -> 19%
where the time goes in v5:
time: 113 us; the launch traced here: 112 us
  waiting for transfers between devices  39.7 us (35%)
  starting transfers between devices  37.6 us (33%)
  Pallas kernels  34.2 us (30%)
    ppermute x19, waiting for transfers between devices, over_frame(): return lax.ppermute(value, 'frame', [(i, i ^ step) for i in range(count)])  28.3 us
    ppermute x19, starting transfers between devices, over_frame(): return lax.ppermute(value, 'frame', [(i, i ^ step) for i in range(count)])  18.9 us
    pallas_call x2, Pallas kernels, grads(): pl.pallas_call(functools.partial(grads_kernel, plan, span, first, last),...  16.3 us
    ppermute x6, waiting for transfers between devices, over_head(): return lax.ppermute(value, 'head', [(i, i ^ step) for i in range(count)])  11.3 us
    ppermute x6, starting transfers between devices, over_head(): return lax.ppermute(value, 'head', [(i, i ^ step) for i in range(count)])  10.3 us
    all_to_all x1, starting transfers between devices, local(): lax.all_to_all(prep(plan, queries, key_states), ('frame', 'head'), 0, 0,...  8.34 us
    pallas_call x1, Pallas kernels, totals(): pl.pallas_call(functools.partial(totals_kernel, plan), out_shape=[sds((pl...  5.66 us
    pallas_call x1, Pallas kernels, lists(): pl.pallas_call(functools.partial(lists_kernel, plan), out_shape=[sds((own...  3.47 us
  transfers between devices with their start and end apart: 26, of which 15 were waited for; matrix products, arithmetic and copies ran while one was open for 0% of the time, Pallas kernels for 19%

profile of v5, /device:TPU:0, one launch (start us, length us, event | category | flops | bytes accessed | tf_op | source)
XLA Modules:
  0.0 112.3 jit_solution(10161236766581651685)
XLA Ops:
  0.7 2.5 %prep.1 = bf16[16,256,128]{2,1,0:T(8,128)(2,1)} custom-call(bf16[128,2048]{1,0:T(8,128)(2,1)} %q_ref.1, bf16[128,2048]{1,0:T(8,128)(2,1)} %k_ref.1), custom_call_target="tpu_custom_call" | custom-call | bytes 5250000 | tf_op jit(solution)/shard_map/prep/pallas_call | solution.py:98
  3.2 8.3 %all-to-all-start = ((bf16[16,256,128]{2,1,0:T(8,128)(2,1)}), bf16[16,256,128]{2,1,0:T(8,128)(2,1)S(1)}, u32[]{:S(2)}, u32[]{:S(2)}) async-start(bf16[16,256,128]{2,1,0:T(8,128)(2,1)} %prep.1), calls=%async_computation | async-start | bytes 2097152 | tf_op jit(solution)/shard_map/all_to_all | solution.py:572
  11.5 0.1 pad_add_fusion.ids
  11.6 0.0 copy-start.3
  11.6 0.0 copy-start.4
  11.6 2.1 %prep_rest.1 = (bf16[4,136,128]{2,1,0:T(8,128)(2,1)S(1)}, bf16[4,136,128]{2,1,0:T(8,128)(2,1)S(1)}, bf16[4,136,128]{2,1,0:T(8,128)(2,1)S(1)}, bf16[4,136,128]{2,...) custom-call(s32[3]{0:T(128)S(1)} %pad_add_fusion.ids, ...), custom_call_target="tpu_custom_call" | custom-call | bytes 7000000 | tf_op jit(solution)/shard_map/prep_rest/pallas_call | solution.py:158
  13.7 2.0 %collective-permute-start.1 = (bf16[4,136,128]{2,1,0:T(8,128)(2,1)S(1)}, bf16[4,136,128]{2,1,0:T(8,128)(2,1)S(1)}, u32[]{:S(2)}, u32[]{:S(2)}) collective-permute-start(bf16[4,136,128]{2,1,0:T(8,128)(2,1)S(1)} %get-tuple-element.51), channel_id=1, source_target_pairs={{0,2},{1,3},{2,0},{3,1},{4,6},{5,7},{6,4},{7,5},{8,10},{9,11},{10,... | collective-permute-start | bytes 417800 | tf_op jit(solution)/shard_map/ppermute | solution.py:69
  15.7 1.5 %collective-permute-start.2 = (bf16[4,136,128]{2,1,0:T(8,128)(2,1)S(1)}, bf16[4,136,128]{2,1,0:T(8,128)(2,1)S(1)}, u32[]{:S(2)}, u32[]{:S(2)}) collective-permute-start(bf16[4,136,128]{2,1,0:T(8,128)(2,1)S(1)} %get-tuple-element.52), channel_id=1, source_target_pairs={{0,4},{1,5},{2,6},{3,7},{4,0},{5,1},{6,2},{7,3},{8,12},{9,13},{10,... | collective-permute-start | bytes 417800 | tf_op jit(solution)/shard_map/ppermute | solution.py:69
  17.2 0.1 collective-permute-start.3
  17.3 9.3 %collective-permute-done.1.refs_1_ = bf16[4,136,128]{2,1,0:T(8,128)(2,1)S(1)} collective-permute-done((bf16[4,136,128]{2,1,0:T(8,128)(2,1)S(1)}, bf16[4,136,128]{2,1,0:T(8,128)(2,1)S(1)}, u32[]{:S(2)}, u32[]{:S(2)}) %collective-permute-start.1) | collective-permute-done | bytes 139296 | tf_op jit(solution)/shard_map/ppermute | solution.py:69
  26.5 1.5 %collective-permute-done.2.refs_2_ = bf16[4,136,128]{2,1,0:T(8,128)(2,1)S(1)} collective-permute-done((bf16[4,136,128]{2,1,0:T(8,128)(2,1)S(1)}, bf16[4,136,128]{2,1,0:T(8,128)(2,1)S(1)}, u32[]{:S(2)}, u32[]{:S(2)}) %collective-permute-start.2) | collective-permute-done | bytes 139296 | tf_op jit(solution)/shard_map/ppermute | solution.py:69
  28.0 2.4 %collective-permute-done.3.refs_3_ = bf16[4,136,128]{2,1,0:T(8,128)(2,1)S(1)} collective-permute-done((bf16[4,136,128]{2,1,0:T(8,128)(2,1)S(1)}, bf16[4,136,128]{2,1,0:T(8,128)(2,1)S(1)}, u32[]{:S(2)}, u32[]{:S(2)}) %collective-permute-start.3) | collective-permute-done | bytes 139296 | tf_op jit(solution)/shard_map/ppermute | solution.py:69
  30.5 0.1 collective-permute-start.4
  30.6 5.2 %collective-permute-start.5 = (bf16[4,136,128]{2,1,0:T(8,128)(2,1)S(1)}, bf16[4,136,128]{2,1,0:T(8,128)(2,1)S(1)}, u32[]{:S(2)}, u32[]{:S(2)}) collective-permute-start(bf16[4,136,128]{2,1,0:T(8,128)(2,1)S(1)} %get-tuple-element.56), channel_id=1, source_target_pairs={{0,16},{8,24},{16,0},{24,8},{1,17},{9,25},{17,1},{25,9},{2,18},{10... | collective-permute-start | bytes 417800 | tf_op jit(solution)/shard_map/ppermute | solution.py:64
  35.8 0.0 collective-permute-start.6
  35.8 0.6 collective-permute-done.4.refs_1_
  36.4 10.7 %collective-permute-done.5.refs_2_ = bf16[4,136,128]{2,1,0:T(8,128)(2,1)S(1)} collective-permute-done((bf16[4,136,128]{2,1,0:T(8,128)(2,1)S(1)}, bf16[4,136,128]{2,1,0:T(8,128)(2,1)S(1)}, u32[]{:S(2)}, u32[]{:S(2)}) %collective-permute-start.5) | collective-permute-done | bytes 139296 | tf_op jit(solution)/shard_map/ppermute | solution.py:64
  47.1 0.0 collective-permute-done.6.refs_3_
  47.2 0.1 collective-permute-start.7
  47.2 0.0 all-to-all-done.x_ref
  47.3 0.6 part.1
  47.9 0.6 collective-permute-start
  48.4 1.5 %collective-permute-start.9 = (bf16[4,128,128]{2,1,0:T(8,128)(2,1)S(1)}, bf16[4,128,128]{2,1,0:T(8,128)(2,1)S(1)}, u32[]{:S(2)}, u32[]{:S(2)}) collective-permute-start(bf16[4,128,128]{2,1,0:T(8,128)(2,1)S(1)} %get-tuple-element.63), channel_id=1, source_target_pairs={{0,2},{1,3},{2,0},{3,1},{4,6},{5,7},{6,4},{7,5},{8,10},{9,11},{10,... | collective-permute-start | bytes 393224 | tf_op jit(solution)/shard_map/ppermute | solution.py:69
  49.9 1.5 %collective-permute-start.10 = (bf16[4,128,128]{2,1,0:T(8,128)(2,1)S(1)}, bf16[4,128,128]{2,1,0:T(8,128)(2,1)S(1)}, u32[]{:S(2)}, u32[]{:S(2)}) collective-permute-start(bf16[4,128,128]{2,1,0:T(8,128)(2,1)S(1)} %get-tuple-element.64), channel_id=1, source_target_pairs={{0,4},{1,5},{2,6},{3,7},{4,0},{5,1},{6,2},{7,3},{8,12},{9,13},{10,... | collective-permute-start | bytes 393224 | tf_op jit(solution)/shard_map/ppermute | solution.py:69
  51.4 0.6 collective-permute-start.11
  51.9 2.4 %collective-permute-done.9.refs_1_ = bf16[4,128,128]{2,1,0:T(8,128)(2,1)S(1)} collective-permute-done((bf16[4,128,128]{2,1,0:T(8,128)(2,1)S(1)}, bf16[4,128,128]{2,1,0:T(8,128)(2,1)S(1)}, u32[]{:S(2)}, u32[]{:S(2)}) %collective-permute-start.9) | collective-permute-done | bytes 131104 | tf_op jit(solution)/shard_map/ppermute | solution.py:69
  54.3 3.6 %collective-permute-done.10.refs_2_ = bf16[4,128,128]{2,1,0:T(8,128)(2,1)S(1)} collective-permute-done((bf16[4,128,128]{2,1,0:T(8,128)(2,1)S(1)}, bf16[4,128,128]{2,1,0:T(8,128)(2,1)S(1)}, u32[]{:S(2)}, u32[]{:S(2)}) %collective-permute-start.10) | collective-permute-done | bytes 131104 | tf_op jit(solution)/shard_map/ppermute | solution.py:69
  57.9 0.0 collective-permute-done.11.refs_3_
  57.9 2.6 %collective-permute-start.14 = (bf16[4,128,128]{2,1,0:T(8,128)(2,1)S(1)}, bf16[4,128,128]{2,1,0:T(8,128)(2,1)S(1)}, u32[]{:S(2)}, u32[]{:S(2)}) collective-permute-start(bf16[4,128,128]{2,1,0:T(8,128)(2,1)S(1)} %get-tuple-element.69), channel_id=1, source_target_pairs={{0,8},{8,0},{16,24},{24,16},{1,9},{9,1},{17,25},{25,17},{2,10},{10... | collective-permute-start | bytes 393224 | tf_op jit(solution)/shard_map/ppermute | solution.py:64
  60.6 0.1 collective-permute-start.12
  60.7 2.3 %collective-permute-start.13 = (bf16[4,128,128]{2,1,0:T(8,128)(2,1)S(1)}, bf16[4,128,128]{2,1,0:T(8,128)(2,1)S(1)}, u32[]{:S(2)}, u32[]{:S(2)}) collective-permute-start(bf16[4,128,128]{2,1,0:T(8,128)(2,1)S(1)} %get-tuple-element.67), channel_id=1, source_target_pairs={{0,24},{8,16},{16,8},{24,0},{1,25},{9,17},{17,9},{25,1},{2,26},{10... | collective-permute-start | bytes 393224 | tf_op jit(solution)/shard_map/ppermute | solution.py:64
  63.0 3.5 %lists.1 = (s32[16,42]{1,0:T(8,128)S(1)}, s32[16]{0:T(128)S(1)}) custom-call(s32[3]{0:T(128)S(1)} %pad_add_fusion.ids, s32[8]{0:T(128)S(1)} %copy-done.4, s32[4,4,8]{2,1,0:T(4,128)S(1)} %bitcast.4), custom_call_target="tpu_custom_call" | custom-call | bytes 10500000 | tf_op jit(solution)/shard_map/lists/pallas_call | solution.py:242
  66.5 0.0 collective-permute-done.refs_1_
  66.5 5.7 %totals.1 = (f32[32,128]{1,0:T(8,128)S(1)}, bf16[32,128,128]{2,1,0:T(8,128)(2,1)S(1)}) custom-call(s32[16,42]{1,0:T(8,128)S(1)} %get-tuple-element.45.by_key, s32[16]{0:T(128)S(1)} %get-tuple-element.46.n_key, bf16[16,128,128]{2,1,0:T(8,128)(2,1)S(1)} %get-tuple-element.47.k_ref, bf16[16,128,128]{2,1,0:T(8,128)(2,1)S(1)} %get-tuple-element.48.refs_0_, ...), custom_call_target="tpu_custom_call" | custom-call | bytes 21000000 | tf_op jit(solution)/shard_map/totals/pallas_call | solution.py:337
  72.2 0.1 collective-permute-start.8
  72.2 0.0 collective-permute-done.7.refs_1_
  72.3 1.2 %collective-permute-done.8.refs_3_ = f32[32,128]{1,0:T(8,128)S(1)} collective-permute-done((f32[32,128]{1,0:T(8,128)S(1)}, f32[32,128]{1,0:T(8,128)S(1)}, u32[]{:S(2)}, u32[]{:S(2)}) %collective-permute-start.8) | collective-permute-done | bytes 16416 | tf_op jit(solution)/shard_map/ppermute | solution.py:69
  73.4 0.1 query_rows.1
  73.5 7.9 %shard_map.97 = (bf16[2,2,128,128]{3,2,1,0:T(8,128)(2,1)S(1)}, bf16[2,2,128,128]{3,2,1,0:T(8,128)(2,1)S(1)}, bf16[2,2,128,128]{3,2,1,0:T(8,128)(2,1)S(1)}, bf16[...) custom-call(s32[16,42]{1,0:T(8,128)S(1)} %get-tuple-element.45.by_key, s32[16]{0:T(128)S(1)} %get-tuple-element.46.n_key, ...), custom_call_target="tpu_custom_call" | custom-call | bytes 24500000 | tf_op jit(solution)/shard_map/pallas_call | solution.py:489
  81.4 0.0 collective-permute-done.13.refs_1_
  81.4 8.5 %shard_map.98 = (bf16[2,2,128,128]{3,2,1,0:T(8,128)(2,1)S(1)}, bf16[2,2,128,128]{3,2,1,0:T(8,128)(2,1)S(1)}, bf16[2,2,128,128]{3,2,1,0:T(8,128)(2,1)S(1)}, bf16[...) custom-call(s32[16,42]{1,0:T(8,128)S(1)} %get-tuple-element.45.by_key, ...), custom_call_target="tpu_custom_call" | custom-call | bytes 24500000 | tf_op jit(solution)/shard_map/pallas_call | solution.py:489
  89.9 0.2 collective-permute-start.15
  90.1 1.2 %collective-permute-start.22 = (bf16[2,2,128,128]{3,2,1,0:T(8,128)(2,1)S(1)}, bf16[2,2,128,128]{3,2,1,0:T(8,128)(2,1)S(1)}, u32[]{:S(2)}, u32[]{:S(2)}) collective-permute-start(bf16[2,2,128,128]{3,2,1,0:T(8,128)(2,1)S(1)} %get-tuple-element.82), channel_id=1, source_target_pairs={{0,2},{1,3},{2,0},{3,1},{4,6},{5,7},{6,4},{7,5},{8,10},{9,11},{10,... | collective-permute-start | bytes 393224 | tf_op jit(solution)/shard_map/ppermute | solution.py:69
  91.3 0.9 collective-permute-start.23
  92.1 1.5 %collective-permute-start.24 = (bf16[2,2,128,128]{3,2,1,0:T(8,128)(2,1)S(1)}, bf16[2,2,128,128]{3,2,1,0:T(8,128)(2,1)S(1)}, u32[]{:S(2)}, u32[]{:S(2)}) collective-permute-start(bf16[2,2,128,128]{3,2,1,0:T(8,128)(2,1)S(1)} %get-tuple-element.84), channel_id=1, source_target_pairs={{0,6},{1,7},{2,4},{3,5},{4,2},{5,3},{6,0},{7,1},{8,14},{9,15},{10,... | collective-permute-start | bytes 393224 | tf_op jit(solution)/shard_map/ppermute | solution.py:69
  93.6 1.2 %collective-permute-start.19 = (bf16[2,2,128,128]{3,2,1,0:T(8,128)(2,1)S(1)}, bf16[2,2,128,128]{3,2,1,0:T(8,128)(2,1)S(1)}, u32[]{:S(2)}, u32[]{:S(2)}) collective-permute-start(bf16[2,2,128,128]{3,2,1,0:T(8,128)(2,1)S(1)} %get-tuple-element.78), channel_id=1, source_target_pairs={{0,2},{1,3},{2,0},{3,1},{4,6},{5,7},{6,4},{7,5},{8,10},{9,11},{10,... | collective-permute-start | bytes 393224 | tf_op jit(solution)/shard_map/ppermute | solution.py:69
  94.8 0.0 collective-permute-done.15.refs_1_
  94.8 0.9 collective-permute-start.20
  95.6 0.2 pack.1
  95.8 0.7 collective-permute-done.22.refs_5_
  96.5 1.3 %collective-permute-start.21 = (bf16[2,2,128,128]{3,2,1,0:T(8,128)(2,1)S(1)}, bf16[2,2,128,128]{3,2,1,0:T(8,128)(2,1)S(1)}, u32[]{:S(2)}, u32[]{:S(2)}) collective-permute-start(bf16[2,2,128,128]{3,2,1,0:T(8,128)(2,1)S(1)} %get-tuple-element.80), channel_id=1, source_target_pairs={{0,6},{1,7},{2,4},{3,5},{4,2},{5,3},{6,0},{7,1},{8,14},{9,15},{10,... | collective-permute-start | bytes 393224 | tf_op jit(solution)/shard_map/ppermute | solution.py:69
  97.8 1.9 %collective-permute-done.23.refs_6_ = bf16[2,2,128,128]{3,2,1,0:T(8,128)(2,1)S(1)} collective-permute-done((bf16[2,2,128,128]{3,2,1,0:T(8,128)(2,1)S(1)}, bf16[2,2,128,128]{3,2,1,0:T(8,128)(2,1)S(1)}, u32[]{:S(2)}, u32[]{:S(2)}) %collective-permute-start.23) | collective-permute-done | bytes 131104 | tf_op jit(solution)/shard_map/ppermute | solution.py:69
  99.6 1.1 %collective-permute-start.16 = (bf16[1,4,128,128]{3,2,1,0:T(8,128)(2,1)S(1)}, bf16[1,4,128,128]{3,2,1,0:T(8,128)(2,1)S(1)}, u32[]{:S(2)}, u32[]{:S(2)}) collective-permute-start(bf16[1,4,128,128]{3,2,1,0:T(8,128)(2,1)S(1)} %get-tuple-element.74), channel_id=1, source_target_pairs={{0,2},{1,3},{2,0},{3,1},{4,6},{5,7},{6,4},{7,5},{8,10},{9,11},{10,... | collective-permute-start | bytes 393224 | tf_op jit(solution)/shard_map/ppermute | solution.py:69
  100.8 0.0 collective-permute-done.24.refs_7_
  100.8 1.8 %collective-permute-start.17 = (bf16[1,4,128,128]{3,2,1,0:T(8,128)(2,1)S(1)}, bf16[1,4,128,128]{3,2,1,0:T(8,128)(2,1)S(1)}, u32[]{:S(2)}, u32[]{:S(2)}) collective-permute-start(bf16[1,4,128,128]{3,2,1,0:T(8,128)(2,1)S(1)} %get-tuple-element.75), channel_id=1, source_target_pairs={{0,4},{1,5},{2,6},{3,7},{4,0},{5,1},{6,2},{7,3},{8,12},{9,13},{10,... | collective-permute-start | bytes 393224 | tf_op jit(solution)/shard_map/ppermute | solution.py:69
  102.6 0.0 collective-permute-done.19.refs_1_
  102.6 1.1 %collective-permute-start.18 = (bf16[1,4,128,128]{3,2,1,0:T(8,128)(2,1)S(1)}, bf16[1,4,128,128]{3,2,1,0:T(8,128)(2,1)S(1)}, u32[]{:S(2)}, u32[]{:S(2)}) collective-permute-start(bf16[1,4,128,128]{3,2,1,0:T(8,128)(2,1)S(1)} %get-tuple-element.76), channel_id=1, source_target_pairs={{0,6},{1,7},{2,4},{3,5},{4,2},{5,3},{6,0},{7,1},{8,14},{9,15},{10,... | collective-permute-start | bytes 393224 | tf_op jit(solution)/shard_map/ppermute | solution.py:69
  103.7 1.5 %collective-permute-done.20.refs_2_ = bf16[2,2,128,128]{3,2,1,0:T(8,128)(2,1)S(1)} collective-permute-done((bf16[2,2,128,128]{3,2,1,0:T(8,128)(2,1)S(1)}, bf16[2,2,128,128]{3,2,1,0:T(8,128)(2,1)S(1)}, u32[]{:S(2)}, u32[]{:S(2)}) %collective-permute-start.20) | collective-permute-done | bytes 131104 | tf_op jit(solution)/shard_map/ppermute | solution.py:69
  105.2 0.7 collective-permute-done.21.refs_3_
  105.9 1.7 %shard_map.100 = (bf16[512,512]{1,0:T(8,128)(2,1)}, bf16[512,512]{1,0:T(8,128)(2,1)}) custom-call(s32[3]{0:T(128)S(1)} %pad_add_fusion.ids, bf16[2,2,128,128]{3,2,1,0:T(8,128)(2,1)S(1)} %get-tuple-element.77.refs_0_, bf16[2,2,128,128]{3,2,1,0:T(8,128)(2,1)S(1)} %collective-permute-done.19.refs_1_, ...), custom_call_target="tpu_custom_call" | custom-call | bytes 5250000 | tf_op jit(solution)/shard_map/pallas_call | solution.py:538
  107.6 0.2 collective-permute-done.16.refs_1_
  107.8 0.7 collective-permute-done.17.refs_2_
  108.5 2.4 %collective-permute-done.18.refs_3_ = bf16[1,4,128,128]{3,2,1,0:T(8,128)(2,1)S(1)} collective-permute-done((bf16[1,4,128,128]{3,2,1,0:T(8,128)(2,1)S(1)}, bf16[1,4,128,128]{3,2,1,0:T(8,128)(2,1)S(1)}, u32[]{:S(2)}, u32[]{:S(2)}) %collective-permute-start.18) | collective-permute-done | bytes 131104 | tf_op jit(solution)/shard_map/ppermute | solution.py:69
  110.9 1.4 %shard_map.99 = bf16[512,512]{1,0:T(8,128)(2,1)} custom-call(s32[3]{0:T(128)S(1)} %pad_add_fusion.ids, bf16[1,4,128,128]{3,2,1,0:T(8,128)(2,1)S(1)} %get-tuple-element.73.refs_0_, bf16[1,4,128,128]{3,2,1,0:T(8,128)(2,1)S(1)} %collective-permute-done.16.refs_1_, bf16[1,4,128,128]{3,2,1,0:T(8,128)(2,1)S(1)} %collective-permute-done.17.refs_2_, ...), custom_call_target="tpu_custom_call" | custom-call | bytes 5250000 | tf_op jit(solution)/shard_map/pallas_call | solution.py:538
  (13 shorter events, 0.1 us)
Async XLA Ops:
  0.6 11.0 %copy-start = (bf16[128,2048]{1,0:T(8,128)(2,1)S(1)}, bf16[128,2048]{1,0:T(8,128)(2,1)}, u32[]{:S(2)}) copy-start(bf16[128,2048]{1,0:T(8,128)(2,1)} %g_ref.1) | copy-start | bytes 1572868
  0.6 11.0 %copy-start.1 = (bf16[128,2048]{1,0:T(8,128)(2,1)S(1)}, bf16[128,2048]{1,0:T(8,128)(2,1)}, u32[]{:S(2)}) copy-start(bf16[128,2048]{1,0:T(8,128)(2,1)} %o_ref.1) | copy-start | bytes 1572868
  0.7 11.0 %copy-start.2 = (bf16[128,2048]{1,0:T(8,128)(2,1)S(1)}, bf16[128,2048]{1,0:T(8,128)(2,1)}, u32[]{:S(2)}) copy-start(bf16[128,2048]{1,0:T(8,128)(2,1)} %v_ref.1) | copy-start | bytes 1572868
  3.2 44.1 %all-to-all-start = ((bf16[16,256,128]{2,1,0:T(8,128)(2,1)}), bf16[16,256,128]{2,1,0:T(8,128)(2,1)S(1)}, u32[]{:S(2)}, u32[]{:S(2)}) async-start(bf16[16,256,128]{2,1,0:T(8,128)(2,1)} %prep.1), calls=%async_computation | async-start | bytes 2097152 | tf_op jit(solution)/shard_map/all_to_all | solution.py:572
  11.6 51.4 %copy-start.3 = (s32[8,4,4]{0,2,1:T(4,128)S(1)}, s32[8,4,4]{0,2,1:T(4,128)}, u32[]{:S(2)}) copy-start(s32[8,4,4]{0,2,1:T(4,128)} %param.13) | copy-start | bytes 1540
  11.6 51.4 %copy-start.4 = (s32[8]{0:T(128)S(1)}, s32[8]{0:T(128)}, u32[]{:S(2)}) copy-start(s32[8]{0:T(128)} %order.1) | copy-start | bytes 100
  13.7 12.8 %collective-permute-start.1 = (bf16[4,136,128]{2,1,0:T(8,128)(2,1)S(1)}, bf16[4,136,128]{2,1,0:T(8,128)(2,1)S(1)}, u32[]{:S(2)}, u32[]{:S(2)}) collective-permute-start(bf16[4,136,128]{2,1,0:T(8,128)(2,1)S(1)} %get-tuple-element.51), channel_id=1, source_target_pairs={{0,2},{1,3},{2,0},{3,1},{4,6},{5,7},{6,4},{7,5},{8,10},{9,11},{10,... | collective-permute-start | bytes 417800 | tf_op jit(solution)/shard_map/ppermute | solution.py:69
  15.7 12.3 %collective-permute-start.2 = (bf16[4,136,128]{2,1,0:T(8,128)(2,1)S(1)}, bf16[4,136,128]{2,1,0:T(8,128)(2,1)S(1)}, u32[]{:S(2)}, u32[]{:S(2)}) collective-permute-start(bf16[4,136,128]{2,1,0:T(8,128)(2,1)S(1)} %get-tuple-element.52), channel_id=1, source_target_pairs={{0,4},{1,5},{2,6},{3,7},{4,0},{5,1},{6,2},{7,3},{8,12},{9,13},{10,... | collective-permute-start | bytes 417800 | tf_op jit(solution)/shard_map/ppermute | solution.py:69
  17.2 13.3 %collective-permute-start.3 = (bf16[4,136,128]{2,1,0:T(8,128)(2,1)S(1)}, bf16[4,136,128]{2,1,0:T(8,128)(2,1)S(1)}, u32[]{:S(2)}, u32[]{:S(2)}) collective-permute-start(bf16[4,136,128]{2,1,0:T(8,128)(2,1)S(1)} %get-tuple-element.53), channel_id=1, source_target_pairs={{0,6},{1,7},{2,4},{3,5},{4,2},{5,3},{6,0},{7,1},{8,14},{9,15},{10,... | collective-permute-start | bytes 417800 | tf_op jit(solution)/shard_map/ppermute | solution.py:69
  30.5 5.9 %collective-permute-start.4 = (bf16[4,136,128]{2,1,0:T(8,128)(2,1)S(1)}, bf16[4,136,128]{2,1,0:T(8,128)(2,1)S(1)}, u32[]{:S(2)}, u32[]{:S(2)}) collective-permute-start(bf16[4,136,128]{2,1,0:T(8,128)(2,1)S(1)} %get-tuple-element.55), channel_id=1, source_target_pairs={{0,8},{8,0},{16,24},{24,16},{1,9},{9,1},{17,25},{25,17},{2,10},{10... | collective-permute-start | bytes 417800 | tf_op jit(solution)/shard_map/ppermute | solution.py:64
  30.6 16.5 %collective-permute-start.5 = (bf16[4,136,128]{2,1,0:T(8,128)(2,1)S(1)}, bf16[4,136,128]{2,1,0:T(8,128)(2,1)S(1)}, u32[]{:S(2)}, u32[]{:S(2)}) collective-permute-start(bf16[4,136,128]{2,1,0:T(8,128)(2,1)S(1)} %get-tuple-element.56), channel_id=1, source_target_pairs={{0,16},{8,24},{16,0},{24,8},{1,17},{9,25},{17,1},{25,9},{2,18},{10... | collective-permute-start | bytes 417800 | tf_op jit(solution)/shard_map/ppermute | solution.py:64
  35.8 11.3 %collective-permute-start.6 = (bf16[4,136,128]{2,1,0:T(8,128)(2,1)S(1)}, bf16[4,136,128]{2,1,0:T(8,128)(2,1)S(1)}, u32[]{:S(2)}, u32[]{:S(2)}) collective-permute-start(bf16[4,136,128]{2,1,0:T(8,128)(2,1)S(1)} %get-tuple-element.57), channel_id=1, source_target_pairs={{0,24},{8,16},{16,8},{24,0},{1,25},{9,17},{17,9},{25,1},{2,26},{10... | collective-permute-start | bytes 417800 | tf_op jit(solution)/shard_map/ppermute | solution.py:64
  47.2 25.1 %collective-permute-start.7 = (bf16[16,136,128]{2,1,0:T(8,128)(2,1)S(1)}, bf16[16,136,128]{2,1,0:T(8,128)(2,1)S(1)}, u32[]{:S(2)}, u32[]{:S(2)}) collective-permute-start(bf16[16,136,128]{2,1,0:T(8,128)(2,1)S(1)} %shard_map.95.refs_0_), channel_id=1, source_target_pairs={{0,1},{1,0},{2,3},{3,2},{4,5},{5,4},{6,7},{7,6},{8,9},{9,8},{10,11... | collective-permute-start | bytes 1671176 | tf_op jit(solution)/shard_map/ppermute | solution.py:69
  47.9 18.6 %collective-permute-start = (bf16[16,128,128]{2,1,0:T(8,128)(2,1)S(1)}, bf16[16,128,128]{2,1,0:T(8,128)(2,1)S(1)}, u32[]{:S(2)}, u32[]{:S(2)}) collective-permute-start(bf16[16,128,128]{2,1,0:T(8,128)(2,1)S(1)} %get-tuple-element.48.refs_0_), channel_id=1, source_target_pairs={{0,1},{1,0},{2,3},{3,2},{4,5},{5,4},{6,7},{7,6},{8,9},{9,8},{10,11... | collective-permute-start | bytes 1572872 | tf_op jit(solution)/shard_map/ppermute | solution.py:69
  48.4 5.9 %collective-permute-start.9 = (bf16[4,128,128]{2,1,0:T(8,128)(2,1)S(1)}, bf16[4,128,128]{2,1,0:T(8,128)(2,1)S(1)}, u32[]{:S(2)}, u32[]{:S(2)}) collective-permute-start(bf16[4,128,128]{2,1,0:T(8,128)(2,1)S(1)} %get-tuple-element.63), channel_id=1, source_target_pairs={{0,2},{1,3},{2,0},{3,1},{4,6},{5,7},{6,4},{7,5},{8,10},{9,11},{10,... | collective-permute-start | bytes 393224 | tf_op jit(solution)/shard_map/ppermute | solution.py:69
  49.9 8.0 %collective-permute-start.10 = (bf16[4,128,128]{2,1,0:T(8,128)(2,1)S(1)}, bf16[4,128,128]{2,1,0:T(8,128)(2,1)S(1)}, u32[]{:S(2)}, u32[]{:S(2)}) collective-permute-start(bf16[4,128,128]{2,1,0:T(8,128)(2,1)S(1)} %get-tuple-element.64), channel_id=1, source_target_pairs={{0,4},{1,5},{2,6},{3,7},{4,0},{5,1},{6,2},{7,3},{8,12},{9,13},{10,... | collective-permute-start | bytes 393224 | tf_op jit(solution)/shard_map/ppermute | solution.py:69
  51.4 6.5 %collective-permute-start.11 = (bf16[4,128,128]{2,1,0:T(8,128)(2,1)S(1)}, bf16[4,128,128]{2,1,0:T(8,128)(2,1)S(1)}, u32[]{:S(2)}, u32[]{:S(2)}) collective-permute-start(bf16[4,128,128]{2,1,0:T(8,128)(2,1)S(1)} %get-tuple-element.65), channel_id=1, source_target_pairs={{0,6},{1,7},{2,4},{3,5},{4,2},{5,3},{6,0},{7,1},{8,14},{9,15},{10,... | collective-permute-start | bytes 393224 | tf_op jit(solution)/shard_map/ppermute | solution.py:69
  57.9 15.6 %collective-permute-start.14 = (bf16[4,128,128]{2,1,0:T(8,128)(2,1)S(1)}, bf16[4,128,128]{2,1,0:T(8,128)(2,1)S(1)}, u32[]{:S(2)}, u32[]{:S(2)}) collective-permute-start(bf16[4,128,128]{2,1,0:T(8,128)(2,1)S(1)} %get-tuple-element.69), channel_id=1, source_target_pairs={{0,8},{8,0},{16,24},{24,16},{1,9},{9,1},{17,25},{25,17},{2,10},{10... | collective-permute-start | bytes 393224 | tf_op jit(solution)/shard_map/ppermute | solution.py:64
  60.6 20.8 %collective-permute-start.12 = (bf16[4,128,128]{2,1,0:T(8,128)(2,1)S(1)}, bf16[4,128,128]{2,1,0:T(8,128)(2,1)S(1)}, u32[]{:S(2)}, u32[]{:S(2)}) collective-permute-start(bf16[4,128,128]{2,1,0:T(8,128)(2,1)S(1)} %get-tuple-element.66), channel_id=1, source_target_pairs={{0,16},{8,24},{16,0},{24,8},{1,17},{9,25},{17,1},{25,9},{2,18},{10... | collective-permute-start | bytes 393224 | tf_op jit(solution)/shard_map/ppermute | solution.py:64
  60.7 20.7 %collective-permute-start.13 = (bf16[4,128,128]{2,1,0:T(8,128)(2,1)S(1)}, bf16[4,128,128]{2,1,0:T(8,128)(2,1)S(1)}, u32[]{:S(2)}, u32[]{:S(2)}) collective-permute-start(bf16[4,128,128]{2,1,0:T(8,128)(2,1)S(1)} %get-tuple-element.67), channel_id=1, source_target_pairs={{0,24},{8,16},{16,8},{24,0},{1,25},{9,17},{17,9},{25,1},{2,26},{10... | collective-permute-start | bytes 393224 | tf_op jit(solution)/shard_map/ppermute | solution.py:64
  72.2 1.2 %collective-permute-start.8 = (f32[32,128]{1,0:T(8,128)S(1)}, f32[32,128]{1,0:T(8,128)S(1)}, u32[]{:S(2)}, u32[]{:S(2)}) collective-permute-start(f32[32,128]{1,0:T(8,128)S(1)} %get-tuple-element.58.refs_2_), channel_id=1, source_target_pairs={{0,1},{1,0},{2,3},{3,2},{4,5},{5,4},{6,7},{7,6},{8,9},{9,8},{10,11... | collective-permute-start | bytes 49160 | tf_op jit(solution)/shard_map/ppermute | solution.py:69
  89.9 4.9 %collective-permute-start.15 = (f32[16,128,128]{2,1,0:T(8,128)S(1)}, f32[16,128,128]{2,1,0:T(8,128)S(1)}, u32[]{:S(2)}, u32[]{:S(2)}) collective-permute-start(f32[16,128,128]{2,1,0:T(8,128)S(1)} %get-tuple-element.72), channel_id=1, source_target_pairs={{0,1},{1,0},{2,3},{3,2},{4,5},{5,4},{6,7},{7,6},{8,9},{9,8},{10,11... | collective-permute-start | bytes 3145736 | tf_op jit(solution)/shard_map/ppermute | solution.py:69
  90.1 6.4 %collective-permute-start.22 = (bf16[2,2,128,128]{3,2,1,0:T(8,128)(2,1)S(1)}, bf16[2,2,128,128]{3,2,1,0:T(8,128)(2,1)S(1)}, u32[]{:S(2)}, u32[]{:S(2)}) collective-permute-start(bf16[2,2,128,128]{3,2,1,0:T(8,128)(2,1)S(1)} %get-tuple-element.82), channel_id=1, source_target_pairs={{0,2},{1,3},{2,0},{3,1},{4,6},{5,7},{6,4},{7,5},{8,10},{9,11},{10,... | collective-permute-start | bytes 393224 | tf_op jit(solution)/shard_map/ppermute | solution.py:69
  91.3 8.3 %collective-permute-start.23 = (bf16[2,2,128,128]{3,2,1,0:T(8,128)(2,1)S(1)}, bf16[2,2,128,128]{3,2,1,0:T(8,128)(2,1)S(1)}, u32[]{:S(2)}, u32[]{:S(2)}) collective-permute-start(bf16[2,2,128,128]{3,2,1,0:T(8,128)(2,1)S(1)} %get-tuple-element.83), channel_id=1, source_target_pairs={{0,4},{1,5},{2,6},{3,7},{4,0},{5,1},{6,2},{7,3},{8,12},{9,13},{10,... | collective-permute-start | bytes 393224 | tf_op jit(solution)/shard_map/ppermute | solution.py:69
  92.1 8.6 %collective-permute-start.24 = (bf16[2,2,128,128]{3,2,1,0:T(8,128)(2,1)S(1)}, bf16[2,2,128,128]{3,2,1,0:T(8,128)(2,1)S(1)}, u32[]{:S(2)}, u32[]{:S(2)}) collective-permute-start(bf16[2,2,128,128]{3,2,1,0:T(8,128)(2,1)S(1)} %get-tuple-element.84), channel_id=1, source_target_pairs={{0,6},{1,7},{2,4},{3,5},{4,2},{5,3},{6,0},{7,1},{8,14},{9,15},{10,... | collective-permute-start | bytes 393224 | tf_op jit(solution)/shard_map/ppermute | solution.py:69
  93.6 9.0 %collective-permute-start.19 = (bf16[2,2,128,128]{3,2,1,0:T(8,128)(2,1)S(1)}, bf16[2,2,128,128]{3,2,1,0:T(8,128)(2,1)S(1)}, u32[]{:S(2)}, u32[]{:S(2)}) collective-permute-start(bf16[2,2,128,128]{3,2,1,0:T(8,128)(2,1)S(1)} %get-tuple-element.78), channel_id=1, source_target_pairs={{0,2},{1,3},{2,0},{3,1},{4,6},{5,7},{6,4},{7,5},{8,10},{9,11},{10,... | collective-permute-start | bytes 393224 | tf_op jit(solution)/shard_map/ppermute | solution.py:69
  94.8 10.4 %collective-permute-start.20 = (bf16[2,2,128,128]{3,2,1,0:T(8,128)(2,1)S(1)}, bf16[2,2,128,128]{3,2,1,0:T(8,128)(2,1)S(1)}, u32[]{:S(2)}, u32[]{:S(2)}) collective-permute-start(bf16[2,2,128,128]{3,2,1,0:T(8,128)(2,1)S(1)} %get-tuple-element.79), channel_id=1, source_target_pairs={{0,4},{1,5},{2,6},{3,7},{4,0},{5,1},{6,2},{7,3},{8,12},{9,13},{10,... | collective-permute-start | bytes 393224 | tf_op jit(solution)/shard_map/ppermute | solution.py:69
  96.5 9.4 %collective-permute-start.21 = (bf16[2,2,128,128]{3,2,1,0:T(8,128)(2,1)S(1)}, bf16[2,2,128,128]{3,2,1,0:T(8,128)(2,1)S(1)}, u32[]{:S(2)}, u32[]{:S(2)}) collective-permute-start(bf16[2,2,128,128]{3,2,1,0:T(8,128)(2,1)S(1)} %get-tuple-element.80), channel_id=1, source_target_pairs={{0,6},{1,7},{2,4},{3,5},{4,2},{5,3},{6,0},{7,1},{8,14},{9,15},{10,... | collective-permute-start | bytes 393224 | tf_op jit(solution)/shard_map/ppermute | solution.py:69
  99.6 8.2 %collective-permute-start.16 = (bf16[1,4,128,128]{3,2,1,0:T(8,128)(2,1)S(1)}, bf16[1,4,128,128]{3,2,1,0:T(8,128)(2,1)S(1)}, u32[]{:S(2)}, u32[]{:S(2)}) collective-permute-start(bf16[1,4,128,128]{3,2,1,0:T(8,128)(2,1)S(1)} %get-tuple-element.74), channel_id=1, source_target_pairs={{0,2},{1,3},{2,0},{3,1},{4,6},{5,7},{6,4},{7,5},{8,10},{9,11},{10,... | collective-permute-start | bytes 393224 | tf_op jit(solution)/shard_map/ppermute | solution.py:69
  100.8 7.7 %collective-permute-start.17 = (bf16[1,4,128,128]{3,2,1,0:T(8,128)(2,1)S(1)}, bf16[1,4,128,128]{3,2,1,0:T(8,128)(2,1)S(1)}, u32[]{:S(2)}, u32[]{:S(2)}) collective-permute-start(bf16[1,4,128,128]{3,2,1,0:T(8,128)(2,1)S(1)} %get-tuple-element.75), channel_id=1, source_target_pairs={{0,4},{1,5},{2,6},{3,7},{4,0},{5,1},{6,2},{7,3},{8,12},{9,13},{10,... | collective-permute-start | bytes 393224 | tf_op jit(solution)/shard_map/ppermute | solution.py:69
  102.6 8.3 %collective-permute-start.18 = (bf16[1,4,128,128]{3,2,1,0:T(8,128)(2,1)S(1)}, bf16[1,4,128,128]{3,2,1,0:T(8,128)(2,1)S(1)}, u32[]{:S(2)}, u32[]{:S(2)}) collective-permute-start(bf16[1,4,128,128]{3,2,1,0:T(8,128)(2,1)S(1)} %get-tuple-element.76), channel_id=1, source_target_pairs={{0,6},{1,7},{2,4},{3,5},{4,2},{5,3},{6,0},{7,1},{8,14},{9,15},{10,... | collective-permute-start | bytes 393224 | tf_op jit(solution)/shard_map/ppermute | solution.py:69
